TPU v7x, 128 devices: a whole 4x4x4 slice. The times are simulated.
128 devices in a mesh: ctx: 64 (over y_lo, x, z, core), tp: 2 (over y_hi).
Axes of the slice: x: 4, y: 4 (y_hi: 2, y_lo: 2; y = y_hi * 2 + y_lo), z: 4, core: 2. Of those that a mesh axis runs over, the one named last changes fastest.
Arguments:
- inputs: bfloat16 [3, 8192, 4096], P(None, 'ctx', 'tp'), may hold values from -6 to 6
- short_weight: float32 [3, 3, 4096], P(None, None, 'tp'), may hold values from -3 to 3
- taps: float32 [8192, 4096], P('ctx', 'tp'), may hold values from -6 to 6
- w_out: bfloat16 [4096, 4096], P('tp'), may hold values from -0.09375 to 0.09375
- grad_out: bfloat16 [8192, 4096], P('ctx', 'tp'), may hold values from -6 to 6
Outputs:
- inputs_grad: bfloat16 [3, 8192, 4096], P(None, 'ctx', 'tp')
- taps_grad: float32 [8192, 4096], P('ctx', 'tp')
- short_grad: float32 [3, 3, 4096], P(None, None, 'tp')
All inputs are finite; a program needn't handle non-finite values.
Results may differ from a plain program's by a relative error of at most 0.0015.
Values may be sent and summed in bfloat16 or wider, within the bound.
No kernel may reach another device: no remote copies, remote signals or barrier semaphores. Data moves between devices by JAX's collectives and lax.ppermute only.
A program may use at most 192 MiB of HBM per device.

v0:
```python
import math

import jax
import jax.numpy as jnp
from jax import lax
from jax.sharding import PartitionSpec as P

HIGH = lax.Precision.HIGHEST


def shifted(x, axis, by):
    peers = lax.axis_size(axis)
    pairs = [(i, i + by) for i in range(peers) if 0 <= i + by < peers]
    return lax.ppermute(x, axis, pairs)


def phase(left_idx, right_idx, period):
    turns = left_idx[:, None] * right_idx[None, :] % period
    angle = turns.astype(jnp.float32) * (2.0 * math.pi / period)
    return (jnp.cos(angle), jnp.sin(angle))


def section_one(blocks, n2_start, period):
    count = blocks.shape[1]
    width = blocks.shape[2]
    cos_a, sin_a = phase(
        jnp.arange(2 * count, dtype=jnp.int32), jnp.arange(count, dtype=jnp.int32), 2 * count
    )
    real_part = jnp.einsum("kn,bnmc->bkmc", cos_a, blocks, precision=HIGH)
    imag_part = -jnp.einsum("kn,bnmc->bkmc", sin_a, blocks, precision=HIGH)
    cos_b, sin_b = phase(
        jnp.arange(2 * count, dtype=jnp.int32),
        n2_start + jnp.arange(width, dtype=jnp.int32),
        period,
    )
    tw_re = cos_b[None, :, :, None]
    tw_im = -sin_b[None, :, :, None]
    return jnp.stack([real_part * tw_re - imag_part * tw_im, real_part * tw_im + imag_part * tw_re])


def section_two(parts):
    length = parts.shape[3]
    cos_a, sin_a = phase(
        jnp.arange(length, dtype=jnp.int32), jnp.arange(length, dtype=jnp.int32), length
    )
    real_in, imag_in = (parts[0], parts[1])
    cc_re = jnp.einsum("qn,bknc->bkqc", cos_a, real_in, precision=HIGH)
    cc_im = jnp.einsum("qn,bknc->bkqc", cos_a, imag_in, precision=HIGH)
    ss_re = jnp.einsum("qn,bknc->bkqc", sin_a, real_in, precision=HIGH)
    ss_im = jnp.einsum("qn,bknc->bkqc", sin_a, imag_in, precision=HIGH)
    return jnp.stack([cc_re + ss_im, cc_im - ss_re])


def inverse_two(spec, k1_start, period):
    classes = spec.shape[2]
    length = spec.shape[3]
    cos_a, sin_a = phase(
        jnp.arange(length, dtype=jnp.int32), jnp.arange(length, dtype=jnp.int32), length
    )
    real_in, imag_in = (spec[0], spec[1])
    cc_re = jnp.einsum("nq,bkqc->bknc", cos_a, real_in, precision=HIGH)
    cc_im = jnp.einsum("nq,bkqc->bknc", cos_a, imag_in, precision=HIGH)
    ss_re = jnp.einsum("nq,bkqc->bknc", sin_a, real_in, precision=HIGH)
    ss_im = jnp.einsum("nq,bkqc->bknc", sin_a, imag_in, precision=HIGH)
    back_re = cc_re - ss_im
    back_im = cc_im + ss_re
    cos_b, sin_b = phase(
        k1_start + jnp.arange(classes, dtype=jnp.int32), jnp.arange(length, dtype=jnp.int32), period
    )
    tw_re = cos_b[None, :, :, None]
    tw_im = sin_b[None, :, :, None]
    return jnp.stack([back_re * tw_re - back_im * tw_im, back_re * tw_im + back_im * tw_re])


def inverse_one(spec, period):
    classes = spec.shape[2]
    count = classes // 2
    cos_a, sin_a = phase(
        jnp.arange(count, dtype=jnp.int32), jnp.arange(classes, dtype=jnp.int32), classes
    )
    real_out = jnp.einsum("nk,bkmc->bnmc", cos_a, spec[0], precision=HIGH)
    real_out = real_out - jnp.einsum("nk,bkmc->bnmc", sin_a, spec[1], precision=HIGH)
    return real_out / period


def products(spec):
    filt_re, filt_im = (spec[0, 0], spec[1, 0])
    prod_re, prod_im = (spec[0, 1], spec[1, 1])
    grad_re, grad_im = (spec[0, 2], spec[1, 2])
    out_re = jnp.stack(
        [
            filt_re * prod_re - filt_im * prod_im,
            filt_re * grad_re + filt_im * grad_im,
            prod_re * grad_re + prod_im * grad_im,
        ]
    )
    out_im = jnp.stack(
        [
            filt_re * prod_im + filt_im * prod_re,
            filt_re * grad_im - filt_im * grad_re,
            prod_re * grad_im - prod_im * grad_re,
        ]
    )
    return jnp.stack([out_re, out_im])


def shards(inputs, short_weight, taps, w_out, grad_out):
    rows = inputs.shape[1]
    span = short_weight.shape[1]
    count = lax.axis_size("ctx")
    where = lax.axis_index("ctx")
    period = 2 * count * rows
    scale = 1.0 / math.sqrt(count * rows)
    prior = shifted(inputs[:, rows - (span - 1) :, :], "ctx", 1)
    extended = jnp.concatenate([prior, inputs], axis=1).astype(jnp.float32)
    mixed = jnp.zeros((3, rows, inputs.shape[2]), jnp.float32)
    for j in range(span):
        mixed = (
            mixed + short_weight[:, j][:, None, :] * extended[:, span - 1 - j : span - 1 - j + rows]
        )
    query, key_s, value = (mixed[0], mixed[1], mixed[2])
    product = key_s * value
    filt = taps * scale
    columns = w_out
    gated_grad = lax.dot_general(
        lax.all_gather(grad_out, "tp", axis=1, tiled=True),
        columns,
        (((1,), (1,)), ((), ())),
        preferred_element_type=jnp.float32,
    )
    dy = gated_grad * query
    stacked = jnp.stack([filt, product, dy])
    width = rows // count
    blocks = stacked.reshape(3, count, width, stacked.shape[2])
    columns = section_one(
        lax.all_to_all(blocks, "ctx", split_axis=1, concat_axis=1, tiled=True),
        n2_start=where * width,
        period=period,
    )
    spec = section_two(lax.all_to_all(columns, "ctx", split_axis=2, concat_axis=3, tiled=True))
    back = inverse_two(products(spec), where * spec.shape[2], period)
    parted = inverse_one(
        lax.all_to_all(back, "ctx", split_axis=3, concat_axis=2, tiled=True), period=period
    )
    result = lax.all_to_all(parted, "ctx", split_axis=1, concat_axis=1, tiled=True).reshape(
        3, rows, stacked.shape[2]
    )
    conv_out, dz, raw = (result[0], result[1], result[2])
    dmixed = jnp.stack([gated_grad * conv_out, dz * value, dz * key_s])
    following = shifted(dmixed[:, : span - 1, :].astype(jnp.bfloat16), "ctx", -1).astype(
        jnp.float32
    )
    dext = jnp.concatenate([dmixed, following], axis=1)
    inputs_grad = jnp.zeros_like(dmixed)
    sums = []
    for j in range(span):
        inputs_grad = inputs_grad + short_weight[:, j][:, None, :] * dext[:, j : j + rows]
        sums.append(jnp.sum(dmixed * extended[:, span - 1 - j : span - 1 - j + rows], axis=1))
    short_grad = lax.psum(jnp.stack(sums, axis=1), "ctx") * scale
    return (inputs_grad.astype(jnp.bfloat16), raw * scale, short_grad)


def solution(mesh):
    return jax.shard_map(
        shards,
        mesh=mesh,
        in_specs=(
            P(None, "ctx", "tp"),
            P(None, None, "tp"),
            P("ctx", "tp"),
            P("tp", None),
            P("ctx", "tp"),
        ),
        out_specs=(P(None, "ctx", "tp"), P("ctx", "tp"), P(None, None, "tp")),
        check_vma=False,
    )
```

profile of v0, /device:TPU:1, one launch (start us, length us, event | category | flops | bytes accessed | tf_op | source)
XLA Modules:
  0.0 1260.1 jit_solution(7700438997746411273)
XLA Ops:
  7.2 1.0 slice.93
  8.3 4.9 collective-permute-start
  13.2 1.1 fusion.132
  14.3 1.3 broadcast_multiply_fusion
  15.8 1.6 stack.68
  17.4 0.5 maximum_convert_fusion
  17.9 0.9 multiply_add_fusion
  18.8 0.7 copy-done
  19.5 1.2 slice_multiply_fusion.4
  20.8 3.0 stack.69
  23.8 16.4 %all-gather.2.cloned.1.call-done = bf16[128,4096]{1,0:T(8,128)(2,1)} async-done(((bf16[128,2048]{1,0:T(8,128)(2,1)}), bf16[128,4096]{1,0:T(8,128)(2,1)}) %all-gather.2.cloned.1.call-update) | async-done | bytes 1048592 | tf_op jit(solution)/shard_map/all_gather | solution.py:126
  40.1 13.1 %fusion.17 = (f32[128,2048]{1,0:T(8,128)}, f32[128,2048]{1,0:T(8,128)}) fusion(f32[3,128,2048]{2,1,0:T(8,128)S(1)} %multiply_add_fusion, bf16[128,4096]{1,0:T(8,128)(2,1)} %all-gather.2.cloned.1.call-done, bf16[2048,4096]{1,0:T(8,128)(2,1)} %param.8), kind=kOutput, calls=%fused_computation.48 | convolution fusion | flops 2147745792 | bytes 20971520 | tf_op jit(solution)/shard_map/dot_general | solution.py:125
  53.2 1.8 stack.70
  55.1 3.2 pad_maximum_fusion.13
  58.2 3.0 copy.33
  61.3 8.1 all-to-all-start
  69.5 40.2 %all-to-all-done = f32[3,64,2,2048]{3,2,0,1:T(2,128)S(1)} async-done(((f32[3,64,2,2048]{3,2,0,1:T(2,128)}), f32[3,64,2,2048]{3,2,0,1:T(2,128)S(1)}, u32[]{:S(2)}, u32[]{:S(2)}) %all-to-all-start) | async-done | bytes 3145760 | tf_op jit(solution)/shard_map/all_to_all | solution.py:136
  109.7 11.2 fusion.13
  120.9 23.9 %fusion.1 = (f32[1,3,128,2,2048]{2,4,3,1,0:T(8,128)}, f32[1,3,128,2,2048]{2,4,3,1,0:T(8,128)}) fusion(f32[3,2,2048,128]{3,2,1,0:T(8,128)S(1)} %fusion.13, f32[128,2]{0,1:T(2,128)S(1)} %get-tuple-element.38, f32[128,2]{0,1:T(2,128)S(1)} %get-tuple-element.37, f32[3,64,2,2048]{3,2,0,1:T(2,128)S(1)} %all-to-all-done), kind=kOutput, calls=%fused_computation.7 | convolution fusion | flops 1219084288 | bytes 22022144 | tf_op jit(solution)/shard_map/kn,bnmc->bkmc/dot_general | solution.py:29
  144.9 9.9 pad_maximum_fusion
  154.8 19.3 %copy.36 = f32[2,3,128,2,2048]{4,3,1,0,2:T(2,128)} copy(f32[2,3,128,2,2048]{2,4,3,1,0:T(8,128)} %pad_maximum_fusion) | data formatting | bytes 25165824 | tf_op jit(solution)/shard_map/stack | solution.py:38
  174.2 6.9 all-to-all-start.1
  181.3 163.9 %all-to-all-done.1 = f32[2,3,128,2,2048]{4,3,1,0,2:T(2,128)} async-done(((f32[2,3,128,2,2048]{4,3,1,0,2:T(2,128)}), f32[2,3,128,2,2048]{4,3,1,0,2:T(2,128)}, u32[]{:S(2)}, u32[]{:S(2)}) %all-to-all-start.1) | async-done | bytes 12582944 | tf_op jit(solution)/shard_map/all_to_all | solution.py:140
  345.2 6.3 copy.37
  351.5 3.9 fusion.131
  355.4 8.9 copy.38
  364.3 10.3 copy.39
  374.6 9.9 fusion.29
  384.6 8.8 copy.40
  393.4 10.2 copy.41
  403.6 8.1 fusion.27
  411.8 7.9 add_bitcast_fusion.1
  419.7 5.4 subtract_bitcast_fusion.1
  425.2 2.6 add_bitcast_fusion.4
  427.8 3.7 subtract_bitcast_fusion.4
  431.5 8.5 fusion.4
  440.1 5.7 fusion.5
  445.8 5.7 fusion.8
  451.5 10.8 subtract_bitcast_fusion
  462.3 8.1 pad_maximum_fusion.1
  470.4 19.3 %copy.44 = f32[2,3,2,128,2048]{4,2,1,0,3:T(2,128)} copy(f32[2,3,2,128,2048]{3,4,2,1,0:T(8,128)} %pad_maximum_fusion.1) | data formatting | bytes 25165824 | tf_op jit(solution)/shard_map/stack | solution.py:72
  489.7 163.5 %all_to_all.40 = f32[2,3,2,128,2048]{4,2,1,0,3:T(2,128)S(1)} all-to-all(f32[2,3,2,128,2048]{4,2,1,0,3:T(2,128)} %copy.44), channel_id=1, replica_groups=mesh['ctx'=64,'tp'=2] {'ctx'}, dimensions={3} | all-to-all | bytes 25165824 | tf_op jit(solution)/shard_map/all_to_all | solution.py:143
  653.2 2.8 copy.45
  656.0 3.9 fusion.130
  659.9 5.6 copy.46
  665.5 8.5 squeeze.33
  674.0 7.4 fusion.41
  681.4 5.6 copy.47
  687.1 8.6 squeeze.34
  695.7 6.5 multiply_bitcast_fusion
  702.2 2.4 copy.48
  704.6 50.6 %all_to_all.41 = f32[3,64,2,2048]{3,2,0,1:T(2,128)S(1)} all-to-all(f32[3,64,2,2048]{3,2,0,1:T(2,128)S(1)} %copy.48), channel_id=1, replica_groups=mesh['ctx'=64,'tp'=2] {'ctx'}, dimensions={1} | all-to-all | bytes 6291456 | tf_op jit(solution)/shard_map/all_to_all | solution.py:145
  755.3 2.4 slice_multiply_fusion.2
  757.7 3.1 squeeze.35
  760.8 2.9 squeeze.36
  763.7 1.6 slice_multiply_fusion.3
  766.1 2.8 collective-permute-start.1
  768.9 2.6 collective-permute-done.1
  772.0 3.0 multiply_reduce_fusion.2
  775.0 0.7 pad_maximum_fusion.15
  775.7 1.7 mul.554
  777.4 473.8 %all-reduce.2.cloned.1.call-done = f32[3,3,2048]{2,0,1:T(4,128)} async-done(((f32[3,3,2048]{2,0,1:T(4,128)}), f32[3,3,2048]{2,0,1:T(4,128)}) %all-reduce.2.cloned.1.call-update) | async-done | bytes 73744 | tf_op jit(solution)/shard_map/psum | solution.py:159
  1251.2 0.9 broadcast_multiply_fusion.1
  1252.1 0.7 copy.49
  (70 shorter events, 1.7 us)
Async XLA Ops:
  7.2 10.2 copy-start.16
  7.2 33.0 %all-gather.2.cloned.1.call-start = ((), (), s32[]{:S(2)}) async-start(), calls=%async_computation.4 | async-start | bytes 1572864 | tf_op jit(solution)/shard_map/all_gather | solution.py:126
  8.3 9.1 collective-permute-start
  15.7 2.2 copy-start.17
  15.7 2.2 copy-start.19
  15.7 2.1 copy-start.21
  17.9 1.7 copy-start
  19.5 33.7 %copy-start.4 = (f32[3,128,2048]{2,1,0:T(8,128)}, f32[3,128,2048]{2,1,0:T(8,128)S(1)}, u32[]{:S(2)}) copy-start(f32[3,128,2048]{2,1,0:T(8,128)S(1)} %multiply_add_fusion) | copy-start | bytes 9437188
  61.3 48.4 %all-to-all-start = ((f32[3,64,2,2048]{3,2,0,1:T(2,128)}), f32[3,64,2,2048]{3,2,0,1:T(2,128)S(1)}, u32[]{:S(2)}, u32[]{:S(2)}) async-start(f32[3,64,2,2048]{3,2,0,1:T(2,128)} %copy.33), calls=%async_computation | async-start | bytes 6291456 | tf_op jit(solution)/shard_map/all_to_all | solution.py:136
  174.2 171.0 %all-to-all-start.1 = ((f32[2,3,128,2,2048]{4,3,1,0,2:T(2,128)}), f32[2,3,128,2,2048]{4,3,1,0,2:T(2,128)}, u32[]{:S(2)}, u32[]{:S(2)}) async-start(f32[2,3,128,2,2048]{4,3,1,0,2:T(2,128)} %copy.36), calls=%async_computation.1 | async-start | bytes 25165824 | tf_op jit(solution)/shard_map/all_to_all | solution.py:140
  181.1 1070.1 %all-reduce.2.cloned.1.call-start = ((), (), s32[]{:S(2)}) async-start(), calls=%async_computation.5 | async-start | bytes 196608 | tf_op jit(solution)/shard_map/psum | solution.py:159
  364.3 20.3 %slice-start.2 = ((s8[6291456]{0:T(1024)(128)(4,1)}), s8[2097152]{0:T(1024)(128)(4,1)S(1)}, s32[]{:S(2)}) async-start(s8[6291456]{0:T(1024)(128)(4,1)} %bitcast.146), calls=%async_computation.8 | async-start | bytes 4194304
  374.6 10.0 slice-start.3
  403.6 8.1 copy-start.2
  403.6 16.1 %slice-start = ((s8[6291456]{0:T(1024)(128)(4,1)}), s8[4194304]{0:T(1024)(128)(4,1)S(1)}, s32[]{:S(2)}) async-start(s8[6291456]{0:T(1024)(128)(4,1)} %bitcast.140), calls=%async_computation.6 | async-start | bytes 8388608
  411.8 8.0 slice-start.1
  431.5 8.5 copy-start.9
  431.5 8.5 copy-start.10
  431.5 8.5 copy-start.11
  440.1 5.7 copy-start.6
  440.1 5.7 copy-start.7
  440.1 5.7 copy-start.8
  674.0 7.4 copy-start.3
  687.1 8.6 copy-start.12
  757.7 6.0 copy-start.5
  763.7 1.6 copy-start.13
  763.7 1.9 copy-start.14
  766.1 5.9 copy-start.1
  766.1 5.9 copy-start.18
  766.1 5.9 copy-start.20
  766.1 5.9 copy-start.22
  766.1 5.4 collective-permute-start.1
  772.0 3.7 copy-start.15
Sparse Core Ops, SparseCore 0:
  13.3 26.7 all-gather.1
  775.9 475.3 all-reduce.1
where the time goes:
time: 1270 us; the launch traced here: 1260 us
  waiting for transfers between devices  697 us (55%)
  blocking collectives  214 us (17%)
  local copies, waits for them, and re-layouts  146 us (11%)
  matrix products  124 us (10%)
  other arithmetic  41.3 us (3%)
  starting transfers between devices  22.8 us (2%)
  between operations  15 us (1%)
    psum x1, waiting for transfers between devices, shards(): short_grad = lax.psum(jnp.stack(sums, axis=1), 'ctx') * scale  474 us
    all_to_all x1, waiting for transfers between devices, shards(): lax.all_to_all(columns, 'ctx', split_axis=2, concat_axis=3, tiled=True)  164 us
    all_to_all x1, blocking collectives, shards(): lax.all_to_all(back, 'ctx', split_axis=3, concat_axis=2, tiled=True)  163 us
    all_to_all x1, blocking collectives, shards(): lax.all_to_all(parted, 'ctx', split_axis=1, concat_axis=1, tiled=True)  50.6 us
    all_to_all x1, waiting for transfers between devices, shards(): lax.all_to_all(blocks, 'ctx', split_axis=1, concat_axis=1, tiled=True)  40.2 us
  transfers between devices with their start and end apart: 6, of which 5 were waited for; matrix products, arithmetic and copies ran while one was open for 1% of the time, Pallas kernels for 0%

commit v1 on v0

v1 whole, which is shorter than its diff:
```python
import math

import jax
import jax.numpy as jnp
import numpy as np
from jax import lax
from jax.experimental import pallas as pl
from jax.experimental.pallas import tpu as pltpu
from jax.sharding import PartitionSpec as P

GROUP = 4


def split_np(x):
    high = x.astype(jnp.bfloat16)
    low = (x - high.astype(np.float64)).astype(jnp.bfloat16)
    return high, low


def tables(blocks, width):
    length = 2 * blocks * width
    n1 = np.arange(blocks)
    n2 = np.arange(width)
    angle = 2.0 * np.pi * np.outer(n1 + 0.5, n1) / (2 * blocks)
    first = np.concatenate([np.cos(angle), -np.sin(angle)], axis=0)
    high, low = split_np(first)
    first3 = np.concatenate([high, high, low], axis=1)
    last = first.T * (2.0 / length)
    high, low = split_np(last)
    last4 = np.concatenate(
        [
            np.concatenate([high, high], axis=1),
            np.concatenate([low, np.zeros_like(low)], axis=1),
        ],
        axis=0,
    )
    angle = 2.0 * np.pi * (np.outer(n2, n2) % width) / width
    cos, sin = np.cos(angle), np.sin(angle)
    forward = np.block([[cos, -sin], [sin, cos]])
    high, low = split_np(forward)
    forward3 = np.concatenate([high, high, low], axis=0)
    backward = np.block([[cos, sin], [-sin, cos]])
    high, low = split_np(backward)
    backward3 = np.concatenate([high, high, low], axis=0)
    angle = 2.0 * np.pi * np.outer(n1 + 0.5, n2) / length
    twiddle = np.stack([np.cos(angle), np.sin(angle)]).astype(np.float32)
    return first3, last4, forward3, backward3, twiddle


def split(x):
    high = x.astype(jnp.bfloat16)
    low = (x - high.astype(jnp.float32)).astype(jnp.bfloat16)
    return high, low


def mm(a, b):
    return jnp.dot(a, b, preferred_element_type=jnp.float32)


def conv_kernel(
    scale,
    in_ref,
    taps_ref,
    grad_ref,
    weight_ref,
    first_ref,
    last_ref,
    forward_ref,
    backward_ref,
    twiddle_ref,
    ig_ref,
    tg_ref,
    sg_ref,
    src,
    res,
    key_ref,
    val_ref,
):
    blocks, _, chans, width = in_ref.shape
    lane = lax.broadcasted_iota(jnp.int32, (chans, width), 1)
    zero = jnp.zeros((chans, width), jnp.float32)

    def load(n1, b):
        cur = in_ref[n1, b].astype(jnp.float32)
        before = in_ref[jnp.maximum(n1 - 1, 0), b].astype(jnp.float32)
        before = jnp.where(n1 > 0, before, zero)
        return [cur] + [
            pltpu.roll(jnp.where(lane >= width - j, before, cur), j, 1) for j in (1, 2)
        ]

    def prepare(n1, carry):
        mixed = []
        for b in range(3):
            parts = load(n1, b)
            mixed.append(
                weight_ref[3 * b] * parts[0]
                + weight_ref[3 * b + 1] * parts[1]
                + weight_ref[3 * b + 2] * parts[2]
            )
        at = pl.ds(pl.multiple_of(n1 * chans, chans), chans)
        src[0, at, :] = taps_ref[n1] * scale
        src[1, at, :] = mixed[1] * mixed[2]
        src[2, at, :] = grad_ref[n1] * mixed[0]
        key_ref[at, :] = mixed[1]
        val_ref[at, :] = mixed[2]
        return carry

    lax.fori_loop(0, blocks, prepare, 0)

    cos, sin = twiddle_ref[0], twiddle_ref[1]

    def convolve(step, carry):
        base = step * GROUP
        rows = []
        for s in range(3):
            for g in range(0, GROUP, 2):
                cols = []
                for h in (0, 1):
                    x = src[s, pl.ds(base + g + h, blocks, stride=chans), :]
                    high, low = split(x)
                    cols.append(jnp.concatenate([high, low, high], axis=0))
                out = mm(first_ref[...], jnp.concatenate(cols, axis=1))
                for h in (0, 1):
                    re = out[:blocks, h * width : (h + 1) * width]
                    im = out[blocks:, h * width : (h + 1) * width]
                    rows.append(
                        jnp.concatenate([re * cos + im * sin, im * cos - re * sin], axis=1)
                    )
        high, low = split(jnp.concatenate(rows, axis=0))
        spec = mm(jnp.concatenate([high, low, high], axis=1), forward_ref[...])
        part = GROUP * blocks
        fr, fi = spec[:part, :width], spec[:part, width:]
        pr, pi = spec[part : 2 * part, :width], spec[part : 2 * part, width:]
        gr, gi = spec[2 * part :, :width], spec[2 * part :, width:]
        prod = jnp.concatenate(
            [
                jnp.concatenate([fr * pr - fi * pi, fr * pi + fi * pr], axis=1),
                jnp.concatenate([fr * gr + fi * gi, fr * gi - fi * gr], axis=1),
                jnp.concatenate([pr * gr + pi * gi, pr * gi - pi * gr], axis=1),
            ],
            axis=0,
        )
        high, low = split(prod)
        back = mm(jnp.concatenate([high, low, high], axis=1), backward_ref[...])
        for s in range(3):
            for g in range(0, GROUP, 2):
                cols = []
                for h in (0, 1):
                    at = (s * GROUP + g + h) * blocks
                    re = back[at : at + blocks, :width]
                    im = back[at : at + blocks, width:]
                    both = jnp.concatenate([re * cos - im * sin, re * sin + im * cos], axis=0)
                    high, low = split(both)
                    cols.append(jnp.concatenate([high, low], axis=0))
                out = mm(last_ref[...], jnp.concatenate(cols, axis=1))
                out = out[:blocks] + out[blocks:]
                for h in (0, 1):
                    res[s, pl.ds(base + g + h, blocks, stride=chans), :] = out[
                        :, h * width : (h + 1) * width
                    ]
        return carry

    lax.fori_loop(0, chans // GROUP, convolve, 0)

    def gradients(n1):
        at = pl.ds(pl.multiple_of(n1 * chans, chans), chans)
        dz = res[1, at, :]
        return grad_ref[n1] * res[0, at, :], dz * val_ref[at, :], dz * key_ref[at, :]

    sg_ref[...] = jnp.zeros_like(sg_ref)

    def finish(n1, cur):
        at = pl.ds(pl.multiple_of(n1 * chans, chans), chans)
        follow = gradients(jnp.minimum(n1 + 1, blocks - 1))
        follow = [jnp.where(n1 + 1 < blocks, f, zero) for f in follow]
        tg_ref[n1] = res[2, at, :] * scale
        for b in range(3):
            parts = load(n1, b)
            out = weight_ref[3 * b] * cur[b]
            for j in (1, 2):
                moved = pltpu.roll(jnp.where(lane < j, follow[b], cur[b]), width - j, 1)
                out = out + weight_ref[3 * b + j] * moved
            ig_ref[n1, b] = out.astype(jnp.bfloat16)
            for j in range(3):
                sg_ref[3 * b + j] += cur[b] * parts[j]
        return tuple(follow)

    lax.fori_loop(0, blocks, finish, gradients(0))


def convolve_all(inputs, taps, grad, weight, scale):
    blocks, _, chans, width = inputs.shape
    consts = [jnp.asarray(t) for t in tables(blocks, width)]
    return pl.pallas_call(
        lambda *refs: conv_kernel(scale, *refs),
        out_shape=(
            jax.ShapeDtypeStruct((blocks, 3, chans, width), jnp.bfloat16),
            jax.ShapeDtypeStruct((blocks, chans, width), jnp.float32),
            jax.ShapeDtypeStruct((9, chans, width), jnp.float32),
        ),
        scratch_shapes=[
            pltpu.VMEM((3, blocks * chans, width), jnp.float32),
            pltpu.VMEM((3, blocks * chans, width), jnp.float32),
            pltpu.VMEM((blocks * chans, width), jnp.float32),
            pltpu.VMEM((blocks * chans, width), jnp.float32),
        ],
        compiler_params=pltpu.CompilerParams(vmem_limit_bytes=56 << 20),
    )(inputs, taps, grad, weight, *consts)


def regroup(x):
    return lax.all_to_all(x, "ctx", split_axis=0, concat_axis=0, tiled=True)


def shards(inputs, short_weight, taps, w_out, grad_out):
    rows, local = inputs.shape[1], inputs.shape[2]
    count = lax.axis_size("ctx")
    where = lax.axis_index("ctx")
    chans = local // count
    scale = 1.0 / math.sqrt(count * rows)

    streams = regroup(inputs.reshape(3, rows, count, chans).transpose(2, 0, 3, 1))
    filt = regroup(taps.reshape(rows, count, chans).transpose(1, 2, 0))

    other = lax.ppermute(grad_out, "tp", [(0, 1), (1, 0)])
    first = lax.axis_index("tp") == 0
    whole = jnp.where(
        first,
        jnp.concatenate([grad_out, other], axis=1),
        jnp.concatenate([other, grad_out], axis=1),
    )
    gated = lax.dot_general(
        w_out, whole, (((1,), (1,)), ((), ())), preferred_element_type=jnp.float32
    )
    gated = regroup(gated.reshape(count, chans, rows))

    weight = lax.dynamic_slice_in_dim(short_weight, where * chans, chans, axis=2)
    weight = jnp.broadcast_to(weight.reshape(9, chans, 1), (9, chans, rows))

    inputs_grad, taps_grad, sums = convolve_all(streams, filt, gated, weight, scale)

    inputs_grad = regroup(inputs_grad).transpose(1, 3, 0, 2).reshape(3, rows, local)
    taps_grad = regroup(taps_grad).transpose(2, 0, 1).reshape(rows, local)
    sums = jnp.sum(sums, axis=2) * scale
    short_grad = lax.all_gather(sums, "ctx", axis=1, tiled=True).reshape(3, 3, local)
    return inputs_grad, taps_grad, short_grad


def solution(mesh):
    return jax.shard_map(
        shards,
        mesh=mesh,
        in_specs=(
            P(None, "ctx", "tp"),
            P(None, None, "tp"),
            P("ctx", "tp"),
            P("tp", None),
            P("ctx", "tp"),
        ),
        out_specs=(P(None, "ctx", "tp"), P("ctx", "tp"), P(None, None, "tp")),
        check_vma=False,
    )
```

time: 1270 us -> 241 us (0.19)
  waiting for transfers between devices: 697 us -> 36 us
  local copies, waits for them, and re-layouts: 146 us -> 13.8 us
  matrix products: 124 us -> 12.8 us
  blocking collectives: 214 us -> 116 us
  other arithmetic: 41.3 us -> 0.11 us
  Pallas kernels: 0 us -> 32.1 us
  between operations: 15 us -> 0.76 us
    psum x1 -> x0, waiting for transfers between devices: 474 us -> none  [shards(): short_grad = lax.psum(jnp.stack(sums, axis=1), 'ctx') * scale]
    all_to_all x2 -> x1, blocking collectives: 214 us -> 22.4 us  [regroup(): return lax.all_to_all(x, 'ctx', split_axis=0, concat_axis=0, tiled=True)]
    all_to_all x2 -> x4, waiting for transfers between devices: 204 us -> 32.5 us  [regroup(): return lax.all_to_all(x, 'ctx', split_axis=0, concat_axis=0, tiled=True)]
    dot_general x13 -> x1, matrix products: 124 us -> 12.8 us  [shards(): lax.dot_general(w_out, whole, (((1,), (1,)), ((), ())), preferred_element...]
    all_gather x0 -> x1, blocking collectives: none -> 93.3 us  [shards(): lax.all_gather(sums, 'ctx', axis=1, tiled=True).reshape(3, 3, local)]
    another operation x6 -> x0, local copies, waits for them, and re-layouts: 48.1 us -> none  [the longest x1 19.3 us: section_one(): jnp.stack([real_part * tw_re - imag_part * tw_im, real_part * tw_im + ima...]
    squeeze x6 -> x0, local copies, waits for them, and re-layouts: 43.7 us -> none  [the longest x2 20.6 us: section_two(): real_in, imag_in = (parts[0], parts[1])]
    slice x9 -> x0, local copies, waits for them, and re-layouts: 38.9 us -> none  [the longest x3 21.6 us: section_two(): real_in, imag_in = (parts[0], parts[1])]
  transfers between devices with their start and end apart: 6 -> 5, of which waited for: 5 -> 4; matrix products, arithmetic and copies ran while one was open for 1% -> 9% of each run, Pallas kernels for 0% -> 0%
where the time goes in v1:
time: 241 us; the launch traced here: 240 us
  blocking collectives  116 us (48%)
  waiting for transfers between devices  36 us (15%)
  Pallas kernels  32.1 us (13%)
  starting transfers between devices  29.1 us (12%)
  local copies, waits for them, and re-layouts  13.8 us (6%)
  matrix products  12.8 us (5%)
    all_gather x1, blocking collectives, shards(): lax.all_gather(sums, 'ctx', axis=1, tiled=True).reshape(3, 3, local)  93.3 us
    all_to_all x4, waiting for transfers between devices, regroup(): return lax.all_to_all(x, 'ctx', split_axis=0, concat_axis=0, tiled=True)  32.5 us
    pallas_call x1, Pallas kernels, convolve_all(): pl.pallas_call(lambda *refs: conv_kernel(scale, *refs), out_shape=(jax.Sh...  32.1 us
    all_to_all x4, starting transfers between devices, regroup(): return lax.all_to_all(x, 'ctx', split_axis=0, concat_axis=0, tiled=True)  26.4 us
    all_to_all x1, blocking collectives, regroup(): return lax.all_to_all(x, 'ctx', split_axis=0, concat_axis=0, tiled=True)  22.4 us
    dot_general x1, matrix products, shards(): lax.dot_general(w_out, whole, (((1,), (1,)), ((), ())), preferred_element...  12.8 us
    unnamed x17, local copies, waits for them, and re-layouts  7.7 us
  transfers between devices with their start and end apart: 5, of which 4 were waited for; matrix products, arithmetic and copies ran while one was open for 9% of the time, Pallas kernels for 0%

profile of v1, /device:TPU:1, one launch (start us, length us, event | category | flops | bytes accessed | tf_op | source)
XLA Modules:
  0.0 240.2 jit_solution(4506369576754382325)
XLA Ops:
  0.6 0.0 copy-start
  0.6 0.0 copy-start.5
  0.7 2.6 %copy.25 = f32[128,2048]{0,1:T(8,128)} copy(f32[128,2048]{1,0:T(8,128)} %param.12) | data formatting | bytes 2097152 | tf_op args[2]
  3.2 10.8 %all-to-all-start.1 = ((f32[64,32,128]{2,1,0:T(8,128)}), f32[64,32,128]{2,1,0:T(8,128)S(1)}, u32[]{:S(2)}, u32[]{:S(2)}) async-start(f32[64,32,128]{2,1,0:T(8,128)} %bitcast.3), calls=%async_computation.1 | async-start | bytes 2097152 | tf_op jit(solution)/shard_map/all_to_all | solution.py:212
  14.1 0.0 copy-done.5
  14.1 2.7 %collective-permute-start = (bf16[128,2048]{1,0:T(8,128)(2,1)S(1)}, bf16[128,2048]{1,0:T(8,128)(2,1)}, u32[]{:S(2)}, u32[]{:S(2)}) collective-permute-start(bf16[128,2048]{1,0:T(8,128)(2,1)S(1)} %copy-done.5), channel_id=1, source_target_pairs={{0,1},{1,0},{2,3},{3,2},{4,5},{5,4},{6,7},{7,6},{8,9},{9,8},{10,11... | collective-permute-start | bytes 1572872 | tf_op jit(solution)/shard_map/ppermute | solution.py:225
  16.8 1.9 copy.23
  18.7 1.4 copy.32
  20.1 11.3 %all-to-all-done.1.refs_1_ = f32[64,32,128]{2,1,0:T(8,128)S(1)} async-done(((f32[64,32,128]{2,1,0:T(8,128)}), f32[64,32,128]{2,1,0:T(8,128)S(1)}, u32[]{:S(2)}, u32[]{:S(2)}) %all-to-all-start.1) | async-done | bytes 1048608 | tf_op jit(solution)/shard_map/all_to_all | solution.py:212
  31.4 0.0 copy-start.2
  31.4 5.0 %all-to-all-start = ((bf16[64,3,32,128]{3,2,1,0:T(8,128)(2,1)}), bf16[64,3,32,128]{3,2,1,0:T(8,128)(2,1)S(1)}, u32[]{:S(2)}, u32[]{:S(2)}) async-start(bf16[64,3,32,128]{3,2,1,0:T(8,128)(2,1)} %bitcast.22), calls=%async_computation | async-start | bytes 3145728 | tf_op jit(solution)/shard_map/all_to_all | solution.py:212
  36.5 3.4 %collective-permute-done = bf16[128,2048]{1,0:T(8,128)(2,1)} collective-permute-done((bf16[128,2048]{1,0:T(8,128)(2,1)S(1)}, bf16[128,2048]{1,0:T(8,128)(2,1)}, u32[]{:S(2)}, u32[]{:S(2)}) %collective-permute-start) | collective-permute-done | bytes 524320 | tf_op jit(solution)/shard_map/ppermute | solution.py:225
  39.9 12.8 %convolution_bitcast_fusion = f32[2048,128]{0,1:T(8,128)} fusion(bf16[2048,4096]{1,0:T(8,128)(2,1)} %param.13, bf16[128,2048]{1,0:T(8,128)(2,1)} %collective-permute-done, bf16[128,2048]{1,0:T(8,128)(2,1)S(1)} %copy-done.5, pred[]{:T(512)S(6)} %eq.3), kind=kOutput, calls=%fused_computation | convolution fusion | flops 2152202240 | bytes 18874368 | tf_op jit(solution)/shard_map/dot_general | solution.py:232
  52.7 0.0 copy-done.2
  52.7 2.6 %copy.26 = f32[2048,128]{1,0:T(8,128)} copy(f32[2048,128]{0,1:T(8,128)} %convolution_bitcast_fusion) | data formatting | bytes 2097152 | tf_op jit(solution)/shard_map/dot_general | solution.py:232
  55.2 4.0 %all-to-all-done.refs_0_ = bf16[64,3,32,128]{3,2,1,0:T(8,128)(2,1)S(1)} async-done(((bf16[64,3,32,128]{3,2,1,0:T(8,128)(2,1)}), bf16[64,3,32,128]{3,2,1,0:T(8,128)(2,1)S(1)}, u32[]{:S(2)}, u32[]{:S(2)}) %all-to-all-start) | async-done | bytes 1572896 | tf_op jit(solution)/shard_map/all_to_all | solution.py:212
  59.2 0.0 copy-start.1
  59.3 5.3 %all-to-all-start.2 = ((f32[64,32,128]{2,1,0:T(8,128)}), f32[64,32,128]{2,1,0:T(8,128)S(1)}, u32[]{:S(2)}, u32[]{:S(2)}) async-start(f32[64,32,128]{2,1,0:T(8,128)} %bitcast.5), calls=%async_computation.2 | async-start | bytes 2097152 | tf_op jit(solution)/shard_map/all_to_all | solution.py:212
  64.6 0.0 copy-done
  64.6 0.1 constant_dynamic-slice_fusion
  64.7 17.2 %all-to-all-done.2.refs_2_ = f32[64,32,128]{2,1,0:T(8,128)S(1)} async-done(((f32[64,32,128]{2,1,0:T(8,128)}), f32[64,32,128]{2,1,0:T(8,128)S(1)}, u32[]{:S(2)}, u32[]{:S(2)}) %all-to-all-start.2) | async-done | bytes 1048608 | tf_op jit(solution)/shard_map/all_to_all | solution.py:212
  81.9 0.0 copy-start.3
  81.9 0.9 broadcast_in_dim.8.refs_3_
  82.8 0.0 copy-done.1
  82.8 0.1 copy-done.3
  83.0 32.1 %shard_map.121 = (bf16[64,3,32,128]{3,2,1,0:T(8,128)(2,1)}, f32[64,32,128]{2,1,0:T(8,128)}, f32[9,32,128]{2,1,0:T(8,128)}) custom-call(bf16[64,3,32,128]{3,2,1,0:T(8,128)(2,1)} %copy-done.1, f32[64,32,128]{2,1,0:T(8,128)} %copy-done.2, f32[64,32,128]{2,1,0:T(8,128)} %copy-done.3, f32[9,32,128]{2,1,0:T(8,128)} %broadcast_in_dim.8.refs_3_, ...), custom_call_target="tpu_custom_call" | custom-call | tf_op jit(solution)/shard_map/pallas_call | solution.py:194
  115.1 22.4 %all_to_all.25 = f32[64,32,128]{2,1,0:T(8,128)S(1)} all-to-all(f32[64,32,128]{2,1,0:T(8,128)} %get-tuple-element.7), channel_id=1, replica_groups=mesh['ctx'=64,'tp'=2] {'ctx'}, dimensions={0} | all-to-all | bytes 2097152 | tf_op jit(solution)/shard_map/all_to_all | solution.py:212
  137.5 0.0 copy-start.4
  137.5 5.2 %all-to-all-start.3 = ((bf16[64,3,32,128]{3,2,1,0:T(8,128)(2,1)}), bf16[64,3,32,128]{3,2,1,0:T(8,128)(2,1)S(1)}, u32[]{:S(2)}, u32[]{:S(2)}) async-start(bf16[64,3,32,128]{3,2,1,0:T(8,128)(2,1)} %get-tuple-element.6), calls=%async_computation.3 | async-start | bytes 3145728 | tf_op jit(solution)/shard_map/all_to_all | solution.py:212
  142.6 0.0 copy-done.4
  142.7 0.1 reduce_sum.9
  142.8 93.3 %all-gather = f32[64,32,9]{1,2,0:T(8,128)S(1)} all-gather(f32[1,32,9]{1,2,0:T(8,128)S(1)} %multiply_bitcast_fusion), channel_id=1, replica_groups=mesh['ctx'=64,'tp'=2] {'ctx'}, dimensions={0}, use_global_device_ids=true | all-gather | bytes 74880 | tf_op jit(solution)/shard_map/all_gather | solution.py:245
  236.1 0.1 copy.28
  236.2 0.2 reshape.33
  236.3 0.7 reshape.31
  237.0 1.3 copy.30
  238.3 0.0 all-to-all-done.3
  238.3 0.3 copy.27
  238.6 1.6 copy.29
  (2 shorter events, 0.0 us)
Async XLA Ops:
  0.6 64.0 %copy-start = (f32[3,3,2048]{2,1,0:T(4,128)S(1)}, f32[3,3,2048]{2,1,0:T(4,128)}, u32[]{:S(2)}) copy-start(f32[3,3,2048]{2,1,0:T(4,128)} %param.11) | copy-start | bytes 221188
  0.6 13.5 %copy-start.5 = (bf16[128,2048]{1,0:T(8,128)(2,1)S(1)}, bf16[128,2048]{1,0:T(8,128)(2,1)}, u32[]{:S(2)}) copy-start(bf16[128,2048]{1,0:T(8,128)(2,1)} %param.14) | copy-start | bytes 1572868
  3.2 28.2 %all-to-all-start.1 = ((f32[64,32,128]{2,1,0:T(8,128)}), f32[64,32,128]{2,1,0:T(8,128)S(1)}, u32[]{:S(2)}, u32[]{:S(2)}) async-start(f32[64,32,128]{2,1,0:T(8,128)} %bitcast.3), calls=%async_computation.1 | async-start | bytes 2097152 | tf_op jit(solution)/shard_map/all_to_all | solution.py:212
  14.1 25.8 %collective-permute-start = (bf16[128,2048]{1,0:T(8,128)(2,1)S(1)}, bf16[128,2048]{1,0:T(8,128)(2,1)}, u32[]{:S(2)}, u32[]{:S(2)}) collective-permute-start(bf16[128,2048]{1,0:T(8,128)(2,1)S(1)} %copy-done.5), channel_id=1, source_target_pairs={{0,1},{1,0},{2,3},{3,2},{4,5},{5,4},{6,7},{7,6},{8,9},{9,8},{10,11... | collective-permute-start | bytes 1572872 | tf_op jit(solution)/shard_map/ppermute | solution.py:225
  31.4 21.2 %copy-start.2 = (f32[64,32,128]{2,1,0:T(8,128)}, f32[64,32,128]{2,1,0:T(8,128)S(1)}, u32[]{:S(2)}) copy-start(f32[64,32,128]{2,1,0:T(8,128)S(1)} %all-to-all-done.1.refs_1_) | copy-start | bytes 3145732
  31.4 27.8 %all-to-all-start = ((bf16[64,3,32,128]{3,2,1,0:T(8,128)(2,1)}), bf16[64,3,32,128]{3,2,1,0:T(8,128)(2,1)S(1)}, u32[]{:S(2)}, u32[]{:S(2)}) async-start(bf16[64,3,32,128]{3,2,1,0:T(8,128)(2,1)} %bitcast.22), calls=%async_computation | async-start | bytes 3145728 | tf_op jit(solution)/shard_map/all_to_all | solution.py:212
  59.2 23.6 %copy-start.1 = (bf16[64,3,32,128]{3,2,1,0:T(8,128)(2,1)}, bf16[64,3,32,128]{3,2,1,0:T(8,128)(2,1)S(1)}, u32[]{:S(2)}) copy-start(bf16[64,3,32,128]{3,2,1,0:T(8,128)(2,1)S(1)} %all-to-all-done.refs_0_) | copy-start | bytes 4718596
  59.3 22.7 %all-to-all-start.2 = ((f32[64,32,128]{2,1,0:T(8,128)}), f32[64,32,128]{2,1,0:T(8,128)S(1)}, u32[]{:S(2)}, u32[]{:S(2)}) async-start(f32[64,32,128]{2,1,0:T(8,128)} %bitcast.5), calls=%async_computation.2 | async-start | bytes 2097152 | tf_op jit(solution)/shard_map/all_to_all | solution.py:212
  81.9 1.0 copy-start.3
  137.5 5.2 %copy-start.4 = (f32[9,32,128]{2,1,0:T(8,128)S(1)}, f32[9,32,128]{2,1,0:T(8,128)}, u32[]{:S(2)}) copy-start(f32[9,32,128]{2,1,0:T(8,128)} %get-tuple-element.8) | copy-start | bytes 442372
  137.5 100.8 %all-to-all-start.3 = ((bf16[64,3,32,128]{3,2,1,0:T(8,128)(2,1)}), bf16[64,3,32,128]{3,2,1,0:T(8,128)(2,1)S(1)}, u32[]{:S(2)}, u32[]{:S(2)}) async-start(bf16[64,3,32,128]{3,2,1,0:T(8,128)(2,1)} %get-tuple-element.6), calls=%async_computation.3 | async-start | bytes 3145728 | tf_op jit(solution)/shard_map/all_to_all | solution.py:212

commit v2 on v1

--- a/solution.py
+++ b/solution.py
@@ -70,11 +70,11 @@
     twiddle_ref,
     ig_ref,
     tg_ref,
-    sg_ref,
     src,
     res,
     key_ref,
     val_ref,
+    sums,
 ):
     blocks, _, chans, width = in_ref.shape
     lane = lax.broadcasted_iota(jnp.int32, (chans, width), 1)
@@ -167,13 +167,13 @@
         dz = res[1, at, :]
         return grad_ref[n1] * res[0, at, :], dz * val_ref[at, :], dz * key_ref[at, :]
 
-    sg_ref[...] = jnp.zeros_like(sg_ref)
+    sums[...] = jnp.zeros_like(sums)
 
     def finish(n1, cur):
         at = pl.ds(pl.multiple_of(n1 * chans, chans), chans)
         follow = gradients(jnp.minimum(n1 + 1, blocks - 1))
         follow = [jnp.where(n1 + 1 < blocks, f, zero) for f in follow]
-        tg_ref[n1] = res[2, at, :] * scale
+        tg_ref[n1, :chans] = res[2, at, :] * scale
         for b in range(3):
             parts = load(n1, b)
             out = weight_ref[3 * b] * cur[b]
@@ -182,10 +182,32 @@
                 out = out + weight_ref[3 * b + j] * moved
             ig_ref[n1, b] = out.astype(jnp.bfloat16)
             for j in range(3):
-                sg_ref[3 * b + j] += cur[b] * parts[j]
+                sums[3 * b + j] += cur[b] * parts[j]
         return tuple(follow)
 
     lax.fori_loop(0, blocks, finish, gradients(0))
+
+    total = jnp.zeros((chans, width), jnp.float32)
+    for t in range(9):
+        column = jnp.sum(sums[t], axis=1, keepdims=True) * scale
+        total = total + jnp.where(lane == t, column, 0.0)
+    total = jnp.concatenate([total] + [zero] * (width // chans - 1), axis=0).T
+    per = width // chans
+    packed = []
+    for r in range(8):
+        row = jnp.zeros((1, width), jnp.float32)
+        for a in range(per):
+            if per * r + a < 9:
+                line = total[per * r + a : per * r + a + 1]
+                row = row + (pltpu.roll(line, a * chans, 1) if a else line)
+        packed.append(row)
+    packed = jnp.concatenate(packed, axis=0)
+
+    def attach(n1, carry):
+        tg_ref[n1, chans:] = packed
+        return carry
+
+    lax.fori_loop(0, blocks, attach, 0)
 
 
 def convolve_all(inputs, taps, grad, weight, scale):
@@ -195,14 +217,14 @@
         lambda *refs: conv_kernel(scale, *refs),
         out_shape=(
             jax.ShapeDtypeStruct((blocks, 3, chans, width), jnp.bfloat16),
-            jax.ShapeDtypeStruct((blocks, chans, width), jnp.float32),
-            jax.ShapeDtypeStruct((9, chans, width), jnp.float32),
+            jax.ShapeDtypeStruct((blocks, chans + 8, width), jnp.float32),
         ),
         scratch_shapes=[
             pltpu.VMEM((3, blocks * chans, width), jnp.float32),
             pltpu.VMEM((3, blocks * chans, width), jnp.float32),
             pltpu.VMEM((blocks * chans, width), jnp.float32),
             pltpu.VMEM((blocks * chans, width), jnp.float32),
+            pltpu.VMEM((9, chans, width), jnp.float32),
         ],
         compiler_params=pltpu.CompilerParams(vmem_limit_bytes=56 << 20),
     )(inputs, taps, grad, weight, *consts)
@@ -237,12 +259,13 @@
     weight = lax.dynamic_slice_in_dim(short_weight, where * chans, chans, axis=2)
     weight = jnp.broadcast_to(weight.reshape(9, chans, 1), (9, chans, rows))
 
-    inputs_grad, taps_grad, sums = convolve_all(streams, filt, gated, weight, scale)
+    inputs_grad, taps_grad = convolve_all(streams, filt, gated, weight, scale)
 
     inputs_grad = regroup(inputs_grad).transpose(1, 3, 0, 2).reshape(3, rows, local)
-    taps_grad = regroup(taps_grad).transpose(2, 0, 1).reshape(rows, local)
-    sums = jnp.sum(sums, axis=2) * scale
-    short_grad = lax.all_gather(sums, "ctx", axis=1, tiled=True).reshape(3, 3, local)
+    taps_grad = regroup(taps_grad)
+    sums = taps_grad[:, chans:].reshape(count, 8 * rows)[:, : 9 * chans]
+    short_grad = sums.reshape(count, 9, chans).transpose(1, 0, 2).reshape(3, 3, local)
+    taps_grad = taps_grad[:, :chans].transpose(2, 0, 1).reshape(rows, local)
     return inputs_grad, taps_grad, short_grad
 
 

time: 241 us -> 172 us (0.71)
  blocking collectives: 116 us -> 24.8 us
  waiting for transfers between devices: 36 us -> 53.9 us
  local copies, waits for them, and re-layouts: 13.8 us -> 16.4 us
    all_gather x1 -> x0, blocking collectives: 93.3 us -> none  [shards(): lax.all_gather(sums, 'ctx', axis=1, tiled=True).reshape(3, 3, local)]
    all_to_all x4, waiting for transfers between devices: 32.5 us -> 50.4 us  [regroup(): return lax.all_to_all(x, 'ctx', split_axis=0, concat_axis=0, tiled=True)]
    all_to_all x1, blocking collectives: 22.4 us -> 24.8 us  [regroup(): return lax.all_to_all(x, 'ctx', split_axis=0, concat_axis=0, tiled=True)]
    unnamed x17 -> x14, local copies, waits for them, and re-layouts: 7.7 us -> 8.77 us
  transfers between devices with their start and end apart: 5 -> 5, of which waited for: 4 -> 5; matrix products, arithmetic and copies ran while one was open for 9% -> 14% of each run, Pallas kernels for 0% -> 0%
where the time goes in v2:
time: 172 us; the launch traced here: 171 us
  waiting for transfers between devices  53.9 us (31%)
  Pallas kernels  32.9 us (19%)
  starting transfers between devices  29.3 us (17%)
  blocking collectives  24.8 us (14%)
  local copies, waits for them, and re-layouts  16.4 us (10%)
  matrix products  12.8 us (7%)
    all_to_all x4, waiting for transfers between devices, regroup(): return lax.all_to_all(x, 'ctx', split_axis=0, concat_axis=0, tiled=True)  50.4 us
    pallas_call x1, Pallas kernels, convolve_all(): pl.pallas_call(lambda *refs: conv_kernel(scale, *refs), out_shape=(jax.Sh...  32.9 us
    all_to_all x4, starting transfers between devices, regroup(): return lax.all_to_all(x, 'ctx', split_axis=0, concat_axis=0, tiled=True)  26.6 us
    all_to_all x1, blocking collectives, regroup(): return lax.all_to_all(x, 'ctx', split_axis=0, concat_axis=0, tiled=True)  24.8 us
    dot_general x1, matrix products, shards(): lax.dot_general(w_out, whole, (((1,), (1,)), ((), ())), preferred_element...  12.8 us
    unnamed x14, local copies, waits for them, and re-layouts  8.77 us
  transfers between devices with their start and end apart: 5, of which 5 were waited for; matrix products, arithmetic and copies ran while one was open for 14% of the time, Pallas kernels for 0%

profile of v2, /device:TPU:1, one launch (start us, length us, event | category | flops | bytes accessed | tf_op | source)
XLA Modules:
  0.0 170.8 jit_solution(1572984914551212148)
XLA Ops:
  0.6 0.0 copy-start
  0.6 0.0 copy-start.4
  0.7 2.6 %copy.19 = f32[128,2048]{0,1:T(8,128)} copy(f32[128,2048]{1,0:T(8,128)} %param.12) | data formatting | bytes 2097152 | tf_op args[2]
  3.2 10.8 %all-to-all-start.1 = ((f32[64,32,128]{2,1,0:T(8,128)}), f32[64,32,128]{2,1,0:T(8,128)S(1)}, u32[]{:S(2)}, u32[]{:S(2)}) async-start(f32[64,32,128]{2,1,0:T(8,128)} %bitcast.3), calls=%async_computation.1 | async-start | bytes 2097152 | tf_op jit(solution)/shard_map/all_to_all | solution.py:234
  14.1 0.0 copy-done.4
  14.1 2.7 %collective-permute-start = (bf16[128,2048]{1,0:T(8,128)(2,1)S(1)}, bf16[128,2048]{1,0:T(8,128)(2,1)}, u32[]{:S(2)}, u32[]{:S(2)}) collective-permute-start(bf16[128,2048]{1,0:T(8,128)(2,1)S(1)} %copy-done.4), channel_id=1, source_target_pairs={{0,1},{1,0},{2,3},{3,2},{4,5},{5,4},{6,7},{7,6},{8,9},{9,8},{10,11... | collective-permute-start | bytes 1572872 | tf_op jit(solution)/shard_map/ppermute | solution.py:247
  16.8 1.9 %copy.17 = bf16[3,128,2048]{1,2,0:T(8,128)(2,1)S(1)} copy(bf16[3,128,2048]{2,1,0:T(8,128)(2,1)} %param.10) | data formatting | bytes 3145728 | tf_op args[0]
  18.7 1.4 copy.28
  20.1 11.3 %all-to-all-done.1.refs_1_ = f32[64,32,128]{2,1,0:T(8,128)S(1)} async-done(((f32[64,32,128]{2,1,0:T(8,128)}), f32[64,32,128]{2,1,0:T(8,128)S(1)}, u32[]{:S(2)}, u32[]{:S(2)}) %all-to-all-start.1) | async-done | bytes 1048608 | tf_op jit(solution)/shard_map/all_to_all | solution.py:234
  31.4 0.0 copy-start.2
  31.4 5.0 %all-to-all-start = ((bf16[64,3,32,128]{3,2,1,0:T(8,128)(2,1)}), bf16[64,3,32,128]{3,2,1,0:T(8,128)(2,1)S(1)}, u32[]{:S(2)}, u32[]{:S(2)}) async-start(bf16[64,3,32,128]{3,2,1,0:T(8,128)(2,1)} %bitcast.19), calls=%async_computation | async-start | bytes 3145728 | tf_op jit(solution)/shard_map/all_to_all | solution.py:234
  36.5 3.4 %collective-permute-done = bf16[128,2048]{1,0:T(8,128)(2,1)} collective-permute-done((bf16[128,2048]{1,0:T(8,128)(2,1)S(1)}, bf16[128,2048]{1,0:T(8,128)(2,1)}, u32[]{:S(2)}, u32[]{:S(2)}) %collective-permute-start) | collective-permute-done | bytes 524320 | tf_op jit(solution)/shard_map/ppermute | solution.py:247
  39.9 12.8 %convolution_bitcast_fusion = f32[2048,128]{0,1:T(8,128)} fusion(bf16[2048,4096]{1,0:T(8,128)(2,1)} %param.13, bf16[128,2048]{1,0:T(8,128)(2,1)} %collective-permute-done, bf16[128,2048]{1,0:T(8,128)(2,1)S(1)} %copy-done.4, pred[]{:T(512)S(6)} %eq.3), kind=kOutput, calls=%fused_computation | convolution fusion | flops 2152202240 | bytes 18874368 | tf_op jit(solution)/shard_map/dot_general | solution.py:254
  52.7 0.0 copy-done.2
  52.7 2.6 %copy.20 = f32[2048,128]{1,0:T(8,128)} copy(f32[2048,128]{0,1:T(8,128)} %convolution_bitcast_fusion) | data formatting | bytes 2097152 | tf_op jit(solution)/shard_map/dot_general | solution.py:254
  55.2 4.0 %all-to-all-done.refs_0_ = bf16[64,3,32,128]{3,2,1,0:T(8,128)(2,1)S(1)} async-done(((bf16[64,3,32,128]{3,2,1,0:T(8,128)(2,1)}), bf16[64,3,32,128]{3,2,1,0:T(8,128)(2,1)S(1)}, u32[]{:S(2)}, u32[]{:S(2)}) %all-to-all-start) | async-done | bytes 1572896 | tf_op jit(solution)/shard_map/all_to_all | solution.py:234
  59.2 0.0 copy-start.1
  59.3 5.3 %all-to-all-start.2 = ((f32[64,32,128]{2,1,0:T(8,128)}), f32[64,32,128]{2,1,0:T(8,128)S(1)}, u32[]{:S(2)}, u32[]{:S(2)}) async-start(f32[64,32,128]{2,1,0:T(8,128)} %bitcast.5), calls=%async_computation.2 | async-start | bytes 2097152 | tf_op jit(solution)/shard_map/all_to_all | solution.py:234
  64.6 0.0 copy-done
  64.6 0.1 constant_dynamic-slice_fusion
  64.7 17.2 %all-to-all-done.2.refs_2_ = f32[64,32,128]{2,1,0:T(8,128)S(1)} async-done(((f32[64,32,128]{2,1,0:T(8,128)}), f32[64,32,128]{2,1,0:T(8,128)S(1)}, u32[]{:S(2)}, u32[]{:S(2)}) %all-to-all-start.2) | async-done | bytes 1048608 | tf_op jit(solution)/shard_map/all_to_all | solution.py:234
  81.9 0.0 copy-start.3
  81.9 0.9 broadcast_in_dim.8.refs_3_
  82.8 0.0 copy-done.1
  82.8 0.1 copy-done.3
  83.0 32.9 %shard_map.121 = (bf16[64,3,32,128]{3,2,1,0:T(8,128)(2,1)}, f32[64,40,128]{2,1,0:T(8,128)}) custom-call(bf16[64,3,32,128]{3,2,1,0:T(8,128)(2,1)} %copy-done.1, f32[64,32,128]{2,1,0:T(8,128)} %copy-done.2, f32[64,32,128]{2,1,0:T(8,128)} %copy-done.3, f32[9,32,128]{2,1,0:T(8,128)} %broadcast_in_dim.8.refs_3_, bf16[128,192]{1,0:T(8,128)(2,1)} %constant.24.clone.refs_4_, ...), custom_call_target="tpu_custom_call" | custom-call | tf_op jit(solution)/shard_map/pallas_call | solution.py:216
  115.9 24.8 %all_to_all.25 = f32[64,40,128]{2,1,0:T(8,128)S(1)} all-to-all(f32[64,40,128]{2,1,0:T(8,128)} %get-tuple-element.6), channel_id=1, replica_groups=mesh['ctx'=64,'tp'=2] {'ctx'}, dimensions={0} | all-to-all | bytes 2621440 | tf_op jit(solution)/shard_map/all_to_all | solution.py:234
  140.7 5.4 %all-to-all-start.3 = ((bf16[64,3,32,128]{3,2,1,0:T(8,128)(2,1)}), bf16[64,3,32,128]{3,2,1,0:T(8,128)(2,1)S(1)}, u32[]{:S(2)}, u32[]{:S(2)}) async-start(bf16[64,3,32,128]{3,2,1,0:T(8,128)(2,1)} %get-tuple-element.5), calls=%async_computation.3 | async-start | bytes 3145728 | tf_op jit(solution)/shard_map/all_to_all | solution.py:234
  146.1 1.1 slice.12
  147.2 2.5 %copy.25 = f32[128,2048]{1,0:T(8,128)} copy(f32[128,2048]{0,1:T(8,128)} %bitcast.23) | data formatting | bytes 2097152
  149.8 0.2 copy.26
  150.0 0.2 copy.23
  150.2 0.8 reshape.39
  151.0 17.9 %all-to-all-done.3 = bf16[64,3,32,128]{3,2,1,0:T(8,128)(2,1)S(1)} async-done(((bf16[64,3,32,128]{3,2,1,0:T(8,128)(2,1)}), bf16[64,3,32,128]{3,2,1,0:T(8,128)(2,1)S(1)}, u32[]{:S(2)}, u32[]{:S(2)}) %all-to-all-start.3) | async-done | bytes 1572896 | tf_op jit(solution)/shard_map/all_to_all | solution.py:234
  168.9 0.3 copy.21
  169.2 1.6 copy.24
  (3 shorter events, 0.0 us)
Async XLA Ops:
  0.6 64.0 %copy-start = (f32[3,3,2048]{2,1,0:T(4,128)S(1)}, f32[3,3,2048]{2,1,0:T(4,128)}, u32[]{:S(2)}) copy-start(f32[3,3,2048]{2,1,0:T(4,128)} %param.11) | copy-start | bytes 221188
  0.6 13.5 %copy-start.4 = (bf16[128,2048]{1,0:T(8,128)(2,1)S(1)}, bf16[128,2048]{1,0:T(8,128)(2,1)}, u32[]{:S(2)}) copy-start(bf16[128,2048]{1,0:T(8,128)(2,1)} %param.14) | copy-start | bytes 1572868
  3.2 28.2 %all-to-all-start.1 = ((f32[64,32,128]{2,1,0:T(8,128)}), f32[64,32,128]{2,1,0:T(8,128)S(1)}, u32[]{:S(2)}, u32[]{:S(2)}) async-start(f32[64,32,128]{2,1,0:T(8,128)} %bitcast.3), calls=%async_computation.1 | async-start | bytes 2097152 | tf_op jit(solution)/shard_map/all_to_all | solution.py:234
  14.1 25.8 %collective-permute-start = (bf16[128,2048]{1,0:T(8,128)(2,1)S(1)}, bf16[128,2048]{1,0:T(8,128)(2,1)}, u32[]{:S(2)}, u32[]{:S(2)}) collective-permute-start(bf16[128,2048]{1,0:T(8,128)(2,1)S(1)} %copy-done.4), channel_id=1, source_target_pairs={{0,1},{1,0},{2,3},{3,2},{4,5},{5,4},{6,7},{7,6},{8,9},{9,8},{10,11... | collective-permute-start | bytes 1572872 | tf_op jit(solution)/shard_map/ppermute | solution.py:247
  31.4 21.2 %copy-start.2 = (f32[64,32,128]{2,1,0:T(8,128)}, f32[64,32,128]{2,1,0:T(8,128)S(1)}, u32[]{:S(2)}) copy-start(f32[64,32,128]{2,1,0:T(8,128)S(1)} %all-to-all-done.1.refs_1_) | copy-start | bytes 3145732
  31.4 27.8 %all-to-all-start = ((bf16[64,3,32,128]{3,2,1,0:T(8,128)(2,1)}), bf16[64,3,32,128]{3,2,1,0:T(8,128)(2,1)S(1)}, u32[]{:S(2)}, u32[]{:S(2)}) async-start(bf16[64,3,32,128]{3,2,1,0:T(8,128)(2,1)} %bitcast.19), calls=%async_computation | async-start | bytes 3145728 | tf_op jit(solution)/shard_map/all_to_all | solution.py:234
  59.2 23.6 %copy-start.1 = (bf16[64,3,32,128]{3,2,1,0:T(8,128)(2,1)}, bf16[64,3,32,128]{3,2,1,0:T(8,128)(2,1)S(1)}, u32[]{:S(2)}) copy-start(bf16[64,3,32,128]{3,2,1,0:T(8,128)(2,1)S(1)} %all-to-all-done.refs_0_) | copy-start | bytes 4718596
  59.3 22.7 %all-to-all-start.2 = ((f32[64,32,128]{2,1,0:T(8,128)}), f32[64,32,128]{2,1,0:T(8,128)S(1)}, u32[]{:S(2)}, u32[]{:S(2)}) async-start(f32[64,32,128]{2,1,0:T(8,128)} %bitcast.5), calls=%async_computation.2 | async-start | bytes 2097152 | tf_op jit(solution)/shard_map/all_to_all | solution.py:234
  81.9 1.0 copy-start.3
  140.7 28.2 %all-to-all-start.3 = ((bf16[64,3,32,128]{3,2,1,0:T(8,128)(2,1)}), bf16[64,3,32,128]{3,2,1,0:T(8,128)(2,1)S(1)}, u32[]{:S(2)}, u32[]{:S(2)}) async-start(bf16[64,3,32,128]{3,2,1,0:T(8,128)(2,1)} %get-tuple-element.5), calls=%async_computation.3 | async-start | bytes 3145728 | tf_op jit(solution)/shard_map/all_to_all | solution.py:234

commit v3 on v2

v3 whole, which is shorter than its diff:
```python
import math

import jax
import jax.numpy as jnp
import numpy as np
from jax import lax
from jax.experimental import pallas as pl
from jax.experimental.pallas import tpu as pltpu
from jax.sharding import PartitionSpec as P

GROUP = 4
UNROLL = 4


def split_np(x):
    high = x.astype(jnp.bfloat16)
    low = (x - high.astype(np.float64)).astype(jnp.bfloat16)
    return high, low


def tables(blocks, width):
    length = 2 * blocks * width
    n1 = np.arange(blocks)
    n2 = np.arange(width)
    angle = 2.0 * np.pi * np.outer(n1 + 0.5, n1) / (2 * blocks)
    first = np.concatenate([np.cos(angle), -np.sin(angle)], axis=0)
    high, low = split_np(first)
    first3 = np.concatenate([high, high, low], axis=1)
    last = first.T * (2.0 / length)
    high, low = split_np(last)
    last4 = np.concatenate(
        [
            np.concatenate([high, high], axis=1),
            np.concatenate([low, np.zeros_like(low)], axis=1),
        ],
        axis=0,
    )
    angle = 2.0 * np.pi * (np.outer(n2, n2) % width) / width
    cos, sin = np.cos(angle), np.sin(angle)
    forward = np.block([[cos, -sin], [sin, cos]])
    high, low = split_np(forward)
    forward3 = np.concatenate([high, high, low], axis=0)
    backward = np.block([[cos, sin], [-sin, cos]])
    high, low = split_np(backward)
    backward3 = np.concatenate([high, high, low], axis=0)
    angle = 2.0 * np.pi * np.outer(n1 + 0.5, n2) / length
    twiddle = np.stack([np.cos(angle), np.sin(angle)]).astype(np.float32)
    return first3, last4, forward3, backward3, twiddle


def split(x):
    high = x.astype(jnp.bfloat16)
    low = (x - high.astype(jnp.float32)).astype(jnp.bfloat16)
    return high, low


def mm(a, b):
    return jnp.dot(a, b, preferred_element_type=jnp.float32)


def forward_rows(x_of, first_ref, cos, sin, blocks, width):
    rows = []
    for g in range(0, GROUP, 2):
        cols = []
        for h in (0, 1):
            high, low = split(x_of(g + h))
            cols.append(jnp.concatenate([high, low, high], axis=0))
        out = mm(first_ref[...], jnp.concatenate(cols, axis=1))
        for h in (0, 1):
            re = out[:blocks, h * width : (h + 1) * width]
            im = out[blocks:, h * width : (h + 1) * width]
            rows.append(jnp.concatenate([re * cos + im * sin, im * cos - re * sin], axis=1))
    return rows


def step_two(rows, table_ref):
    high, low = split(rows)
    return mm(jnp.concatenate([high, low, high], axis=1), table_ref[...])


def inverse_one(back, put, last_ref, cos, sin, blocks, width):
    for g in range(0, GROUP, 2):
        cols = []
        for h in (0, 1):
            at = (g + h) * blocks
            re = back[at : at + blocks, :width]
            im = back[at : at + blocks, width:]
            both = jnp.concatenate([re * cos - im * sin, re * sin + im * cos], axis=0)
            high, low = split(both)
            cols.append(jnp.concatenate([high, low], axis=0))
        out = mm(last_ref[...], jnp.concatenate(cols, axis=1))
        out = out[:blocks] + out[blocks:]
        for h in (0, 1):
            put(g + h, out[:, h * width : (h + 1) * width])


def times(a, b, width):
    ar, ai, br, bi = a[:, :width], a[:, width:], b[:, :width], b[:, width:]
    return jnp.concatenate([ar * br - ai * bi, ar * bi + ai * br], axis=1)


def conj_times(a, b, width):
    ar, ai, br, bi = a[:, :width], a[:, width:], b[:, :width], b[:, width:]
    return jnp.concatenate([ar * br + ai * bi, ar * bi - ai * br], axis=1)


def row_of(n1, chans):
    return pl.ds(pl.multiple_of(n1 * chans, chans), chans)


def lagged(in_ref, n1, b, chans, width):
    lane = lax.broadcasted_iota(jnp.int32, (chans, width), 1)
    at = pl.ds(b * chans, chans)
    cur = in_ref[n1, at, :].astype(jnp.float32)
    before = in_ref[jnp.maximum(n1 - 1, 0), at, :].astype(jnp.float32)
    before = jnp.where(n1 > 0, before, 0.0)
    return [cur] + [
        pltpu.roll(jnp.where(lane >= width - j, before, cur), j, 1) for j in (1, 2)
    ]


def ahead(weights, cur, follow, chans, width):
    lane = lax.broadcasted_iota(jnp.int32, (chans, width), 1)
    out = weights[0] * cur
    for j in (1, 2):
        moved = pltpu.roll(jnp.where(lane < j, follow, cur), width - j, 1)
        out = out + weights[j] * moved
    return out


def first_kernel(
    scale,
    in_ref,
    weight_ref,
    first_ref,
    last_ref,
    forward_ref,
    backward_ref,
    twiddle_ref,
    mixed_ref,
    filt_ref,
    prod_ref,
    conv_ref,
    src,
):
    blocks, width = in_ref.shape[0], in_ref.shape[2]
    chans = weight_ref.shape[1]

    def prepare(step, carry):
        for u in range(UNROLL):
            n1 = step * UNROLL + u
            at = row_of(n1, chans)
            mixed = []
            for b in range(3):
                parts = lagged(in_ref, n1, b, chans, width)
                mixed.append(
                    weight_ref[3 * b] * parts[0]
                    + weight_ref[3 * b + 1] * parts[1]
                    + weight_ref[3 * b + 2] * parts[2]
                )
                mixed_ref[b, at, :] = mixed[b]
            taps = in_ref[n1, pl.ds(3 * chans, chans), :].astype(jnp.float32)
            taps = taps + in_ref[n1, pl.ds(4 * chans, chans), :].astype(jnp.float32)
            src[0, at, :] = taps * scale
            src[1, at, :] = mixed[1] * mixed[2]
        return carry

    lax.fori_loop(0, blocks // UNROLL, prepare, 0)
    cos, sin = twiddle_ref[0], twiddle_ref[1]

    def convolve(step, carry):
        base = step * GROUP
        part = GROUP * blocks
        rows = []
        for s in range(2):
            rows += forward_rows(
                lambda g: src[s, pl.ds(base + g, blocks, stride=chans), :],
                first_ref,
                cos,
                sin,
                blocks,
                width,
            )
        spec = step_two(jnp.concatenate(rows, axis=0), forward_ref)
        at = row_of(step, part)
        filt_ref[at, :] = spec[:part]
        prod_ref[at, :] = spec[part:]
        back = step_two(times(spec[:part], spec[part:], width), backward_ref)

        def put(g, out):
            conv_ref[pl.ds(base + g, blocks, stride=chans), :] = out

        inverse_one(back, put, last_ref, cos, sin, blocks, width)
        return carry

    lax.fori_loop(0, chans // GROUP, convolve, 0)


def query_kernel(grad_ref, conv_ref, weight_ref, ig_ref):
    blocks, chans, width = grad_ref.shape
    weights = [weight_ref[j] for j in range(3)]

    def dm(n1):
        return grad_ref[n1] * conv_ref[row_of(n1, chans), :]

    def finish(step, cur):
        for u in range(UNROLL):
            n1 = step * UNROLL + u
            follow = dm(jnp.minimum(n1 + 1, blocks - 1))
            if u == UNROLL - 1:
                follow = jnp.where(n1 + 1 < blocks, follow, 0.0)
            ig_ref[n1] = ahead(weights, cur, follow, chans, width).astype(jnp.bfloat16)
            cur = follow
        return cur

    lax.fori_loop(0, blocks // UNROLL, finish, dm(0))


def last_kernel(
    scale,
    grad_ref,
    in_ref,
    mixed_ref,
    filt_ref,
    prod_ref,
    conv_ref,
    weight_ref,
    first_ref,
    last_ref,
    forward_ref,
    backward_ref,
    twiddle_ref,
    out_ref,
    src,
    res,
    sums,
):
    blocks, chans, width = grad_ref.shape
    lane = lax.broadcasted_iota(jnp.int32, (chans, width), 1)

    def prepare(step, carry):
        for u in range(UNROLL):
            n1 = step * UNROLL + u
            at = row_of(n1, chans)
            src[at, :] = grad_ref[n1] * mixed_ref[0, at, :]
        return carry

    lax.fori_loop(0, blocks // UNROLL, prepare, 0)
    cos, sin = twiddle_ref[0], twiddle_ref[1]

    def convolve(step, carry):
        base = step * GROUP
        part = GROUP * blocks
        rows = forward_rows(
            lambda g: src[pl.ds(base + g, blocks, stride=chans), :],
            first_ref,
            cos,
            sin,
            blocks,
            width,
        )
        spec = step_two(jnp.concatenate(rows, axis=0), forward_ref)
        at = row_of(step, part)
        both = [conj_times(r[at, :], spec, width) for r in (filt_ref, prod_ref)]
        back = step_two(jnp.concatenate(both, axis=0), backward_ref)
        for s in range(2):

            def put(g, out):
                res[s, pl.ds(base + g, blocks, stride=chans), :] = out

            inverse_one(
                back[s * part : (s + 1) * part], put, last_ref, cos, sin, blocks, width
            )
        return carry

    lax.fori_loop(0, chans // GROUP, convolve, 0)

    def gradients(n1):
        at = row_of(n1, chans)
        dz = res[0, at, :]
        return [dz * mixed_ref[2, at, :], dz * mixed_ref[1, at, :]]

    sums[...] = jnp.zeros_like(sums)

    def finish(step, cur):
        cur = list(cur)
        adds = [None] * 9
        for u in range(UNROLL):
            n1 = step * UNROLL + u
            at = row_of(n1, chans)
            follow = gradients(jnp.minimum(n1 + 1, blocks - 1))
            if u == UNROLL - 1:
                follow = [jnp.where(n1 + 1 < blocks, f, 0.0) for f in follow]
            for b in (1, 2):
                weights = [weight_ref[3 * b + j] for j in range(3)]
                out = ahead(weights, cur[b - 1], follow[b - 1], chans, width)
                out_ref[n1, pl.ds((b - 1) * chans, chans), :] = out.astype(jnp.bfloat16)
            high, low = split(res[1, at, :] * scale)
            out_ref[n1, pl.ds(2 * chans, chans), :] = high
            out_ref[n1, pl.ds(3 * chans, chans), :] = low
            full = [grad_ref[n1] * conv_ref[at, :]] + cur
            for b in range(3):
                parts = lagged(in_ref, n1, b, chans, width)
                for j in range(3):
                    term = full[b] * parts[j]
                    old = adds[3 * b + j]
                    adds[3 * b + j] = term if old is None else old + term
            cur = follow
        for t in range(9):
            sums[t] += adds[t]
        return tuple(cur)

    lax.fori_loop(0, blocks // UNROLL, finish, tuple(gradients(0)))

    total = jnp.zeros((chans, width), jnp.float32)
    for t in range(9):
        column = jnp.sum(sums[t], axis=1, keepdims=True) * scale
        total = total + jnp.where(lane == t, column, 0.0)
    per = width // chans
    total = jnp.concatenate([total] + [jnp.zeros_like(total)] * (per - 1), axis=0).T
    high = total.astype(jnp.bfloat16).astype(jnp.float32)
    mid = (total - high).astype(jnp.bfloat16).astype(jnp.float32)
    low = total - high - mid
    lines = [p[t : t + 1] for p in (high, mid, low) for t in range(9)]
    packed = []
    for r in range(8):
        row = jnp.zeros((1, width), jnp.float32)
        for a, line in enumerate(lines[per * r : per * r + per]):
            row = row + (pltpu.roll(line, a * chans, 1) if a else line)
        packed.append(row)
    packed = jnp.concatenate(packed, axis=0).astype(jnp.bfloat16)

    def attach(n1, carry):
        out_ref[n1, pl.ds(4 * chans, 8), :] = packed
        return carry

    lax.fori_loop(0, blocks, attach, 0)


def f32(*shape):
    return jax.ShapeDtypeStruct(shape, jnp.float32)


def bf16(*shape):
    return jax.ShapeDtypeStruct(shape, jnp.bfloat16)


def estimate(us):
    return pl.CostEstimate(flops=int(us * 1e8), bytes_accessed=int(us * 3e6), transcendentals=0)


def params(mib):
    return pltpu.CompilerParams(vmem_limit_bytes=mib << 20)


def stage_one(streams, weight, consts, scale):
    blocks, width = streams.shape[0], streams.shape[2]
    chans = weight.shape[1]
    rows = blocks * chans
    return pl.pallas_call(
        lambda *refs: first_kernel(scale, *refs),
        name="stage_one",
        out_shape=(
            f32(3, rows, width),
            f32(rows, 2 * width),
            f32(rows, 2 * width),
            f32(rows, width),
        ),
        scratch_shapes=[pltpu.VMEM((2, rows, width), jnp.float32)],
        cost_estimate=estimate(14),
        compiler_params=params(24),
    )(streams, weight, *consts)


def stage_two(grad, conv, weight):
    return pl.pallas_call(
        query_kernel,
        name="stage_two",
        out_shape=bf16(*grad.shape),
        cost_estimate=estimate(3),
        compiler_params=params(8),
    )(grad, conv, weight)


def stage_three(grad, streams, mixed, filt, prod, conv, weight, consts, scale):
    blocks, chans, width = grad.shape
    rows = blocks * chans
    return pl.pallas_call(
        lambda *refs: last_kernel(scale, *refs),
        name="stage_three",
        out_shape=bf16(blocks, 4 * chans + 8, width),
        scratch_shapes=[
            pltpu.VMEM((rows, width), jnp.float32),
            pltpu.VMEM((2, rows, width), jnp.float32),
            pltpu.VMEM((9, chans, width), jnp.float32),
        ],
        cost_estimate=estimate(14),
        compiler_params=params(32),
    )(grad, streams, mixed, filt, prod, conv, weight, *consts)


def regroup(x):
    return lax.all_to_all(x, "ctx", split_axis=0, concat_axis=0, tiled=True)


def shards(inputs, short_weight, taps, w_out, grad_out):
    rows, local = inputs.shape[1], inputs.shape[2]
    count = lax.axis_size("ctx")
    where = lax.axis_index("ctx")
    chans = local // count
    scale = 1.0 / math.sqrt(count * rows)

    high = lax.reduce_precision(taps, 8, 7)
    low = (taps - high).astype(jnp.bfloat16)
    streams = jnp.concatenate([inputs, high.astype(jnp.bfloat16)[None], low[None]], axis=0)
    streams = streams.reshape(5, rows, count, chans).transpose(2, 0, 3, 1)
    streams = regroup(streams.reshape(count, 5 * chans, rows))

    other = lax.ppermute(grad_out, "tp", [(0, 1), (1, 0)])
    first = lax.axis_index("tp") == 0
    whole = jnp.where(
        first,
        jnp.concatenate([grad_out, other], axis=1),
        jnp.concatenate([other, grad_out], axis=1),
    )
    gated = lax.dot_general(
        w_out, whole, (((1,), (1,)), ((), ())), preferred_element_type=jnp.float32
    )
    gated = regroup(gated.reshape(count, chans, rows))

    weight = lax.dynamic_slice_in_dim(short_weight, where * chans, chans, axis=2)
    weight = jnp.broadcast_to(weight.reshape(9, chans, 1), (9, chans, rows))

    consts = [jnp.asarray(t) for t in tables(count, rows)]
    mixed, filt, prod, conv = stage_one(streams, weight, consts, scale)
    query = stage_two(gated, conv, weight)
    query, gated, mixed = lax.optimization_barrier((query, gated, mixed))
    rest = stage_three(gated, streams, mixed, filt, prod, conv, weight, consts, scale)

    query = regroup(query)
    query, rest = lax.optimization_barrier((query, rest))
    rest = regroup(rest)
    grads = jnp.stack(
        [query, rest[:, :chans], rest[:, chans : 2 * chans]], axis=1
    )
    inputs_grad = grads.transpose(1, 3, 0, 2).reshape(3, rows, local)
    taps_grad = rest[:, 2 * chans : 3 * chans].astype(jnp.float32)
    taps_grad = taps_grad + rest[:, 3 * chans : 4 * chans].astype(jnp.float32)
    taps_grad = taps_grad.transpose(2, 0, 1).reshape(rows, local)
    sums = rest[:, 4 * chans :].astype(jnp.float32)
    sums = sums.reshape(count, 8 * rows)[:, : 27 * chans].reshape(count, 3, 9, chans)
    short_grad = jnp.sum(sums, axis=1).transpose(1, 0, 2).reshape(3, 3, local)
    return inputs_grad, taps_grad, short_grad


def solution(mesh):
    return jax.shard_map(
        shards,
        mesh=mesh,
        in_specs=(
            P(None, "ctx", "tp"),
            P(None, None, "tp"),
            P("ctx", "tp"),
            P("tp", None),
            P("ctx", "tp"),
        ),
        out_specs=(P(None, "ctx", "tp"), P("ctx", "tp"), P(None, None, "tp")),
        check_vma=False,
    )
```

time: 172 us -> 191 us (1.11)
  blocking collectives: 24.8 us -> 39.9 us
  waiting for transfers between devices: 53.9 us -> 40.6 us
  local copies, waits for them, and re-layouts: 16.4 us -> 29.6 us
  starting transfers between devices: 29.3 us -> 32.5 us
  other arithmetic: 0 us -> 3.05 us
  Pallas kernels: 32.9 us -> 30.3 us
    all_to_all x4 -> x3, waiting for transfers between devices: 50.4 us -> 0.01 us  [regroup(): return lax.all_to_all(x, 'ctx', split_axis=0, concat_axis=0, tiled=True)]
    ppermute x1, waiting for transfers between devices: 3.43 us -> 40.6 us  [shards(): other = lax.ppermute(grad_out, 'tp', [(0, 1), (1, 0)])]
    all_to_all x1, blocking collectives: 24.8 us -> 39.9 us  [regroup(): return lax.all_to_all(x, 'ctx', split_axis=0, concat_axis=0, tiled=True)]
    unnamed x14 -> x40, local copies, waits for them, and re-layouts: 8.77 us -> 23.6 us
    all_to_all x4 -> x3, starting transfers between devices: 26.6 us -> 29.8 us  [regroup(): return lax.all_to_all(x, 'ctx', split_axis=0, concat_axis=0, tiled=True)]
    pallas_call x1 -> x3, Pallas kernels: 32.9 us -> 30.3 us  [the longest x1 15.2 us: stage_three(): pl.pallas_call(lambda *refs: last_kernel(scale, *refs), name='stage_three...]
    another operation x0 -> x1, other arithmetic: none -> 2.38 us  [shards(): jnp.stack([query, rest[:, :chans], rest[:, chans:2 * chans]], axis=1)]
  transfers between devices with their start and end apart: 5 -> 4, of which waited for: 5 -> 1; matrix products, arithmetic and copies ran while one was open for 14% -> 8% of each run, Pallas kernels for 0% -> 14%
where the time goes in v3:
time: 191 us; the launch traced here: 190 us
  waiting for transfers between devices  40.6 us (21%)
  blocking collectives  39.9 us (21%)
  starting transfers between devices  32.5 us (17%)
  Pallas kernels  30.3 us (16%)
  local copies, waits for them, and re-layouts  29.6 us (15%)
  matrix products  12.8 us (7%)
  other arithmetic  3.05 us (2%)
    ppermute x1, waiting for transfers between devices, shards(): other = lax.ppermute(grad_out, 'tp', [(0, 1), (1, 0)])  40.6 us
    all_to_all x1, blocking collectives, regroup(): return lax.all_to_all(x, 'ctx', split_axis=0, concat_axis=0, tiled=True)  39.9 us
    all_to_all x3, starting transfers between devices, regroup(): return lax.all_to_all(x, 'ctx', split_axis=0, concat_axis=0, tiled=True)  29.8 us
    unnamed x40, local copies, waits for them, and re-layouts  23.6 us
    pallas_call x1, Pallas kernels, stage_three(): pl.pallas_call(lambda *refs: last_kernel(scale, *refs), name='stage_three...  15.2 us
    dot_general x1, matrix products, shards(): lax.dot_general(w_out, whole, (((1,), (1,)), ((), ())), preferred_element...  12.8 us
    pallas_call x1, Pallas kernels, stage_one(): pl.pallas_call(lambda *refs: first_kernel(scale, *refs), name='stage_one'...  11.4 us
  transfers between devices with their start and end apart: 4, of which 1 were waited for; matrix products, arithmetic and copies ran while one was open for 8% of the time, Pallas kernels for 14%

profile of v3, /device:TPU:1, one launch (start us, length us, event | category | flops | bytes accessed | tf_op | source)
XLA Modules:
  0.0 189.5 jit_solution(9557427542646324277)
XLA Ops:
  0.6 0.0 copy-start
  0.6 1.6 copy.29
  2.2 0.2 reduce-precision_convert_fusion
  2.4 1.9 %copy.28 = bf16[3,128,2048]{1,2,0:T(8,128)(2,1)S(1)} copy(bf16[3,128,2048]{2,1,0:T(8,128)(2,1)} %param.10) | data formatting | bytes 3145728 | tf_op args[0]
  4.3 0.3 maximum_bitcast_fusion
  4.6 2.0 %copy.31 = bf16[64,5,32,128]{3,2,1,0:T(8,128)(2,1)} copy(bf16[64,5,32,128]{3,2,0,1:T(8,128)(2,1)S(1)} %maximum_bitcast_fusion) | data formatting | bytes 5242880 | tf_op jit(solution)/shard_map/transpose | solution.py:416
  6.6 0.0 copy-start.17
  6.6 11.0 %all-to-all-start.1 = ((bf16[64,160,128]{2,1,0:T(8,128)(2,1)}), bf16[64,160,128]{2,1,0:T(8,128)(2,1)S(1)}, u32[]{:S(2)}, u32[]{:S(2)}) async-start(bf16[64,160,128]{2,1,0:T(8,128)(2,1)} %bitcast.25), calls=%async_computation.1 | async-start | bytes 5242880 | tf_op jit(solution)/shard_map/all_to_all | solution.py:403
  17.6 0.0 copy-done.17
  17.6 2.7 %collective-permute-start = (bf16[128,2048]{1,0:T(8,128)(2,1)S(1)}, bf16[128,2048]{1,0:T(8,128)(2,1)}, u32[]{:S(2)}, u32[]{:S(2)}) collective-permute-start(bf16[128,2048]{1,0:T(8,128)(2,1)S(1)} %copy-done.17), channel_id=1, source_target_pairs={{0,1},{1,0},{2,3},{3,2},{4,5},{5,4},{6,7},{7,6},{8,9},{9,8},{10,11... | collective-permute-start | bytes 1572872 | tf_op jit(solution)/shard_map/ppermute | solution.py:419
  20.3 40.6 %collective-permute-done = bf16[128,2048]{1,0:T(8,128)(2,1)} collective-permute-done((bf16[128,2048]{1,0:T(8,128)(2,1)S(1)}, bf16[128,2048]{1,0:T(8,128)(2,1)}, u32[]{:S(2)}, u32[]{:S(2)}) %collective-permute-start) | collective-permute-done | bytes 524320 | tf_op jit(solution)/shard_map/ppermute | solution.py:419
  60.9 12.8 %convolution_bitcast_fusion = f32[2048,128]{0,1:T(8,128)} fusion(bf16[2048,4096]{1,0:T(8,128)(2,1)} %param.13, bf16[128,2048]{1,0:T(8,128)(2,1)} %collective-permute-done, bf16[128,2048]{1,0:T(8,128)(2,1)S(1)} %copy-done.17, pred[]{:T(512)S(6)} %eq.3), kind=kOutput, calls=%fused_computation.1 | convolution fusion | flops 2152202240 | bytes 18874368 | tf_op jit(solution)/shard_map/dot_general | solution.py:426
  73.6 0.0 copy-start.11
  73.6 0.0 copy-start.14
  73.6 0.0 copy-start.15
  73.6 0.0 copy-start.16
  73.6 2.6 %copy.27 = f32[2048,128]{1,0:T(8,128)} copy(f32[2048,128]{0,1:T(8,128)} %convolution_bitcast_fusion) | data formatting | bytes 2097152 | tf_op jit(solution)/shard_map/dot_general | solution.py:426
  76.2 0.0 all-to-all-done.1.refs_0_.refs_1_
  76.2 9.7 %all-to-all-start = ((f32[64,32,128]{2,1,0:T(8,128)}), f32[64,32,128]{2,1,0:T(8,128)}, u32[]{:S(2)}, u32[]{:S(2)}) async-start(f32[64,32,128]{2,1,0:T(8,128)} %bitcast.28), calls=%async_computation | async-start | bytes 2097152 | tf_op jit(solution)/shard_map/all_to_all | solution.py:403
  86.0 0.0 copy-done
  86.0 0.1 constant_dynamic-slice_fusion
  86.1 0.1 broadcast_in_dim.10.refs_1_.weight_ref.refs_6_
  86.2 0.0 copy-done.11
  86.2 0.0 copy-done.14
  86.2 0.0 copy-done.15
  86.2 0.0 copy-done.16
  86.2 0.0 copy-start.12
  86.2 1.0 copy-done.12
  87.2 11.4 %stage_one.1 = (f32[3,2048,128]{2,1,0:T(8,128)S(1)}, f32[2048,256]{1,0:T(8,128)S(1)}, f32[2048,256]{1,0:T(8,128)S(1)}, f32[2048,128]{1,0:T(8,128)S(1)}) custom-call(bf16[64,160,128]{2,1,0:T(8,128)(2,1)S(1)} %all-to-all-done.1.refs_0_.refs_1_, f32[9,32,128]{2,1,0:T(8,128)S(1)} %broadcast_in_dim.10.refs_1_.weight_ref.refs_6_, bf16[128,192]{1,0:T(8,128)(2,1)S(1)} %copy-done.14, ...), custom_call_target="tpu_custom_call" | custom-call | flops 1400000000 | bytes 42000000 | tf_op jit(solution)/shard_map/stage_one/pallas_call | solution.py:360
  98.6 0.0 copy-start.2
  98.6 1.0 copy-done.2
  99.5 0.0 copy-start.5
  99.5 1.6 copy-done.5
  101.2 0.0 copy-start.7
  101.2 1.4 copy-done.7
  102.6 0.0 copy-start.9
  102.6 1.3 copy-done.9
  103.9 0.0 all-to-all-done.grad_ref.refs_0_
  103.9 0.0 copy-start.3
  103.9 1.2 copy-done.3
  105.1 3.7 %stage_two.1 = bf16[64,32,128]{2,1,0:T(8,128)(2,1)} custom-call(f32[64,32,128]{2,1,0:T(8,128)} %all-to-all-done.grad_ref.refs_0_, f32[2048,128]{1,0:T(8,128)S(1)} %copy-done.3, f32[9,32,128]{2,1,0:T(8,128)S(1)} %broadcast_in_dim.10.refs_1_.weight_ref.refs_6_), custom_call_target="tpu_custom_call" | custom-call | flops 300000000 | bytes 9000000 | tf_op jit(solution)/shard_map/stage_two/pallas_call | solution.py:376
  108.9 9.1 %all-to-all-start.2 = ((bf16[64,32,128]{2,1,0:T(8,128)(2,1)}), bf16[64,32,128]{2,1,0:T(8,128)(2,1)}, u32[]{:S(2)}, u32[]{:S(2)}) async-start(bf16[64,32,128]{2,1,0:T(8,128)(2,1)} %stage_two.1), calls=%async_computation.2 | async-start | bytes 1048576 | tf_op jit(solution)/shard_map/all_to_all | solution.py:403
  118.0 0.0 copy-start.4
  118.0 1.2 copy-done.4
  119.2 0.0 copy-start.6
  119.2 1.9 copy-done.6
  121.1 0.0 copy-start.8
  121.1 1.6 copy-done.8
  122.7 1.6 copy-done.10
  124.3 0.0 copy-start.13
  124.3 1.0 copy-done.13
  125.3 15.2 %stage_three.1 = bf16[64,136,128]{2,1,0:T(8,128)(2,1)S(1)} custom-call(f32[64,32,128]{2,1,0:T(8,128)} %all-to-all-done.grad_ref.refs_0_, bf16[64,160,128]{2,1,0:T(8,128)(2,1)S(1)} %all-to-all-done.1.refs_0_.refs_1_, f32[3,2048,128]{2,1,0:T(8,128)S(1)} %copy-done.6, f32[2048,256]{1,0:T(8,128)S(1)} %copy-done.8, f32[2048,256]{1,0:T(8,128)S(1)} %copy-done.10, ...), custom_call_target="tpu_custom_call" | custom-call | flops 1400000000 | bytes 42000000 | tf_op jit(solution)/shard_map/stage_three/pallas_call | solution.py:388
  140.5 0.0 copy-start.1
  140.5 1.4 copy-done.1
  141.9 0.0 all-to-all-done.2
  141.9 39.9 %all_to_all.20 = bf16[64,136,128]{2,1,0:T(8,128)(2,1)S(1)} all-to-all(bf16[64,136,128]{2,1,0:T(8,128)(2,1)} %copy-done.1), channel_id=1, replica_groups=mesh['ctx'=64,'tp'=2] {'ctx'}, dimensions={0} | all-to-all | bytes 4456448 | tf_op jit(solution)/shard_map/all_to_all | solution.py:403
  181.8 0.1 slice_bitcast_fusion.1
  181.8 2.4 %pad_maximum_fusion = bf16[64,3,32,128]{3,2,0,1:T(8,128)(2,1)} fusion(bf16[64,1,32,128]{3,2,0,1:T(8,128)(2,1)S(1)} %get-tuple-element.31, bf16[64,1,32,128]{3,2,0,1:T(8,128)(2,1)S(1)} %get-tuple-element.30, bf16[64,1,32,128]{3,2,0,1:T(8,128)(2,1)} %bitcast.7), kind=kLoop, calls=%fused_computation.2 | loop fusion | flops 1572864 | bytes 3145728 | tf_op jit(solution)/shard_map/stack | solution.py:443
  184.2 2.6 %copy.34 = bf16[3,128,2048]{2,1,0:T(8,128)(2,1)} copy(bf16[3,128,2048]{1,2,0:T(8,128)(2,1)} %bitcast.26) | data formatting | bytes 3145728
  186.8 0.1 convert_add_fusion
  187.0 1.3 copy.35
  188.3 0.2 copy.36
  188.6 0.2 copy.33
  188.7 0.8 reshape.46
  (5 shorter events, 0.1 us)
Async XLA Ops:
  0.6 85.3 %copy-start = (f32[3,3,2048]{2,1,0:T(4,128)S(1)}, f32[3,3,2048]{2,1,0:T(4,128)}, u32[]{:S(2)}) copy-start(f32[3,3,2048]{2,1,0:T(4,128)} %param.11) | copy-start | bytes 221188
  6.6 11.0 %copy-start.17 = (bf16[128,2048]{1,0:T(8,128)(2,1)S(1)}, bf16[128,2048]{1,0:T(8,128)(2,1)}, u32[]{:S(2)}) copy-start(bf16[128,2048]{1,0:T(8,128)(2,1)} %param.14) | copy-start | bytes 1572868
  6.6 69.6 %all-to-all-start.1 = ((bf16[64,160,128]{2,1,0:T(8,128)(2,1)}), bf16[64,160,128]{2,1,0:T(8,128)(2,1)S(1)}, u32[]{:S(2)}, u32[]{:S(2)}) async-start(bf16[64,160,128]{2,1,0:T(8,128)(2,1)} %bitcast.25), calls=%async_computation.1 | async-start | bytes 5242880 | tf_op jit(solution)/shard_map/all_to_all | solution.py:403
  17.6 43.3 %collective-permute-start = (bf16[128,2048]{1,0:T(8,128)(2,1)S(1)}, bf16[128,2048]{1,0:T(8,128)(2,1)}, u32[]{:S(2)}, u32[]{:S(2)}) collective-permute-start(bf16[128,2048]{1,0:T(8,128)(2,1)S(1)} %copy-done.17), channel_id=1, source_target_pairs={{0,1},{1,0},{2,3},{3,2},{4,5},{5,4},{6,7},{7,6},{8,9},{9,8},{10,11... | collective-permute-start | bytes 1572872 | tf_op jit(solution)/shard_map/ppermute | solution.py:419
  73.6 12.5 %copy-start.11 = (bf16[768,256]{1,0:T(8,128)(2,1)S(1)}, bf16[768,256]{1,0:T(8,128)(2,1)}, u32[]{:S(2)}) copy-start(bf16[768,256]{1,0:T(8,128)(2,1)} %constant.28.clone.refs_4_.refs_9_) | copy-start | bytes 1179652
  73.6 12.6 %copy-start.14 = (bf16[128,192]{1,0:T(8,128)(2,1)S(1)}, bf16[128,192]{1,0:T(8,128)(2,1)}, u32[]{:S(2)}) copy-start(bf16[128,192]{1,0:T(8,128)(2,1)} %constant.26.clone.refs_2_.refs_7_) | copy-start | bytes 147460
  73.6 12.6 %copy-start.15 = (bf16[128,256]{1,0:T(8,128)(2,1)S(1)}, bf16[128,256]{1,0:T(8,128)(2,1)}, u32[]{:S(2)}) copy-start(bf16[128,256]{1,0:T(8,128)(2,1)} %constant.27.clone.refs_3_.refs_8_) | copy-start | bytes 196612
  73.6 12.6 %copy-start.16 = (f32[2,64,128]{2,1,0:T(8,128)S(1)}, f32[2,64,128]{2,1,0:T(8,128)}, u32[]{:S(2)}) copy-start(f32[2,64,128]{2,1,0:T(8,128)} %constant.30.clone.refs_6_.refs_11_) | copy-start | bytes 196612
  76.2 27.7 %all-to-all-start = ((f32[64,32,128]{2,1,0:T(8,128)}), f32[64,32,128]{2,1,0:T(8,128)}, u32[]{:S(2)}, u32[]{:S(2)}) async-start(f32[64,32,128]{2,1,0:T(8,128)} %bitcast.28), calls=%async_computation | async-start | bytes 2097152 | tf_op jit(solution)/shard_map/all_to_all | solution.py:403
  86.2 1.0 copy-start.12
  98.6 1.0 copy-start.2
  99.5 1.6 copy-start.5
  101.2 1.4 copy-start.7
  102.6 1.3 copy-start.9
  103.9 1.2 copy-start.3
  108.9 33.0 %all-to-all-start.2 = ((bf16[64,32,128]{2,1,0:T(8,128)(2,1)}), bf16[64,32,128]{2,1,0:T(8,128)(2,1)}, u32[]{:S(2)}, u32[]{:S(2)}) async-start(bf16[64,32,128]{2,1,0:T(8,128)(2,1)} %stage_two.1), calls=%async_computation.2 | async-start | bytes 1048576 | tf_op jit(solution)/shard_map/all_to_all | solution.py:403
  118.0 1.2 copy-start.4
  119.2 1.9 copy-start.6
  121.1 1.6 copy-start.8
  122.7 1.6 copy-start.10
  124.3 1.0 copy-start.13
  140.5 1.4 copy-start.1

commit v4 on v3

--- a/solution.py
+++ b/solution.py
@@ -137,14 +137,30 @@
     forward_ref,
     backward_ref,
     twiddle_ref,
+    mixed_out,
+    filt_out,
+    prod_out,
+    conv_out,
+    src,
     mixed_ref,
     filt_ref,
     prod_ref,
     conv_ref,
-    src,
+    sems,
 ):
     blocks, width = in_ref.shape[0], in_ref.shape[2]
     chans = weight_ref.shape[1]
+    copies = [
+        pltpu.make_async_copy(a, b, sems.at[i])
+        for i, (a, b) in enumerate(
+            (
+                (mixed_ref, mixed_out),
+                (filt_ref, filt_out),
+                (prod_ref, prod_out),
+                (conv_ref, conv_out),
+            )
+        )
+    ]
 
     def prepare(step, carry):
         for u in range(UNROLL):
@@ -166,6 +182,7 @@
         return carry
 
     lax.fori_loop(0, blocks // UNROLL, prepare, 0)
+    copies[0].start()
     cos, sin = twiddle_ref[0], twiddle_ref[1]
 
     def convolve(step, carry):
@@ -194,71 +211,72 @@
         return carry
 
     lax.fori_loop(0, chans // GROUP, convolve, 0)
-
-
-def query_kernel(grad_ref, conv_ref, weight_ref, ig_ref):
-    blocks, chans, width = grad_ref.shape
-    weights = [weight_ref[j] for j in range(3)]
-
-    def dm(n1):
-        return grad_ref[n1] * conv_ref[row_of(n1, chans), :]
-
-    def finish(step, cur):
-        for u in range(UNROLL):
-            n1 = step * UNROLL + u
-            follow = dm(jnp.minimum(n1 + 1, blocks - 1))
-            if u == UNROLL - 1:
-                follow = jnp.where(n1 + 1 < blocks, follow, 0.0)
-            ig_ref[n1] = ahead(weights, cur, follow, chans, width).astype(jnp.bfloat16)
-            cur = follow
-        return cur
-
-    lax.fori_loop(0, blocks // UNROLL, finish, dm(0))
+    for copy in copies[1:]:
+        copy.start()
+    for copy in copies:
+        copy.wait()
 
 
 def last_kernel(
     scale,
+    grad_in,
+    streams_in,
+    mixed_in,
+    filt_in,
+    prod_in,
+    conv_in,
+    weight_ref,
+    first_ref,
+    last_ref,
+    forward_ref,
+    backward_ref,
+    twiddle_ref,
+    out_hbm,
     grad_ref,
     in_ref,
     mixed_ref,
     filt_ref,
     prod_ref,
     conv_ref,
-    weight_ref,
-    first_ref,
-    last_ref,
-    forward_ref,
-    backward_ref,
-    twiddle_ref,
-    out_ref,
-    src,
     res,
     sums,
+    out_ref,
+    tail_ref,
+    sems,
+    out_sems,
 ):
-    blocks, chans, width = grad_ref.shape
+    blocks, width = in_ref.shape[0], in_ref.shape[2]
+    chans = weight_ref.shape[1]
     lane = lax.broadcasted_iota(jnp.int32, (chans, width), 1)
-
-    def prepare(step, carry):
-        for u in range(UNROLL):
-            n1 = step * UNROLL + u
-            at = row_of(n1, chans)
-            src[at, :] = grad_ref[n1] * mixed_ref[0, at, :]
-        return carry
-
-    lax.fori_loop(0, blocks // UNROLL, prepare, 0)
+    copies = [
+        pltpu.make_async_copy(a, b, sems.at[i])
+        for i, (a, b) in enumerate(
+            (
+                (grad_in, grad_ref),
+                (mixed_in.at[0], mixed_ref.at[0]),
+                (filt_in, filt_ref),
+                (prod_in, prod_ref),
+                (mixed_in.at[pl.ds(1, 2)], mixed_ref.at[pl.ds(1, 2)]),
+                (conv_in, conv_ref),
+                (streams_in, in_ref),
+            )
+        )
+    ]
+    for copy in copies:
+        copy.start()
+    for copy in copies[:4]:
+        copy.wait()
     cos, sin = twiddle_ref[0], twiddle_ref[1]
 
     def convolve(step, carry):
         base = step * GROUP
         part = GROUP * blocks
-        rows = forward_rows(
-            lambda g: src[pl.ds(base + g, blocks, stride=chans), :],
-            first_ref,
-            cos,
-            sin,
-            blocks,
-            width,
-        )
+
+        def dy(g):
+            at = pl.ds(base + g, blocks, stride=chans)
+            return grad_ref[at, :] * mixed_ref[0, at, :]
+
+        rows = forward_rows(dy, first_ref, cos, sin, blocks, width)
         spec = step_two(jnp.concatenate(rows, axis=0), forward_ref)
         at = row_of(step, part)
         both = [conj_times(r[at, :], spec, width) for r in (filt_ref, prod_ref)]
@@ -274,11 +292,17 @@
         return carry
 
     lax.fori_loop(0, chans // GROUP, convolve, 0)
+    for copy in copies[4:]:
+        copy.wait()
 
     def gradients(n1):
         at = row_of(n1, chans)
         dz = res[0, at, :]
-        return [dz * mixed_ref[2, at, :], dz * mixed_ref[1, at, :]]
+        return [
+            grad_ref[at, :] * conv_ref[at, :],
+            dz * mixed_ref[2, at, :],
+            dz * mixed_ref[1, at, :],
+        ]
 
     sums[...] = jnp.zeros_like(sums)
 
@@ -291,23 +315,26 @@
             follow = gradients(jnp.minimum(n1 + 1, blocks - 1))
             if u == UNROLL - 1:
                 follow = [jnp.where(n1 + 1 < blocks, f, 0.0) for f in follow]
-            for b in (1, 2):
+            for b in range(3):
                 weights = [weight_ref[3 * b + j] for j in range(3)]
-                out = ahead(weights, cur[b - 1], follow[b - 1], chans, width)
-                out_ref[n1, pl.ds((b - 1) * chans, chans), :] = out.astype(jnp.bfloat16)
+                out = ahead(weights, cur[b], follow[b], chans, width)
+                out_ref[n1, pl.ds(b * chans, chans), :] = out.astype(jnp.bfloat16)
             high, low = split(res[1, at, :] * scale)
-            out_ref[n1, pl.ds(2 * chans, chans), :] = high
-            out_ref[n1, pl.ds(3 * chans, chans), :] = low
-            full = [grad_ref[n1] * conv_ref[at, :]] + cur
+            out_ref[n1, pl.ds(3 * chans, chans), :] = high
+            out_ref[n1, pl.ds(4 * chans, chans), :] = low
             for b in range(3):
                 parts = lagged(in_ref, n1, b, chans, width)
                 for j in range(3):
-                    term = full[b] * parts[j]
+                    term = cur[b] * parts[j]
                     old = adds[3 * b + j]
                     adds[3 * b + j] = term if old is None else old + term
             cur = follow
         for t in range(9):
             sums[t] += adds[t]
+        some = pl.ds(step * UNROLL, UNROLL)
+        pltpu.make_async_copy(
+            out_ref.at[some], out_hbm.at[some, pl.ds(0, 5 * chans)], out_sems.at[0]
+        ).start()
         return tuple(cur)
 
     lax.fori_loop(0, blocks // UNROLL, finish, tuple(gradients(0)))
@@ -331,10 +358,18 @@
     packed = jnp.concatenate(packed, axis=0).astype(jnp.bfloat16)
 
     def attach(n1, carry):
-        out_ref[n1, pl.ds(4 * chans, 8), :] = packed
+        tail_ref[n1] = packed
         return carry
 
     lax.fori_loop(0, blocks, attach, 0)
+    tail = pltpu.make_async_copy(
+        tail_ref, out_hbm.at[:, pl.ds(5 * chans, 8)], out_sems.at[1]
+    )
+    tail.start()
+    tail.wait()
+    pltpu.make_async_copy(
+        out_ref, out_hbm.at[:, pl.ds(0, 5 * chans)], out_sems.at[0]
+    ).wait()
 
 
 def f32(*shape):
@@ -351,51 +386,61 @@
 
 def params(mib):
     return pltpu.CompilerParams(vmem_limit_bytes=mib << 20)
+
+
+def hbm():
+    return pl.BlockSpec(memory_space=pltpu.HBM)
+
+
+def vmem():
+    return pl.BlockSpec(memory_space=pltpu.VMEM)
 
 
 def stage_one(streams, weight, consts, scale):
     blocks, width = streams.shape[0], streams.shape[2]
     chans = weight.shape[1]
     rows = blocks * chans
+    shapes = [(3, rows, width), (rows, 2 * width), (rows, 2 * width), (rows, width)]
     return pl.pallas_call(
         lambda *refs: first_kernel(scale, *refs),
         name="stage_one",
-        out_shape=(
-            f32(3, rows, width),
-            f32(rows, 2 * width),
-            f32(rows, 2 * width),
-            f32(rows, width),
-        ),
-        scratch_shapes=[pltpu.VMEM((2, rows, width), jnp.float32)],
+        out_shape=tuple(f32(*shape) for shape in shapes),
+        in_specs=[vmem()] * 7,
+        out_specs=(hbm(),) * 4,
+        scratch_shapes=[pltpu.VMEM((2, rows, width), jnp.float32)]
+        + [pltpu.VMEM(shape, jnp.float32) for shape in shapes]
+        + [pltpu.SemaphoreType.DMA((4,))],
         cost_estimate=estimate(14),
-        compiler_params=params(24),
+        compiler_params=params(60),
     )(streams, weight, *consts)
 
 
-def stage_two(grad, conv, weight):
-    return pl.pallas_call(
-        query_kernel,
-        name="stage_two",
-        out_shape=bf16(*grad.shape),
-        cost_estimate=estimate(3),
-        compiler_params=params(8),
-    )(grad, conv, weight)
-
-
-def stage_three(grad, streams, mixed, filt, prod, conv, weight, consts, scale):
-    blocks, chans, width = grad.shape
+def stage_two(grad, streams, mixed, filt, prod, conv, weight, consts, scale):
+    blocks, width = streams.shape[0], streams.shape[2]
+    chans = weight.shape[1]
     rows = blocks * chans
     return pl.pallas_call(
         lambda *refs: last_kernel(scale, *refs),
-        name="stage_three",
-        out_shape=bf16(blocks, 4 * chans + 8, width),
+        name="stage_two",
+        out_shape=bf16(blocks, 5 * chans + 8, width),
+        in_specs=[hbm()] * 6 + [vmem()] * 6,
+        out_specs=hbm(),
         scratch_shapes=[
+            pltpu.VMEM((rows, width), jnp.float32),
+            pltpu.VMEM(streams.shape, jnp.bfloat16),
+            pltpu.VMEM((3, rows, width), jnp.float32),
+            pltpu.VMEM((rows, 2 * width), jnp.float32),
+            pltpu.VMEM((rows, 2 * width), jnp.float32),
             pltpu.VMEM((rows, width), jnp.float32),
             pltpu.VMEM((2, rows, width), jnp.float32),
             pltpu.VMEM((9, chans, width), jnp.float32),
+            pltpu.VMEM((blocks, 5 * chans, width), jnp.bfloat16),
+            pltpu.VMEM((blocks, 8, width), jnp.bfloat16),
+            pltpu.SemaphoreType.DMA((7,)),
+            pltpu.SemaphoreType.DMA((2,)),
         ],
         cost_estimate=estimate(14),
-        compiler_params=params(32),
+        compiler_params=params(60),
     )(grad, streams, mixed, filt, prod, conv, weight, *consts)
 
 
@@ -414,9 +459,11 @@
     low = (taps - high).astype(jnp.bfloat16)
     streams = jnp.concatenate([inputs, high.astype(jnp.bfloat16)[None], low[None]], axis=0)
     streams = streams.reshape(5, rows, count, chans).transpose(2, 0, 3, 1)
-    streams = regroup(streams.reshape(count, 5 * chans, rows))
-
+    streams = streams.reshape(count, 5 * chans, rows)
     other = lax.ppermute(grad_out, "tp", [(0, 1), (1, 0)])
+    streams, other = lax.optimization_barrier((streams, other))
+    streams = regroup(streams)
+
     first = lax.axis_index("tp") == 0
     whole = jnp.where(
         first,
@@ -426,28 +473,22 @@
     gated = lax.dot_general(
         w_out, whole, (((1,), (1,)), ((), ())), preferred_element_type=jnp.float32
     )
-    gated = regroup(gated.reshape(count, chans, rows))
+    gated = regroup(gated.reshape(count, chans, rows)).reshape(count * chans, rows)
 
     weight = lax.dynamic_slice_in_dim(short_weight, where * chans, chans, axis=2)
     weight = jnp.broadcast_to(weight.reshape(9, chans, 1), (9, chans, rows))
 
     consts = [jnp.asarray(t) for t in tables(count, rows)]
     mixed, filt, prod, conv = stage_one(streams, weight, consts, scale)
-    query = stage_two(gated, conv, weight)
-    query, gated, mixed = lax.optimization_barrier((query, gated, mixed))
-    rest = stage_three(gated, streams, mixed, filt, prod, conv, weight, consts, scale)
-
-    query = regroup(query)
-    query, rest = lax.optimization_barrier((query, rest))
-    rest = regroup(rest)
-    grads = jnp.stack(
-        [query, rest[:, :chans], rest[:, chans : 2 * chans]], axis=1
-    )
+    back = stage_two(gated, streams, mixed, filt, prod, conv, weight, consts, scale)
+
+    back = regroup(back)
+    grads = back[:, : 3 * chans].reshape(count, 3, chans, rows)
     inputs_grad = grads.transpose(1, 3, 0, 2).reshape(3, rows, local)
-    taps_grad = rest[:, 2 * chans : 3 * chans].astype(jnp.float32)
-    taps_grad = taps_grad + rest[:, 3 * chans : 4 * chans].astype(jnp.float32)
+    taps_grad = back[:, 3 * chans : 4 * chans].astype(jnp.float32)
+    taps_grad = taps_grad + back[:, 4 * chans : 5 * chans].astype(jnp.float32)
     taps_grad = taps_grad.transpose(2, 0, 1).reshape(rows, local)
-    sums = rest[:, 4 * chans :].astype(jnp.float32)
+    sums = back[:, 5 * chans :].astype(jnp.float32)
     sums = sums.reshape(count, 8 * rows)[:, : 27 * chans].reshape(count, 3, 9, chans)
     short_grad = jnp.sum(sums, axis=1).transpose(1, 0, 2).reshape(3, 3, local)
     return inputs_grad, taps_grad, short_grad

time: 191 us -> 159 us (0.83)
  waiting for transfers between devices: 40.6 us -> 25.9 us
  local copies, waits for them, and re-layouts: 29.6 us -> 17.4 us
  starting transfers between devices: 32.5 us -> 21.1 us
  Pallas kernels: 30.3 us -> 35.1 us
  blocking collectives: 39.9 us -> 43.6 us
    ppermute x1, waiting for transfers between devices: 40.6 us -> 5.65 us  [shards(): other = lax.ppermute(grad_out, 'tp', [(0, 1), (1, 0)])]
    all_to_all x3 -> x2, waiting for transfers between devices: 0.01 us -> 20.2 us  [regroup(): return lax.all_to_all(x, 'ctx', split_axis=0, concat_axis=0, tiled=True)]
    unnamed x40 -> x12, local copies, waits for them, and re-layouts: 23.6 us -> 9.38 us
    all_to_all x3 -> x2, starting transfers between devices: 29.8 us -> 17.3 us  [regroup(): return lax.all_to_all(x, 'ctx', split_axis=0, concat_axis=0, tiled=True)]
    pallas_call x1, Pallas kernels: 11.4 us -> 15.2 us  [stage_one(): pl.pallas_call(lambda *refs: first_kernel(scale, *refs), name='stage_one'...]
    all_to_all x1, blocking collectives: 39.9 us -> 43.6 us  [regroup(): return lax.all_to_all(x, 'ctx', split_axis=0, concat_axis=0, tiled=True)]
    another operation x1 -> x0, other arithmetic: 2.38 us -> none  [shards(): jnp.stack([query, rest[:, :chans], rest[:, chans:2 * chans]], axis=1)]
    pallas_call x2 -> x1, Pallas kernels: 19 us -> 19.9 us  [stage_two(): pl.pallas_call(lambda *refs: last_kernel(scale, *refs), name='stage_two',...]
  transfers between devices with their start and end apart: 4 -> 3, of which waited for: 1 -> 3; matrix products, arithmetic and copies ran while one was open for 8% -> 14% of each run, Pallas kernels for 14% -> 10%
where the time goes in v4:
time: 159 us; the launch traced here: 158 us
  blocking collectives  43.6 us (27%)
  Pallas kernels  35.1 us (22%)
  waiting for transfers between devices  25.9 us (16%)
  starting transfers between devices  21.1 us (13%)
  local copies, waits for them, and re-layouts  17.4 us (11%)
  matrix products  12.8 us (8%)
  other arithmetic  1.64 us (1%)
    all_to_all x1, blocking collectives, regroup(): return lax.all_to_all(x, 'ctx', split_axis=0, concat_axis=0, tiled=True)  43.6 us
    all_to_all x2, waiting for transfers between devices, regroup(): return lax.all_to_all(x, 'ctx', split_axis=0, concat_axis=0, tiled=True)  20.2 us
    pallas_call x1, Pallas kernels, stage_two(): pl.pallas_call(lambda *refs: last_kernel(scale, *refs), name='stage_two',...  19.9 us
    all_to_all x2, starting transfers between devices, regroup(): return lax.all_to_all(x, 'ctx', split_axis=0, concat_axis=0, tiled=True)  17.3 us
    pallas_call x1, Pallas kernels, stage_one(): pl.pallas_call(lambda *refs: first_kernel(scale, *refs), name='stage_one'...  15.2 us
    dot_general x1, matrix products, shards(): lax.dot_general(w_out, whole, (((1,), (1,)), ((), ())), preferred_element...  12.8 us
    unnamed x12, local copies, waits for them, and re-layouts  9.38 us
    ppermute x1, waiting for transfers between devices, shards(): other = lax.ppermute(grad_out, 'tp', [(0, 1), (1, 0)])  5.65 us
  transfers between devices with their start and end apart: 3, of which 3 were waited for; matrix products, arithmetic and copies ran while one was open for 14% of the time, Pallas kernels for 10%

profile of v4, /device:TPU:1, one launch (start us, length us, event | category | flops | bytes accessed | tf_op | source)
XLA Modules:
  0.0 158.3 jit_solution(18009726870970591891)
XLA Ops:
  0.6 0.0 copy-start
  0.6 3.8 %collective-permute-start = (bf16[128,2048]{1,0:T(8,128)(2,1)}, bf16[128,2048]{1,0:T(8,128)(2,1)S(1)}, u32[]{:S(2)}, u32[]{:S(2)}) collective-permute-start(bf16[128,2048]{1,0:T(8,128)(2,1)} %param.14), channel_id=1, source_target_pairs={{0,1},{1,0},{2,3},{3,2},{4,5},{5,4},{6,7},{7,6},{8,9},{9,8},{10,11... | collective-permute-start | bytes 1572872 | tf_op jit(solution)/shard_map/ppermute | solution.py:463
  4.5 1.5 copy.29
  6.0 1.9 %copy.28 = bf16[3,128,2048]{1,2,0:T(8,128)(2,1)S(1)} copy(bf16[3,128,2048]{2,1,0:T(8,128)(2,1)} %param.10) | data formatting | bytes 3145728 | tf_op args[0]
  7.9 0.2 reduce-precision_convert_fusion
  8.1 0.3 maximum_bitcast_fusion
  8.4 2.0 %copy.31 = bf16[64,5,32,128]{3,2,1,0:T(8,128)(2,1)} copy(bf16[64,5,32,128]{3,2,0,1:T(8,128)(2,1)S(1)} %maximum_bitcast_fusion) | data formatting | bytes 5242880 | tf_op jit(solution)/shard_map/transpose | solution.py:461
  10.4 5.7 %collective-permute-done = bf16[128,2048]{1,0:T(8,128)(2,1)S(1)} collective-permute-done((bf16[128,2048]{1,0:T(8,128)(2,1)}, bf16[128,2048]{1,0:T(8,128)(2,1)S(1)}, u32[]{:S(2)}, u32[]{:S(2)}) %collective-permute-start) | collective-permute-done | bytes 524320 | tf_op jit(solution)/shard_map/ppermute | solution.py:463
  16.1 0.0 copy-start.3
  16.1 0.8 copy-done.3
  16.8 0.0 copy-start.2
  16.8 11.0 %all-to-all-start.1 = ((bf16[64,160,128]{2,1,0:T(8,128)(2,1)}), bf16[64,160,128]{2,1,0:T(8,128)(2,1)S(1)}, u32[]{:S(2)}, u32[]{:S(2)}) async-start(bf16[64,160,128]{2,1,0:T(8,128)(2,1)} %bitcast.22), calls=%async_computation.1 | async-start | bytes 5242880 | tf_op jit(solution)/shard_map/all_to_all | solution.py:448
  27.9 0.0 copy-done.2
  27.9 12.8 %convolution_bitcast_fusion = f32[2048,128]{0,1:T(8,128)} fusion(bf16[2048,4096]{1,0:T(8,128)(2,1)} %param.13, bf16[128,2048]{1,0:T(8,128)(2,1)} %copy-done.3, bf16[128,2048]{1,0:T(8,128)(2,1)S(1)} %copy-done.2, pred[]{:T(512)S(6)} %eq.3), kind=kOutput, calls=%fused_computation.1 | convolution fusion | flops 2152202240 | bytes 18874368 | tf_op jit(solution)/shard_map/dot_general | solution.py:473
  40.7 2.5 %copy.32 = f32[2048,128]{1,0:T(8,128)} copy(f32[2048,128]{0,1:T(8,128)} %convolution_bitcast_fusion) | data formatting | bytes 2097152 | tf_op jit(solution)/shard_map/dot_general | solution.py:473
  43.2 19.1 %all-to-all-done.1.refs_0_.refs_1_ = bf16[64,160,128]{2,1,0:T(8,128)(2,1)S(1)} async-done(((bf16[64,160,128]{2,1,0:T(8,128)(2,1)}), bf16[64,160,128]{2,1,0:T(8,128)(2,1)S(1)}, u32[]{:S(2)}, u32[]{:S(2)}) %all-to-all-start.1) | async-done | bytes 2621472 | tf_op jit(solution)/shard_map/all_to_all | solution.py:448
  62.3 0.0 copy-start.1
  62.3 6.3 %all-to-all-start = ((f32[64,32,128]{2,1,0:T(8,128)}), f32[64,32,128]{2,1,0:T(8,128)}, u32[]{:S(2)}, u32[]{:S(2)}) async-start(f32[64,32,128]{2,1,0:T(8,128)} %bitcast.26), calls=%async_computation | async-start | bytes 2097152 | tf_op jit(solution)/shard_map/all_to_all | solution.py:448
  68.5 0.0 copy-done
  68.6 0.1 constant_dynamic-slice_fusion
  68.6 0.8 broadcast_in_dim.10.refs_1_.refs_6_
  69.4 0.0 copy-done.1
  69.4 15.2 %stage_one.1 = (f32[3,2048,128]{2,1,0:T(8,128)}, f32[2048,256]{1,0:T(8,128)}, f32[2048,256]{1,0:T(8,128)}, f32[2048,128]{1,0:T(8,128)}) custom-call(bf16[64,160,128]{2,1,0:T(8,128)(2,1)} %copy-done.1, f32[9,32,128]{2,1,0:T(8,128)} %broadcast_in_dim.10.refs_1_.refs_6_, bf16[128,192]{1,0:T(8,128)(2,1)} %constant.26.clone.refs_2_.refs_7_, ...), custom_call_target="tpu_custom_call" | custom-call | flops 1400000000 | bytes 42000000 | tf_op jit(solution)/shard_map/stage_one/pallas_call | solution.py:404
  84.6 1.1 all-to-all-done
  85.8 19.9 %stage_two.1 = bf16[64,168,128]{2,1,0:T(8,128)(2,1)} custom-call(f32[2048,128]{1,0:T(8,128)} %bitcast.7.refs_0_, bf16[64,160,128]{2,1,0:T(8,128)(2,1)} %copy-done.1, f32[3,2048,128]{2,1,0:T(8,128)} %get-tuple-element.11.refs_2_, f32[2048,256]{1,0:T(8,128)} %get-tuple-element.12.refs_3_, f32[2048,256]{1,0:T(8,128)} %get-tuple-element.13.refs_4_, ...), custom_call_target="tpu_custom_call" | custom-call | flops 1400000000 | bytes 42000000 | tf_op jit(solution)/shard_map/stage_two/pallas_call | solution.py:422
  105.7 43.6 %all_to_all.15 = bf16[64,168,128]{2,1,0:T(8,128)(2,1)S(1)} all-to-all(bf16[64,168,128]{2,1,0:T(8,128)(2,1)} %stage_two.1), channel_id=1, replica_groups=mesh['ctx'=64,'tp'=2] {'ctx'}, dimensions={0} | all-to-all | bytes 5505024 | tf_op jit(solution)/shard_map/all_to_all | solution.py:448
  149.3 0.2 copy.38
  149.6 0.2 copy.35
  149.7 0.8 reshape.54
  150.5 0.1 slice.21
  150.6 1.4 copy.33
  152.1 2.6 %copy.36 = bf16[3,128,2048]{2,1,0:T(8,128)(2,1)} copy(bf16[3,128,2048]{1,2,0:T(8,128)(2,1)} %bitcast.23) | data formatting | bytes 3145728
  154.6 1.1 convert_add_fusion
  155.8 2.5 %copy.37 = f32[128,2048]{1,0:T(8,128)} copy(f32[128,2048]{0,1:T(8,128)} %bitcast.27) | data formatting | bytes 2097152
  (4 shorter events, 0.1 us)
Async XLA Ops:
  0.6 67.9 %copy-start = (f32[3,3,2048]{2,1,0:T(4,128)S(1)}, f32[3,3,2048]{2,1,0:T(4,128)}, u32[]{:S(2)}) copy-start(f32[3,3,2048]{2,1,0:T(4,128)} %param.11) | copy-start | bytes 221188
  0.6 15.4 %collective-permute-start = (bf16[128,2048]{1,0:T(8,128)(2,1)}, bf16[128,2048]{1,0:T(8,128)(2,1)S(1)}, u32[]{:S(2)}, u32[]{:S(2)}) collective-permute-start(bf16[128,2048]{1,0:T(8,128)(2,1)} %param.14), channel_id=1, source_target_pairs={{0,1},{1,0},{2,3},{3,2},{4,5},{5,4},{6,7},{7,6},{8,9},{9,8},{10,11... | collective-permute-start | bytes 1572872 | tf_op jit(solution)/shard_map/ppermute | solution.py:463
  16.1 0.8 copy-start.3
  16.8 11.0 %copy-start.2 = (bf16[128,2048]{1,0:T(8,128)(2,1)S(1)}, bf16[128,2048]{1,0:T(8,128)(2,1)}, u32[]{:S(2)}) copy-start(bf16[128,2048]{1,0:T(8,128)(2,1)} %param.14) | copy-start | bytes 1572868
  16.8 45.4 %all-to-all-start.1 = ((bf16[64,160,128]{2,1,0:T(8,128)(2,1)}), bf16[64,160,128]{2,1,0:T(8,128)(2,1)S(1)}, u32[]{:S(2)}, u32[]{:S(2)}) async-start(bf16[64,160,128]{2,1,0:T(8,128)(2,1)} %bitcast.22), calls=%async_computation.1 | async-start | bytes 5242880 | tf_op jit(solution)/shard_map/all_to_all | solution.py:448
  62.3 7.2 %copy-start.1 = (bf16[64,160,128]{2,1,0:T(8,128)(2,1)}, bf16[64,160,128]{2,1,0:T(8,128)(2,1)S(1)}, u32[]{:S(2)}) copy-start(bf16[64,160,128]{2,1,0:T(8,128)(2,1)S(1)} %all-to-all-done.1.refs_0_.refs_1_) | copy-start | bytes 7864324
  62.3 23.5 %all-to-all-start = ((f32[64,32,128]{2,1,0:T(8,128)}), f32[64,32,128]{2,1,0:T(8,128)}, u32[]{:S(2)}, u32[]{:S(2)}) async-start(f32[64,32,128]{2,1,0:T(8,128)} %bitcast.26), calls=%async_computation | async-start | bytes 2097152 | tf_op jit(solution)/shard_map/all_to_all | solution.py:448

commit v5 on v4

--- a/solution.py
+++ b/solution.py
@@ -8,8 +8,8 @@
 from jax.experimental.pallas import tpu as pltpu
 from jax.sharding import PartitionSpec as P
 
-GROUP = 4
-UNROLL = 4
+GROUP = 16
+UNROLL = 8
 
 
 def split_np(x):
@@ -39,13 +39,13 @@
     cos, sin = np.cos(angle), np.sin(angle)
     forward = np.block([[cos, -sin], [sin, cos]])
     high, low = split_np(forward)
-    forward3 = np.concatenate([high, high, low], axis=0)
+    forward2 = np.stack([high, low])
     backward = np.block([[cos, sin], [-sin, cos]])
     high, low = split_np(backward)
-    backward3 = np.concatenate([high, high, low], axis=0)
+    backward2 = np.stack([high, low])
     angle = 2.0 * np.pi * np.outer(n1 + 0.5, n2) / length
     twiddle = np.stack([np.cos(angle), np.sin(angle)]).astype(np.float32)
-    return first3, last4, forward3, backward3, twiddle
+    return first3, last4, forward2, backward2, twiddle
 
 
 def split(x):
@@ -75,7 +75,7 @@
 
 def step_two(rows, table_ref):
     high, low = split(rows)
-    return mm(jnp.concatenate([high, low, high], axis=1), table_ref[...])
+    return mm(high, table_ref[0]) + mm(low, table_ref[0]) + mm(high, table_ref[1])
 
 
 def inverse_one(back, put, last_ref, cos, sin, blocks, width):
@@ -128,41 +128,31 @@
     return out
 
 
-def first_kernel(
-    scale,
-    in_ref,
-    weight_ref,
-    first_ref,
-    last_ref,
-    forward_ref,
-    backward_ref,
-    twiddle_ref,
-    mixed_out,
-    filt_out,
-    prod_out,
-    conv_out,
-    src,
-    mixed_ref,
-    filt_ref,
-    prod_ref,
-    conv_ref,
-    sems,
-):
+def load_consts(sources, targets, sems):
+    copies = [pltpu.make_async_copy(a, b, sems.at[i]) for i, (a, b) in enumerate(zip(sources, targets))]
+    for copy in copies:
+        copy.start()
+    return copies
+
+
+def first_kernel(scale, in_hbm, weight_ref, *refs):
+    const_in, (mixed_out, filt_out, prod_out, conv_out) = refs[:5], refs[5:9]
+    in_ref, src, mixed_ref, filt_ref, prod_ref, conv_ref = refs[9:15]
+    consts, const_sems, in_sems, out_sems = refs[15:20], refs[20], refs[21], refs[22]
+    first_ref, last_ref, forward_ref, backward_ref, twiddle_ref = consts
     blocks, width = in_ref.shape[0], in_ref.shape[2]
     chans = weight_ref.shape[1]
-    copies = [
-        pltpu.make_async_copy(a, b, sems.at[i])
-        for i, (a, b) in enumerate(
-            (
-                (mixed_ref, mixed_out),
-                (filt_ref, filt_out),
-                (prod_ref, prod_out),
-                (conv_ref, conv_out),
-            )
-        )
-    ]
+
+    def fetch(step):
+        some = pl.ds(step * UNROLL, UNROLL)
+        return pltpu.make_async_copy(in_hbm.at[some], in_ref.at[some], in_sems.at[step])
+
+    for step in range(blocks // UNROLL):
+        fetch(step).start()
+    const_copies = load_consts(const_in, consts, const_sems)
 
     def prepare(step, carry):
+        fetch(step).wait()
         for u in range(UNROLL):
             n1 = step * UNROLL + u
             at = row_of(n1, chans)
@@ -182,7 +172,10 @@
         return carry
 
     lax.fori_loop(0, blocks // UNROLL, prepare, 0)
-    copies[0].start()
+    mixed_copy = pltpu.make_async_copy(mixed_ref, mixed_out, out_sems.at[0])
+    mixed_copy.start()
+    for copy in const_copies:
+        copy.wait()
     cos, sin = twiddle_ref[0], twiddle_ref[1]
 
     def convolve(step, carry):
@@ -202,6 +195,8 @@
         at = row_of(step, part)
         filt_ref[at, :] = spec[:part]
         prod_ref[at, :] = spec[part:]
+        pltpu.make_async_copy(filt_ref.at[at], filt_out.at[at], out_sems.at[1]).start()
+        pltpu.make_async_copy(prod_ref.at[at], prod_out.at[at], out_sems.at[2]).start()
         back = step_two(times(spec[:part], spec[part:], width), backward_ref)
 
         def put(g, out):
@@ -211,40 +206,20 @@
         return carry
 
     lax.fori_loop(0, chans // GROUP, convolve, 0)
-    for copy in copies[1:]:
-        copy.start()
-    for copy in copies:
-        copy.wait()
-
-
-def last_kernel(
-    scale,
-    grad_in,
-    streams_in,
-    mixed_in,
-    filt_in,
-    prod_in,
-    conv_in,
-    weight_ref,
-    first_ref,
-    last_ref,
-    forward_ref,
-    backward_ref,
-    twiddle_ref,
-    out_hbm,
-    grad_ref,
-    in_ref,
-    mixed_ref,
-    filt_ref,
-    prod_ref,
-    conv_ref,
-    res,
-    sums,
-    out_ref,
-    tail_ref,
-    sems,
-    out_sems,
-):
+    conv_copy = pltpu.make_async_copy(conv_ref, conv_out, out_sems.at[3])
+    conv_copy.start()
+    mixed_copy.wait()
+    pltpu.make_async_copy(filt_ref, filt_out, out_sems.at[1]).wait()
+    pltpu.make_async_copy(prod_ref, prod_out, out_sems.at[2]).wait()
+    conv_copy.wait()
+
+
+def last_kernel(scale, grad_in, streams_in, mixed_in, filt_in, prod_in, conv_in, weight_ref, *refs):
+    const_in, out_hbm = refs[:5], refs[5]
+    grad_ref, in_ref, mixed_ref, filt_ref, prod_ref, conv_ref = refs[6:12]
+    res, sums, out_ref, tail_ref = refs[12:16]
+    consts, const_sems, sems, spec_sems, out_sems = refs[16:21], *refs[21:25]
+    first_ref, last_ref, forward_ref, backward_ref, twiddle_ref = consts
     blocks, width = in_ref.shape[0], in_ref.shape[2]
     chans = weight_ref.shape[1]
     lane = lax.broadcasted_iota(jnp.int32, (chans, width), 1)
@@ -254,19 +229,29 @@
             (
                 (grad_in, grad_ref),
                 (mixed_in.at[0], mixed_ref.at[0]),
-                (filt_in, filt_ref),
-                (prod_in, prod_ref),
                 (mixed_in.at[pl.ds(1, 2)], mixed_ref.at[pl.ds(1, 2)]),
                 (conv_in, conv_ref),
                 (streams_in, in_ref),
             )
         )
     ]
-    for copy in copies:
+
+    def fetch(step):
+        at = row_of(step, GROUP * blocks)
+        return [
+            pltpu.make_async_copy(a.at[at], b.at[at], spec_sems.at[i, step])
+            for i, (a, b) in enumerate(((filt_in, filt_ref), (prod_in, prod_ref)))
+        ]
+
+    for copy in copies[:2]:
         copy.start()
-    for copy in copies[:4]:
+    const_copies = load_consts(const_in, consts, const_sems)
+    for copy in copies[:2] + const_copies:
         copy.wait()
+    for copy in fetch(0):
+        copy.start()
     cos, sin = twiddle_ref[0], twiddle_ref[1]
+    steps = chans // GROUP
 
     def convolve(step, carry):
         base = step * GROUP
@@ -276,9 +261,21 @@
             at = pl.ds(base + g, blocks, stride=chans)
             return grad_ref[at, :] * mixed_ref[0, at, :]
 
+        @pl.when(step + 1 < steps)
+        def _():
+            for copy in fetch(step + 1):
+                copy.start()
+
+        @pl.when(step + 1 == steps)
+        def _():
+            for copy in copies[2:]:
+                copy.start()
+
         rows = forward_rows(dy, first_ref, cos, sin, blocks, width)
         spec = step_two(jnp.concatenate(rows, axis=0), forward_ref)
         at = row_of(step, part)
+        for copy in fetch(step):
+            copy.wait()
         both = [conj_times(r[at, :], spec, width) for r in (filt_ref, prod_ref)]
         back = step_two(jnp.concatenate(both, axis=0), backward_ref)
         for s in range(2):
@@ -291,8 +288,8 @@
             )
         return carry
 
-    lax.fori_loop(0, chans // GROUP, convolve, 0)
-    for copy in copies[4:]:
+    lax.fori_loop(0, steps, convolve, 0)
+    for copy in copies[2:]:
         copy.wait()
 
     def gradients(n1):
@@ -396,20 +393,35 @@
     return pl.BlockSpec(memory_space=pltpu.VMEM)
 
 
+def hbm():
+    return pl.BlockSpec(memory_space=pltpu.HBM)
+
+
+def vmem():
+    return pl.BlockSpec(memory_space=pltpu.VMEM)
+
+
+def room(*arrays):
+    return [pltpu.VMEM(a.shape, a.dtype) for a in arrays]
+
+
 def stage_one(streams, weight, consts, scale):
     blocks, width = streams.shape[0], streams.shape[2]
     chans = weight.shape[1]
     rows = blocks * chans
-    shapes = [(3, rows, width), (rows, 2 * width), (rows, 2 * width), (rows, width)]
+    shapes = [f32(3, rows, width), f32(rows, 2 * width), f32(rows, 2 * width), f32(rows, width)]
     return pl.pallas_call(
         lambda *refs: first_kernel(scale, *refs),
         name="stage_one",
-        out_shape=tuple(f32(*shape) for shape in shapes),
-        in_specs=[vmem()] * 7,
+        out_shape=tuple(shapes),
+        in_specs=[hbm(), vmem()] + [hbm()] * 5,
         out_specs=(hbm(),) * 4,
-        scratch_shapes=[pltpu.VMEM((2, rows, width), jnp.float32)]
-        + [pltpu.VMEM(shape, jnp.float32) for shape in shapes]
-        + [pltpu.SemaphoreType.DMA((4,))],
+        scratch_shapes=room(streams, f32(2, rows, width), *shapes, *consts)
+        + [
+            pltpu.SemaphoreType.DMA((5,)),
+            pltpu.SemaphoreType.DMA((blocks // UNROLL,)),
+            pltpu.SemaphoreType.DMA((4,)),
+        ],
         cost_estimate=estimate(14),
         compiler_params=params(60),
     )(streams, weight, *consts)
@@ -423,25 +435,61 @@
         lambda *refs: last_kernel(scale, *refs),
         name="stage_two",
         out_shape=bf16(blocks, 5 * chans + 8, width),
-        in_specs=[hbm()] * 6 + [vmem()] * 6,
+        in_specs=[hbm()] * 6 + [vmem()] + [hbm()] * 5,
         out_specs=hbm(),
-        scratch_shapes=[
-            pltpu.VMEM((rows, width), jnp.float32),
-            pltpu.VMEM(streams.shape, jnp.bfloat16),
-            pltpu.VMEM((3, rows, width), jnp.float32),
-            pltpu.VMEM((rows, 2 * width), jnp.float32),
-            pltpu.VMEM((rows, 2 * width), jnp.float32),
-            pltpu.VMEM((rows, width), jnp.float32),
-            pltpu.VMEM((2, rows, width), jnp.float32),
-            pltpu.VMEM((9, chans, width), jnp.float32),
-            pltpu.VMEM((blocks, 5 * chans, width), jnp.bfloat16),
-            pltpu.VMEM((blocks, 8, width), jnp.bfloat16),
-            pltpu.SemaphoreType.DMA((7,)),
+        scratch_shapes=room(
+            grad,
+            streams,
+            mixed,
+            filt,
+            prod,
+            conv,
+            f32(2, rows, width),
+            f32(9, chans, width),
+            bf16(blocks, 5 * chans, width),
+            bf16(blocks, 8, width),
+            *consts,
+        )
+        + [
+            pltpu.SemaphoreType.DMA((5,)),
+            pltpu.SemaphoreType.DMA((5,)),
+            pltpu.SemaphoreType.DMA((2, chans // GROUP)),
             pltpu.SemaphoreType.DMA((2,)),
         ],
         cost_estimate=estimate(14),
         compiler_params=params(60),
     )(grad, streams, mixed, filt, prod, conv, weight, *consts)
+
+
+def spread_kernel(back_ref, ig_ref, tg_ref):
+    some, _, width = back_ref.shape
+    chans = width // some
+
+    def part(i):
+        rows = [back_ref[d, pl.ds(i * chans, chans), :].astype(jnp.float32) for d in range(some)]
+        return jnp.concatenate(rows, axis=0)
+
+    for b in range(3):
+        ig_ref[b] = part(b).T.astype(jnp.bfloat16)
+    tg_ref[...] = (part(3) + part(4)).T
+
+
+def spread(back, chans):
+    count, height, width = back.shape
+    some = width // chans
+    return pl.pallas_call(
+        spread_kernel,
+        name="spread",
+        grid=(count // some,),
+        out_shape=(bf16(3, width, count * chans), f32(width, count * chans)),
+        in_specs=[pl.BlockSpec((some, height, width), lambda i: (i, 0, 0))],
+        out_specs=(
+            pl.BlockSpec((3, width, width), lambda i: (0, 0, i)),
+            pl.BlockSpec((width, width), lambda i: (0, i)),
+        ),
+        cost_estimate=estimate(4),
+        compiler_params=params(16),
+    )(back)
 
 
 def regroup(x):
@@ -483,11 +531,7 @@
     back = stage_two(gated, streams, mixed, filt, prod, conv, weight, consts, scale)
 
     back = regroup(back)
-    grads = back[:, : 3 * chans].reshape(count, 3, chans, rows)
-    inputs_grad = grads.transpose(1, 3, 0, 2).reshape(3, rows, local)
-    taps_grad = back[:, 3 * chans : 4 * chans].astype(jnp.float32)
-    taps_grad = taps_grad + back[:, 4 * chans : 5 * chans].astype(jnp.float32)
-    taps_grad = taps_grad.transpose(2, 0, 1).reshape(rows, local)
+    inputs_grad, taps_grad = spread(back, chans)
     sums = back[:, 5 * chans :].astype(jnp.float32)
     sums = sums.reshape(count, 8 * rows)[:, : 27 * chans].reshape(count, 3, 9, chans)
     short_grad = jnp.sum(sums, axis=1).transpose(1, 0, 2).reshape(3, 3, local)

time: 159 us -> 150 us (0.943)
  local copies, waits for them, and re-layouts: 17.4 us -> 10.8 us
  waiting for transfers between devices: 25.9 us -> 29.3 us
  blocking collectives: 43.6 us -> 40.9 us
  Pallas kernels: 35.1 us -> 33.3 us
    pallas_call x0 -> x1, Pallas kernels: none -> 6.26 us  [spread(): pl.pallas_call(spread_kernel, name='spread', grid=(count // some,), out_s...]
    unnamed x12 -> x10, local copies, waits for them, and re-layouts: 9.38 us -> 4.27 us
    pallas_call x1, Pallas kernels: 19.9 us -> 15.2 us  [stage_two(): pl.pallas_call(lambda *refs: last_kernel(scale, *refs), name='stage_two',...]
    pallas_call x1, Pallas kernels: 15.2 us -> 11.8 us  [stage_one(): pl.pallas_call(lambda *refs: first_kernel(scale, *refs), name='stage_one'...]
    all_to_all x2, waiting for transfers between devices: 20.2 us -> 23.6 us  [regroup(): return lax.all_to_all(x, 'ctx', split_axis=0, concat_axis=0, tiled=True)]
    all_to_all x1, blocking collectives: 43.6 us -> 40.9 us  [regroup(): return lax.all_to_all(x, 'ctx', split_axis=0, concat_axis=0, tiled=True)]
  transfers between devices with their start and end apart: 3 -> 3, of which waited for: 3 -> 3; matrix products, arithmetic and copies ran while one was open for 14% -> 15% of each run, Pallas kernels for 10% -> 8%
where the time goes in v5:
time: 150 us; the launch traced here: 149 us
  blocking collectives  40.9 us (27%)
  Pallas kernels  33.3 us (22%)
  waiting for transfers between devices  29.3 us (20%)
  starting transfers between devices  21.1 us (14%)
  matrix products  12.8 us (9%)
  local copies, waits for them, and re-layouts  10.8 us (7%)
    all_to_all x1, blocking collectives, regroup(): return lax.all_to_all(x, 'ctx', split_axis=0, concat_axis=0, tiled=True)  40.9 us
    all_to_all x2, waiting for transfers between devices, regroup(): return lax.all_to_all(x, 'ctx', split_axis=0, concat_axis=0, tiled=True)  23.6 us
    all_to_all x2, starting transfers between devices, regroup(): return lax.all_to_all(x, 'ctx', split_axis=0, concat_axis=0, tiled=True)  17.3 us
    pallas_call x1, Pallas kernels, stage_two(): pl.pallas_call(lambda *refs: last_kernel(scale, *refs), name='stage_two',...  15.2 us
    dot_general x1, matrix products, shards(): lax.dot_general(w_out, whole, (((1,), (1,)), ((), ())), preferred_element...  12.8 us
    pallas_call x1, Pallas kernels, stage_one(): pl.pallas_call(lambda *refs: first_kernel(scale, *refs), name='stage_one'...  11.8 us
    pallas_call x1, Pallas kernels, spread(): pl.pallas_call(spread_kernel, name='spread', grid=(count // some,), out_s...  6.26 us
    ppermute x1, waiting for transfers between devices, shards(): other = lax.ppermute(grad_out, 'tp', [(0, 1), (1, 0)])  5.66 us
  transfers between devices with their start and end apart: 3, of which 3 were waited for; matrix products, arithmetic and copies ran while one was open for 15% of the time, Pallas kernels for 8%

profile of v5, /device:TPU:1, one launch (start us, length us, event | category | flops | bytes accessed | tf_op | source)
XLA Modules:
  0.0 149.4 jit_solution(16952820584781592915)
XLA Ops:
  0.6 0.0 copy-start
  0.6 3.8 %collective-permute-start = (bf16[128,2048]{1,0:T(8,128)(2,1)}, bf16[128,2048]{1,0:T(8,128)(2,1)S(1)}, u32[]{:S(2)}, u32[]{:S(2)}) collective-permute-start(bf16[128,2048]{1,0:T(8,128)(2,1)} %param.14), channel_id=1, source_target_pairs={{0,1},{1,0},{2,3},{3,2},{4,5},{5,4},{6,7},{7,6},{8,9},{9,8},{10,11... | collective-permute-start | bytes 1572872 | tf_op jit(solution)/shard_map/ppermute | solution.py:511
  4.5 1.5 %copy.24 = f32[128,2048]{0,1:T(8,128)S(1)} copy(f32[128,2048]{1,0:T(8,128)} %param.12) | data formatting | bytes 2097152 | tf_op args[2]
  6.0 1.9 %copy.23 = bf16[3,128,2048]{1,2,0:T(8,128)(2,1)S(1)} copy(bf16[3,128,2048]{2,1,0:T(8,128)(2,1)} %param.10) | data formatting | bytes 3145728 | tf_op args[0]
  7.9 0.2 reduce-precision_convert_fusion
  8.1 0.3 maximum_bitcast_fusion
  8.4 2.0 %copy.26 = bf16[64,5,32,128]{3,2,1,0:T(8,128)(2,1)} copy(bf16[64,5,32,128]{3,2,0,1:T(8,128)(2,1)S(1)} %maximum_bitcast_fusion) | data formatting | bytes 5242880 | tf_op jit(solution)/shard_map/transpose | solution.py:509
  10.4 5.7 %collective-permute-done = bf16[128,2048]{1,0:T(8,128)(2,1)S(1)} collective-permute-done((bf16[128,2048]{1,0:T(8,128)(2,1)}, bf16[128,2048]{1,0:T(8,128)(2,1)S(1)}, u32[]{:S(2)}, u32[]{:S(2)}) %collective-permute-start) | collective-permute-done | bytes 524320 | tf_op jit(solution)/shard_map/ppermute | solution.py:511
  16.1 0.0 copy-start.3
  16.1 0.8 copy-done.3
  16.8 0.0 copy-start.2
  16.8 11.0 %all-to-all-start.1 = ((bf16[64,160,128]{2,1,0:T(8,128)(2,1)}), bf16[64,160,128]{2,1,0:T(8,128)(2,1)S(1)}, u32[]{:S(2)}, u32[]{:S(2)}) async-start(bf16[64,160,128]{2,1,0:T(8,128)(2,1)} %bitcast.4), calls=%async_computation.1 | async-start | bytes 5242880 | tf_op jit(solution)/shard_map/all_to_all | solution.py:496
  27.9 0.0 copy-done.2
  27.9 12.8 %convolution_bitcast_fusion = f32[2048,128]{0,1:T(8,128)} fusion(bf16[2048,4096]{1,0:T(8,128)(2,1)} %param.13, bf16[128,2048]{1,0:T(8,128)(2,1)} %copy-done.3, bf16[128,2048]{1,0:T(8,128)(2,1)S(1)} %copy-done.2, pred[]{:T(512)S(6)} %eq.3), kind=kOutput, calls=%fused_computation.1 | convolution fusion | flops 2152202240 | bytes 18874368 | tf_op jit(solution)/shard_map/dot_general | solution.py:521
  40.7 2.5 %copy.27 = f32[2048,128]{1,0:T(8,128)} copy(f32[2048,128]{0,1:T(8,128)} %convolution_bitcast_fusion) | data formatting | bytes 2097152 | tf_op jit(solution)/shard_map/dot_general | solution.py:521
  43.2 19.1 %all-to-all-done.1.refs_0_.refs_1_ = bf16[64,160,128]{2,1,0:T(8,128)(2,1)S(1)} async-done(((bf16[64,160,128]{2,1,0:T(8,128)(2,1)}), bf16[64,160,128]{2,1,0:T(8,128)(2,1)S(1)}, u32[]{:S(2)}, u32[]{:S(2)}) %all-to-all-start.1) | async-done | bytes 2621472 | tf_op jit(solution)/shard_map/all_to_all | solution.py:496
  62.3 0.0 copy-start.1
  62.3 6.3 %all-to-all-start = ((f32[64,32,128]{2,1,0:T(8,128)}), f32[64,32,128]{2,1,0:T(8,128)}, u32[]{:S(2)}, u32[]{:S(2)}) async-start(f32[64,32,128]{2,1,0:T(8,128)} %bitcast.16), calls=%async_computation | async-start | bytes 2097152 | tf_op jit(solution)/shard_map/all_to_all | solution.py:496
  68.6 0.0 copy-done
  68.6 0.1 constant_dynamic-slice_fusion
  68.7 0.8 broadcast_in_dim.10.refs_1_.refs_6_
  69.4 0.0 copy-done.1
  69.4 11.8 %stage_one.1 = (f32[3,2048,128]{2,1,0:T(8,128)}, f32[2048,256]{1,0:T(8,128)}, f32[2048,256]{1,0:T(8,128)}, f32[2048,128]{1,0:T(8,128)}) custom-call(bf16[64,160,128]{2,1,0:T(8,128)(2,1)} %copy-done.1, f32[9,32,128]{2,1,0:T(8,128)} %broadcast_in_dim.10.refs_1_.refs_6_, bf16[128,192]{1,0:T(8,128)(2,1)} %constant.26.clone.refs_2_.refs_7_, ...), custom_call_target="tpu_custom_call" | custom-call | flops 1400000000 | bytes 42000000 | tf_op jit(solution)/shard_map/stage_one/pallas_call | solution.py:413
  81.2 4.5 %all-to-all-done = f32[64,32,128]{2,1,0:T(8,128)} async-done(((f32[64,32,128]{2,1,0:T(8,128)}), f32[64,32,128]{2,1,0:T(8,128)}, u32[]{:S(2)}, u32[]{:S(2)}) %all-to-all-start) | async-done | bytes 1048608 | tf_op jit(solution)/shard_map/all_to_all | solution.py:496
  85.8 15.2 %stage_two.1 = bf16[64,168,128]{2,1,0:T(8,128)(2,1)} custom-call(f32[2048,128]{1,0:T(8,128)} %bitcast.7.refs_0_, bf16[64,160,128]{2,1,0:T(8,128)(2,1)} %copy-done.1, f32[3,2048,128]{2,1,0:T(8,128)} %get-tuple-element.13.refs_2_, f32[2048,256]{1,0:T(8,128)} %get-tuple-element.14.refs_3_, f32[2048,256]{1,0:T(8,128)} %get-tuple-element.15.refs_4_, ...), custom_call_target="tpu_custom_call" | custom-call | flops 1400000000 | bytes 42000000 | tf_op jit(solution)/shard_map/stage_two/pallas_call | solution.py:434
  101.0 40.9 %all_to_all.15.back_ref = bf16[64,168,128]{2,1,0:T(8,128)(2,1)S(1)} all-to-all(bf16[64,168,128]{2,1,0:T(8,128)(2,1)} %stage_two.1), channel_id=1, replica_groups=mesh['ctx'=64,'tp'=2] {'ctx'}, dimensions={0} | all-to-all | bytes 5505024 | tf_op jit(solution)/shard_map/all_to_all | solution.py:496
  141.9 0.2 copy.30
  142.1 0.2 copy.29
  142.3 0.8 reshape.42
  143.1 6.3 %spread.1 = (bf16[3,128,2048]{2,1,0:T(8,128)(2,1)}, f32[128,2048]{1,0:T(8,128)}) custom-call(bf16[64,168,128]{2,1,0:T(8,128)(2,1)S(1)} %all_to_all.15.back_ref), custom_call_target="tpu_custom_call" | custom-call | flops 400000000 | bytes 12000000 | tf_op jit(solution)/shard_map/spread/pallas_call | solution.py:480
  (4 shorter events, 0.1 us)
Async XLA Ops:
  0.6 67.9 %copy-start = (f32[3,3,2048]{2,1,0:T(4,128)S(1)}, f32[3,3,2048]{2,1,0:T(4,128)}, u32[]{:S(2)}) copy-start(f32[3,3,2048]{2,1,0:T(4,128)} %param.11) | copy-start | bytes 221188
  0.6 15.4 %collective-permute-start = (bf16[128,2048]{1,0:T(8,128)(2,1)}, bf16[128,2048]{1,0:T(8,128)(2,1)S(1)}, u32[]{:S(2)}, u32[]{:S(2)}) collective-permute-start(bf16[128,2048]{1,0:T(8,128)(2,1)} %param.14), channel_id=1, source_target_pairs={{0,1},{1,0},{2,3},{3,2},{4,5},{5,4},{6,7},{7,6},{8,9},{9,8},{10,11... | collective-permute-start | bytes 1572872 | tf_op jit(solution)/shard_map/ppermute | solution.py:511
  16.1 0.8 copy-start.3
  16.8 11.0 %copy-start.2 = (bf16[128,2048]{1,0:T(8,128)(2,1)S(1)}, bf16[128,2048]{1,0:T(8,128)(2,1)}, u32[]{:S(2)}) copy-start(bf16[128,2048]{1,0:T(8,128)(2,1)} %param.14) | copy-start | bytes 1572868
  16.8 45.4 %all-to-all-start.1 = ((bf16[64,160,128]{2,1,0:T(8,128)(2,1)}), bf16[64,160,128]{2,1,0:T(8,128)(2,1)S(1)}, u32[]{:S(2)}, u32[]{:S(2)}) async-start(bf16[64,160,128]{2,1,0:T(8,128)(2,1)} %bitcast.4), calls=%async_computation.1 | async-start | bytes 5242880 | tf_op jit(solution)/shard_map/all_to_all | solution.py:496
  62.3 7.2 %copy-start.1 = (bf16[64,160,128]{2,1,0:T(8,128)(2,1)}, bf16[64,160,128]{2,1,0:T(8,128)(2,1)S(1)}, u32[]{:S(2)}) copy-start(bf16[64,160,128]{2,1,0:T(8,128)(2,1)S(1)} %all-to-all-done.1.refs_0_.refs_1_) | copy-start | bytes 7864324
  62.3 23.5 %all-to-all-start = ((f32[64,32,128]{2,1,0:T(8,128)}), f32[64,32,128]{2,1,0:T(8,128)}, u32[]{:S(2)}, u32[]{:S(2)}) async-start(f32[64,32,128]{2,1,0:T(8,128)} %bitcast.16), calls=%async_computation | async-start | bytes 2097152 | tf_op jit(solution)/shard_map/all_to_all | solution.py:496

commit v6 on v5

--- a/solution.py
+++ b/solution.py
@@ -10,6 +10,7 @@
 
 GROUP = 16
 UNROLL = 8
+STEPS = 240
 
 
 def split_np(x):
@@ -54,6 +55,27 @@
     return high, low
 
 
+def limit(peak):
+    return jnp.maximum(lax.reduce_precision(peak * (1.0 + 2.0**-7), 8, 7), 2.0**-100)
+
+
+def encode(x, bound):
+    root = jnp.minimum(jnp.sqrt(jnp.abs(x) * (1.0 / bound)), 1.0)
+    n = jnp.floor(root * (STEPS * 128.0) + 0.5)
+    high = jnp.floor(n * (1.0 / 128.0))
+    code = jnp.exp2(high - STEPS / 2) * (1.0 + (n - 128.0 * high) * (1.0 / 128.0))
+    return jnp.where(x < 0, -code, code).astype(jnp.bfloat16)
+
+
+def decode(code, bound):
+    code = code.astype(jnp.float32)
+    size = jnp.abs(code)
+    high = jnp.floor(jnp.log2(size))
+    root = (high + size * jnp.exp2(-high) + (STEPS / 2 - 1.0)) * (1.0 / STEPS)
+    size = root * root * bound
+    return jnp.where(code < 0, -size, size)
+
+
 def mm(a, b):
     return jnp.dot(a, b, preferred_element_type=jnp.float32)
 
@@ -119,6 +141,20 @@
     ]
 
 
+def mix(weight_ref, b, parts):
+    return (
+        weight_ref[3 * b] * parts[0]
+        + weight_ref[3 * b + 1] * parts[1]
+        + weight_ref[3 * b + 2] * parts[2]
+    )
+
+
+def coded(in_ref, n1, b, chans):
+    bound = in_ref[n1, pl.ds((b + 1) * chans, 8), :].astype(jnp.float32)
+    bound = jnp.concatenate([bound] * (chans // 8), axis=0)
+    return decode(in_ref[n1, pl.ds(b * chans, chans), :], bound)
+
+
 def ahead(weights, cur, follow, chans, width):
     lane = lax.broadcasted_iota(jnp.int32, (chans, width), 1)
     out = weights[0] * cur
@@ -157,18 +193,11 @@
             n1 = step * UNROLL + u
             at = row_of(n1, chans)
             mixed = []
-            for b in range(3):
-                parts = lagged(in_ref, n1, b, chans, width)
-                mixed.append(
-                    weight_ref[3 * b] * parts[0]
-                    + weight_ref[3 * b + 1] * parts[1]
-                    + weight_ref[3 * b + 2] * parts[2]
-                )
+            for b in range(2):
+                mixed.append(mix(weight_ref, b + 1, lagged(in_ref, n1, b, chans, width)))
                 mixed_ref[b, at, :] = mixed[b]
-            taps = in_ref[n1, pl.ds(3 * chans, chans), :].astype(jnp.float32)
-            taps = taps + in_ref[n1, pl.ds(4 * chans, chans), :].astype(jnp.float32)
-            src[0, at, :] = taps * scale
-            src[1, at, :] = mixed[1] * mixed[2]
+            src[0, at, :] = coded(in_ref, n1, 2, chans) * scale
+            src[1, at, :] = mixed[0] * mixed[1]
         return carry
 
     lax.fori_loop(0, blocks // UNROLL, prepare, 0)
@@ -216,9 +245,9 @@
 
 def last_kernel(scale, grad_in, streams_in, mixed_in, filt_in, prod_in, conv_in, weight_ref, *refs):
     const_in, out_hbm = refs[:5], refs[5]
-    grad_ref, in_ref, mixed_ref, filt_ref, prod_ref, conv_ref = refs[6:12]
-    res, sums, out_ref, tail_ref = refs[12:16]
-    consts, const_sems, sems, spec_sems, out_sems = refs[16:21], *refs[21:25]
+    query_ref, in_ref, mixed_ref, filt_ref, prod_ref, conv_ref = refs[6:12]
+    grad_ref, src, res, sums, peak, out_ref, tail_ref = refs[12:19]
+    consts, const_sems, grad_sems, sems, spec_sems, out_sems = refs[19:24], *refs[24:29]
     first_ref, last_ref, forward_ref, backward_ref, twiddle_ref = consts
     blocks, width = in_ref.shape[0], in_ref.shape[2]
     chans = weight_ref.shape[1]
@@ -226,15 +255,13 @@
     copies = [
         pltpu.make_async_copy(a, b, sems.at[i])
         for i, (a, b) in enumerate(
-            (
-                (grad_in, grad_ref),
-                (mixed_in.at[0], mixed_ref.at[0]),
-                (mixed_in.at[pl.ds(1, 2)], mixed_ref.at[pl.ds(1, 2)]),
-                (conv_in, conv_ref),
-                (streams_in, in_ref),
-            )
+            ((mixed_in, mixed_ref), (conv_in, conv_ref), (streams_in, in_ref))
         )
     ]
+
+    def fetch_grad(step):
+        some = pl.ds(step * UNROLL, UNROLL)
+        return pltpu.make_async_copy(grad_in.at[some], query_ref.at[some], grad_sems.at[step])
 
     def fetch(step):
         at = row_of(step, GROUP * blocks)
@@ -243,13 +270,26 @@
             for i, (a, b) in enumerate(((filt_in, filt_ref), (prod_in, prod_ref)))
         ]
 
-    for copy in copies[:2]:
-        copy.start()
+    for step in range(blocks // UNROLL):
+        fetch_grad(step).start()
     const_copies = load_consts(const_in, consts, const_sems)
-    for copy in copies[:2] + const_copies:
-        copy.wait()
     for copy in fetch(0):
         copy.start()
+
+    def prepare(step, carry):
+        fetch_grad(step).wait()
+        for u in range(UNROLL):
+            n1 = step * UNROLL + u
+            at = row_of(n1, chans)
+            grad = coded(query_ref, n1, 1, chans)
+            grad_ref[at, :] = grad
+            src[at, :] = grad * mix(weight_ref, 0, lagged(query_ref, n1, 0, chans, width))
+        return carry
+
+    lax.fori_loop(0, blocks // UNROLL, prepare, 0)
+    peak[...] = jnp.zeros_like(peak)
+    for copy in const_copies:
+        copy.wait()
     cos, sin = twiddle_ref[0], twiddle_ref[1]
     steps = chans // GROUP
 
@@ -258,8 +298,7 @@
         part = GROUP * blocks
 
         def dy(g):
-            at = pl.ds(base + g, blocks, stride=chans)
-            return grad_ref[at, :] * mixed_ref[0, at, :]
+            return src[pl.ds(base + g, blocks, stride=chans), :]
 
         @pl.when(step + 1 < steps)
         def _():
@@ -268,7 +307,7 @@
 
         @pl.when(step + 1 == steps)
         def _():
-            for copy in copies[2:]:
+            for copy in copies:
                 copy.start()
 
         rows = forward_rows(dy, first_ref, cos, sin, blocks, width)
@@ -282,6 +321,8 @@
 
             def put(g, out):
                 res[s, pl.ds(base + g, blocks, stride=chans), :] = out
+                if s == 1:
+                    peak[...] = jnp.maximum(peak[...], jnp.abs(out))
 
             inverse_one(
                 back[s * part : (s + 1) * part], put, last_ref, cos, sin, blocks, width
@@ -289,7 +330,7 @@
         return carry
 
     lax.fori_loop(0, steps, convolve, 0)
-    for copy in copies[2:]:
+    for copy in copies:
         copy.wait()
 
     def gradients(n1):
@@ -297,11 +338,14 @@
         dz = res[0, at, :]
         return [
             grad_ref[at, :] * conv_ref[at, :],
-            dz * mixed_ref[2, at, :],
             dz * mixed_ref[1, at, :],
+            dz * mixed_ref[0, at, :],
         ]
 
     sums[...] = jnp.zeros_like(sums)
+    most = jnp.max(jnp.max(peak[...], axis=0, keepdims=True), axis=1, keepdims=True)
+    most = jnp.maximum(most * scale * (1.0 + 2.0**-7), 2.0**-100)
+    bound = jnp.broadcast_to(most.astype(jnp.bfloat16).astype(jnp.float32), (chans, width))
 
     def finish(step, cur):
         cur = list(cur)
@@ -316,11 +360,10 @@
                 weights = [weight_ref[3 * b + j] for j in range(3)]
                 out = ahead(weights, cur[b], follow[b], chans, width)
                 out_ref[n1, pl.ds(b * chans, chans), :] = out.astype(jnp.bfloat16)
-            high, low = split(res[1, at, :] * scale)
-            out_ref[n1, pl.ds(3 * chans, chans), :] = high
-            out_ref[n1, pl.ds(4 * chans, chans), :] = low
+            out_ref[n1, pl.ds(3 * chans, chans), :] = encode(res[1, at, :] * scale, bound)
             for b in range(3):
-                parts = lagged(in_ref, n1, b, chans, width)
+                ref, place = (in_ref, b - 1) if b else (query_ref, 0)
+                parts = lagged(ref, n1, place, chans, width)
                 for j in range(3):
                     term = cur[b] * parts[j]
                     old = adds[3 * b + j]
@@ -330,7 +373,7 @@
             sums[t] += adds[t]
         some = pl.ds(step * UNROLL, UNROLL)
         pltpu.make_async_copy(
-            out_ref.at[some], out_hbm.at[some, pl.ds(0, 5 * chans)], out_sems.at[0]
+            out_ref.at[some], out_hbm.at[some, pl.ds(0, 4 * chans)], out_sems.at[0]
         ).start()
         return tuple(cur)
 
@@ -346,6 +389,7 @@
     mid = (total - high).astype(jnp.bfloat16).astype(jnp.float32)
     low = total - high - mid
     lines = [p[t : t + 1] for p in (high, mid, low) for t in range(9)]
+    lines += [jnp.where(lane[:1] < chans, bound[:1], 0.0)] * (8 * per - 27)
     packed = []
     for r in range(8):
         row = jnp.zeros((1, width), jnp.float32)
@@ -360,12 +404,12 @@
 
     lax.fori_loop(0, blocks, attach, 0)
     tail = pltpu.make_async_copy(
-        tail_ref, out_hbm.at[:, pl.ds(5 * chans, 8)], out_sems.at[1]
+        tail_ref, out_hbm.at[:, pl.ds(4 * chans, 8)], out_sems.at[1]
     )
     tail.start()
     tail.wait()
     pltpu.make_async_copy(
-        out_ref, out_hbm.at[:, pl.ds(0, 5 * chans)], out_sems.at[0]
+        out_ref, out_hbm.at[:, pl.ds(0, 4 * chans)], out_sems.at[0]
     ).wait()
 
 
@@ -409,7 +453,7 @@
     blocks, width = streams.shape[0], streams.shape[2]
     chans = weight.shape[1]
     rows = blocks * chans
-    shapes = [f32(3, rows, width), f32(rows, 2 * width), f32(rows, 2 * width), f32(rows, width)]
+    shapes = [f32(2, rows, width), f32(rows, 2 * width), f32(rows, 2 * width), f32(rows, width)]
     return pl.pallas_call(
         lambda *refs: first_kernel(scale, *refs),
         name="stage_one",
@@ -434,7 +478,7 @@
     return pl.pallas_call(
         lambda *refs: last_kernel(scale, *refs),
         name="stage_two",
-        out_shape=bf16(blocks, 5 * chans + 8, width),
+        out_shape=bf16(blocks, 4 * chans + 8, width),
         in_specs=[hbm()] * 6 + [vmem()] + [hbm()] * 5,
         out_specs=hbm(),
         scratch_shapes=room(
@@ -444,15 +488,19 @@
             filt,
             prod,
             conv,
+            f32(rows, width),
+            f32(rows, width),
             f32(2, rows, width),
             f32(9, chans, width),
-            bf16(blocks, 5 * chans, width),
+            f32(blocks, width),
+            bf16(blocks, 4 * chans, width),
             bf16(blocks, 8, width),
             *consts,
         )
         + [
             pltpu.SemaphoreType.DMA((5,)),
-            pltpu.SemaphoreType.DMA((5,)),
+            pltpu.SemaphoreType.DMA((blocks // UNROLL,)),
+            pltpu.SemaphoreType.DMA((3,)),
             pltpu.SemaphoreType.DMA((2, chans // GROUP)),
             pltpu.SemaphoreType.DMA((2,)),
         ],
@@ -471,7 +519,12 @@
 
     for b in range(3):
         ig_ref[b] = part(b).T.astype(jnp.bfloat16)
-    tg_ref[...] = (part(3) + part(4)).T
+    rows = []
+    for d in range(some):
+        bound = back_ref[d, pl.ds(4 * chans, 8), :].astype(jnp.float32)[7:8]
+        bound = jnp.broadcast_to(bound, (chans, width))
+        rows.append(decode(back_ref[d, pl.ds(3 * chans, chans), :], bound))
+    tg_ref[...] = jnp.concatenate(rows, axis=0).T
 
 
 def spread(back, chans):
@@ -503,11 +556,16 @@
     chans = local // count
     scale = 1.0 / math.sqrt(count * rows)
 
-    high = lax.reduce_precision(taps, 8, 7)
-    low = (taps - high).astype(jnp.bfloat16)
-    streams = jnp.concatenate([inputs, high.astype(jnp.bfloat16)[None], low[None]], axis=0)
-    streams = streams.reshape(5, rows, count, chans).transpose(2, 0, 3, 1)
-    streams = streams.reshape(count, 5 * chans, rows)
+    def by_owner(x):
+        return x.reshape(-1, rows, count, chans).transpose(2, 0, 3, 1).reshape(count, -1, rows)
+
+    def with_bound(x, bound):
+        bound = jnp.broadcast_to(bound.astype(jnp.bfloat16), (count, 8, rows))
+        return jnp.concatenate([x, bound], axis=1)
+
+    bound = limit(jnp.max(jnp.abs(taps)))
+    streams = jnp.concatenate([inputs[1:], encode(taps, bound)[None]], axis=0)
+    streams = with_bound(by_owner(streams), bound)
     other = lax.ppermute(grad_out, "tp", [(0, 1), (1, 0)])
     streams, other = lax.optimization_barrier((streams, other))
     streams = regroup(streams)
@@ -521,7 +579,9 @@
     gated = lax.dot_general(
         w_out, whole, (((1,), (1,)), ((), ())), preferred_element_type=jnp.float32
     )
-    gated = regroup(gated.reshape(count, chans, rows)).reshape(count * chans, rows)
+    bound = limit(jnp.max(jnp.abs(gated)))
+    gated = encode(gated, bound).reshape(count, chans, rows)
+    gated = regroup(with_bound(jnp.concatenate([by_owner(inputs[:1]), gated], axis=1), bound))
 
     weight = lax.dynamic_slice_in_dim(short_weight, where * chans, chans, axis=2)
     weight = jnp.broadcast_to(weight.reshape(9, chans, 1), (9, chans, rows))
@@ -532,7 +592,7 @@
 
     back = regroup(back)
     inputs_grad, taps_grad = spread(back, chans)
-    sums = back[:, 5 * chans :].astype(jnp.float32)
+    sums = back[:, 4 * chans :].astype(jnp.float32)
     sums = sums.reshape(count, 8 * rows)[:, : 27 * chans].reshape(count, 3, 9, chans)
     short_grad = jnp.sum(sums, axis=1).transpose(1, 0, 2).reshape(3, 3, local)
     return inputs_grad, taps_grad, short_grad

time: 150 us -> 137 us (0.913)
  waiting for transfers between devices: 29.3 us -> 13 us
  other arithmetic: 0.52 us -> 6.05 us
  blocking collectives: 40.9 us -> 36.4 us
  between operations: 0.77 us -> 4.6 us
  local copies, waits for them, and re-layouts: 10.8 us -> 8.37 us
    all_to_all x2, waiting for transfers between devices: 23.6 us -> 8.98 us  [regroup(): return lax.all_to_all(x, 'ctx', split_axis=0, concat_axis=0, tiled=True)]
    all_to_all x1, blocking collectives: 40.9 us -> 36.4 us  [regroup(): return lax.all_to_all(x, 'ctx', split_axis=0, concat_axis=0, tiled=True)]
    convert_element_type x1 -> x2, other arithmetic: 0.17 us -> 3.89 us  [encode(): return jnp.where(x < 0, -code, code).astype(jnp.bfloat16)]
    dot_general x1 -> x0, local copies, waits for them, and re-layouts: 2.53 us -> none  [shards(): lax.dot_general(w_out, whole, (((1,), (1,)), ((), ())), preferred_element...]
    convert_element_type x0 -> x2, local copies, waits for them, and re-layouts: none -> 2.31 us  [encode(): return jnp.where(x < 0, -code, code).astype(jnp.bfloat16)]
    unnamed x10 -> x13, local copies, waits for them, and re-layouts: 4.27 us -> 2.06 us
    transpose x1, local copies, waits for them, and re-layouts: 1.96 us -> 0.27 us  [by_owner(): x.reshape(-1, rows, count, chans).transpose(2, 0, 3, 1)]
    ppermute x1, waiting for transfers between devices: 5.66 us -> 4.03 us  [shards(): other = lax.ppermute(grad_out, 'tp', [(0, 1), (1, 0)])]
  transfers between devices with their start and end apart: 3 -> 3, of which waited for: 3 -> 3; matrix products, arithmetic and copies ran while one was open for 15% -> 18% of each run, Pallas kernels for 8% -> 9%
where the time goes in v6:
time: 137 us; the launch traced here: 136 us
  blocking collectives  36.4 us (27%)
  Pallas kernels  33.9 us (25%)
  starting transfers between devices  20.3 us (15%)
  matrix products  13.3 us (10%)
  waiting for transfers between devices  13 us (9%)
  local copies, waits for them, and re-layouts  8.37 us (6%)
  other arithmetic  6.05 us (4%)
  between operations  4.6 us (3%)
    all_to_all x1, blocking collectives, regroup(): return lax.all_to_all(x, 'ctx', split_axis=0, concat_axis=0, tiled=True)  36.4 us
    all_to_all x2, starting transfers between devices, regroup(): return lax.all_to_all(x, 'ctx', split_axis=0, concat_axis=0, tiled=True)  16.5 us
    pallas_call x1, Pallas kernels, stage_two(): pl.pallas_call(lambda *refs: last_kernel(scale, *refs), name='stage_two',...  15.8 us
    dot_general x1, matrix products, shards(): lax.dot_general(w_out, whole, (((1,), (1,)), ((), ())), preferred_element...  13.3 us
    pallas_call x1, Pallas kernels, stage_one(): pl.pallas_call(lambda *refs: first_kernel(scale, *refs), name='stage_one'...  11.9 us
    all_to_all x2, waiting for transfers between devices, regroup(): return lax.all_to_all(x, 'ctx', split_axis=0, concat_axis=0, tiled=True)  8.98 us
    pallas_call x1, Pallas kernels, spread(): pl.pallas_call(spread_kernel, name='spread', grid=(count // some,), out_s...  6.26 us
    ppermute x1, waiting for transfers between devices, shards(): other = lax.ppermute(grad_out, 'tp', [(0, 1), (1, 0)])  4.03 us
  transfers between devices with their start and end apart: 3, of which 3 were waited for; matrix products, arithmetic and copies ran while one was open for 18% of the time, Pallas kernels for 9%

profile of v6, /device:TPU:1, one launch (start us, length us, event | category | flops | bytes accessed | tf_op | source)
XLA Modules:
  0.0 136.0 jit_solution(15852041709503291099)
XLA Ops:
  0.6 0.0 copy-start
  0.6 0.0 copy-start.3
  0.7 3.8 %collective-permute-start = (bf16[128,2048]{1,0:T(8,128)(2,1)}, bf16[128,2048]{1,0:T(8,128)(2,1)}, u32[]{:S(2)}, u32[]{:S(2)}) collective-permute-start(bf16[128,2048]{1,0:T(8,128)(2,1)} %param.14), channel_id=1, source_target_pairs={{0,1},{1,0},{2,3},{3,2},{4,5},{5,4},{6,7},{7,6},{8,9},{9,8},{10,11... | collective-permute-start | bytes 1572872 | tf_op jit(solution)/shard_map/ppermute | solution.py:569
  4.5 0.0 slice-start
  4.5 0.0 copy-done.3
  4.5 0.7 abs_reduce_fusion.1
  5.2 0.0 slice-start.1
  7.1 0.9 fusion
  8.0 1.0 copy.25
  9.0 0.0 slice-done
  9.0 0.3 copy.23
  9.3 0.0 slice-done.1
  9.3 0.0 copy-start.4
  9.3 0.7 copy.31
  10.0 0.4 copy-done.4
  10.4 0.1 maximum_bitcast_fusion
  10.5 0.3 copy.26
  10.8 1.3 concatenate.23
  12.1 0.0 copy-start.5
  12.1 4.0 %collective-permute-done = bf16[128,2048]{1,0:T(8,128)(2,1)} collective-permute-done((bf16[128,2048]{1,0:T(8,128)(2,1)}, bf16[128,2048]{1,0:T(8,128)(2,1)}, u32[]{:S(2)}, u32[]{:S(2)}) %collective-permute-start) | collective-permute-done | bytes 524320 | tf_op jit(solution)/shard_map/ppermute | solution.py:569
  16.2 10.9 %all-to-all-start.1 = ((bf16[64,104,128]{2,1,0:T(8,128)(2,1)}), bf16[64,104,128]{2,1,0:T(8,128)(2,1)S(1)}, u32[]{:S(2)}, u32[]{:S(2)}) async-start(bf16[64,104,128]{2,1,0:T(8,128)(2,1)} %concatenate.23), calls=%async_computation.1 | async-start | bytes 3407872 | tf_op jit(solution)/shard_map/all_to_all | solution.py:549
  27.1 0.0 copy-done.5
  27.1 13.3 %abs_reduce_fusion = (f32[]{:T(128)}, f32[128,2048]{1,0:T(8,128)}) fusion(bf16[2048,4096]{1,0:T(8,128)(2,1)} %param.13, bf16[128,2048]{1,0:T(8,128)(2,1)} %collective-permute-done, bf16[128,2048]{1,0:T(8,128)(2,1)S(1)} %copy-done.5, pred[]{:T(512)S(6)} %eq.3), kind=kOutput, calls=%fused_computation.21 | convolution fusion | flops 2152726528 | bytes 18874372 | tf_op jit(solution)/shard_map/dot_general | solution.py:579
  42.3 3.0 %fusion.1 = bf16[2048,128]{0,1:T(8,128)(2,1)} fusion(f32[128,2048]{1,0:T(8,128)} %get-tuple-element.20, f32[]{:T(128)S(6)} %div.7), kind=kLoop, calls=%fused_computation.5 | loop fusion | flops 4980736 | bytes 1572868 | tf_op jit(solution)/shard_map/convert_element_type | solution.py:67
  45.2 1.3 copy.27
  46.6 0.1 pad.3.clone
  46.6 1.3 maximum_maximum_fusion
  47.9 3.3 %all-to-all-done.1.refs_0_.refs_1_ = bf16[64,104,128]{2,1,0:T(8,128)(2,1)S(1)} async-done(((bf16[64,104,128]{2,1,0:T(8,128)(2,1)}), bf16[64,104,128]{2,1,0:T(8,128)(2,1)S(1)}, u32[]{:S(2)}, u32[]{:S(2)}) %all-to-all-start.1) | async-done | bytes 1703968 | tf_op jit(solution)/shard_map/all_to_all | solution.py:549
  51.3 0.0 copy-start.1
  51.3 5.6 %all-to-all-start = ((bf16[64,72,128]{2,1,0:T(8,128)(2,1)}), bf16[64,72,128]{2,1,0:T(8,128)(2,1)S(1)}, u32[]{:S(2)}, u32[]{:S(2)}) async-start(bf16[64,72,128]{2,1,0:T(8,128)(2,1)} %maximum_maximum_fusion), calls=%async_computation | async-start | bytes 2359296 | tf_op jit(solution)/shard_map/all_to_all | solution.py:549
  56.9 0.0 copy-done
  56.9 0.1 constant_dynamic-slice_fusion
  57.0 0.8 broadcast_in_dim.14.refs_1_.refs_6_
  57.7 0.0 copy-done.1
  57.7 11.9 %stage_one.1 = (f32[2,2048,128]{2,1,0:T(8,128)}, f32[2048,256]{1,0:T(8,128)}, f32[2048,256]{1,0:T(8,128)}, f32[2048,128]{1,0:T(8,128)}) custom-call(bf16[64,104,128]{2,1,0:T(8,128)(2,1)} %copy-done.1, f32[9,32,128]{2,1,0:T(8,128)} %broadcast_in_dim.14.refs_1_.refs_6_, bf16[128,192]{1,0:T(8,128)(2,1)} %constant.15.clone.refs_2_.refs_7_, ...), custom_call_target="tpu_custom_call" | custom-call | flops 1400000000 | bytes 42000000 | tf_op jit(solution)/shard_map/stage_one/pallas_call | solution.py:457
  69.6 5.7 %all-to-all-done.refs_0_ = bf16[64,72,128]{2,1,0:T(8,128)(2,1)S(1)} async-done(((bf16[64,72,128]{2,1,0:T(8,128)(2,1)}), bf16[64,72,128]{2,1,0:T(8,128)(2,1)S(1)}, u32[]{:S(2)}, u32[]{:S(2)}) %all-to-all-start) | async-done | bytes 1179680 | tf_op jit(solution)/shard_map/all_to_all | solution.py:549
  75.3 0.0 copy-start.2
  75.3 1.0 copy-done.2
  76.3 15.8 %stage_two.1 = bf16[64,136,128]{2,1,0:T(8,128)(2,1)} custom-call(bf16[64,72,128]{2,1,0:T(8,128)(2,1)} %copy-done.2, bf16[64,104,128]{2,1,0:T(8,128)(2,1)} %copy-done.1, f32[2,2048,128]{2,1,0:T(8,128)} %get-tuple-element.13.refs_2_, f32[2048,256]{1,0:T(8,128)} %get-tuple-element.14.refs_3_, f32[2048,256]{1,0:T(8,128)} %get-tuple-element.15.refs_4_, ...), custom_call_target="tpu_custom_call" | custom-call | flops 1400000000 | bytes 42000000 | tf_op jit(solution)/shard_map/stage_two/pallas_call | solution.py:478
  92.1 36.4 %all_to_all.15.back_ref = bf16[64,136,128]{2,1,0:T(8,128)(2,1)S(1)} all-to-all(bf16[64,136,128]{2,1,0:T(8,128)(2,1)} %stage_two.1), channel_id=1, replica_groups=mesh['ctx'=64,'tp'=2] {'ctx'}, dimensions={0} | all-to-all | bytes 4456448 | tf_op jit(solution)/shard_map/all_to_all | solution.py:549
  128.4 0.2 copy.30
  128.7 0.2 copy.29
  128.9 0.8 reshape.44
  129.7 6.3 %spread.1 = (bf16[3,128,2048]{2,1,0:T(8,128)(2,1)}, f32[128,2048]{1,0:T(8,128)}) custom-call(bf16[64,136,128]{2,1,0:T(8,128)(2,1)S(1)} %all_to_all.15.back_ref), custom_call_target="tpu_custom_call" | custom-call | flops 400000000 | bytes 12000000 | tf_op jit(solution)/shard_map/spread/pallas_call | solution.py:533
  (5 shorter events, 0.1 us)
Async XLA Ops:
  0.6 56.2 %copy-start = (f32[3,3,2048]{2,1,0:T(4,128)S(1)}, f32[3,3,2048]{2,1,0:T(4,128)}, u32[]{:S(2)}) copy-start(f32[3,3,2048]{2,1,0:T(4,128)} %param.11) | copy-start | bytes 221188
  0.6 3.8 %copy-start.3 = (f32[128,2048]{1,0:T(8,128)S(1)}, f32[128,2048]{1,0:T(8,128)}, u32[]{:S(2)}) copy-start(f32[128,2048]{1,0:T(8,128)} %param.12) | copy-start | bytes 3145732
  0.7 15.5 %collective-permute-start = (bf16[128,2048]{1,0:T(8,128)(2,1)}, bf16[128,2048]{1,0:T(8,128)(2,1)}, u32[]{:S(2)}, u32[]{:S(2)}) collective-permute-start(bf16[128,2048]{1,0:T(8,128)(2,1)} %param.14), channel_id=1, source_target_pairs={{0,1},{1,0},{2,3},{3,2},{4,5},{5,4},{6,7},{7,6},{8,9},{9,8},{10,11... | collective-permute-start | bytes 1572872 | tf_op jit(solution)/shard_map/ppermute | solution.py:569
  4.5 4.6 %slice-start = ((bf16[3,128,2048]{2,1,0:T(8,128)(2,1)}), bf16[1,128,2048]{2,1,0:T(8,128)(2,1)S(1)}, s32[]{:S(2)}) async-start(bf16[3,128,2048]{2,1,0:T(8,128)(2,1)} %param.10), calls=%async_computation.3 | async-start | bytes 1048576 | tf_op jit(solution)/shard_map/slice | solution.py:584
  5.2 4.2 %slice-start.1 = ((bf16[3,128,2048]{2,1,0:T(8,128)(2,1)}), bf16[2,128,2048]{2,1,0:T(8,128)(2,1)S(1)}, s32[]{:S(2)}) async-start(bf16[3,128,2048]{2,1,0:T(8,128)(2,1)} %param.10), calls=%async_computation.4 | async-start | bytes 2097152 | tf_op jit(solution)/shard_map/slice | solution.py:567
  9.3 1.0 copy-start.4
  12.1 14.9 %copy-start.5 = (bf16[128,2048]{1,0:T(8,128)(2,1)S(1)}, bf16[128,2048]{1,0:T(8,128)(2,1)}, u32[]{:S(2)}) copy-start(bf16[128,2048]{1,0:T(8,128)(2,1)} %param.14) | copy-start | bytes 1572868
  16.2 35.1 %all-to-all-start.1 = ((bf16[64,104,128]{2,1,0:T(8,128)(2,1)}), bf16[64,104,128]{2,1,0:T(8,128)(2,1)S(1)}, u32[]{:S(2)}, u32[]{:S(2)}) async-start(bf16[64,104,128]{2,1,0:T(8,128)(2,1)} %concatenate.23), calls=%async_computation.1 | async-start | bytes 3407872 | tf_op jit(solution)/shard_map/all_to_all | solution.py:549
  51.3 6.5 %copy-start.1 = (bf16[64,104,128]{2,1,0:T(8,128)(2,1)}, bf16[64,104,128]{2,1,0:T(8,128)(2,1)S(1)}, u32[]{:S(2)}) copy-start(bf16[64,104,128]{2,1,0:T(8,128)(2,1)S(1)} %all-to-all-done.1.refs_0_.refs_1_) | copy-start | bytes 5111812
  51.3 24.0 %all-to-all-start = ((bf16[64,72,128]{2,1,0:T(8,128)(2,1)}), bf16[64,72,128]{2,1,0:T(8,128)(2,1)S(1)}, u32[]{:S(2)}, u32[]{:S(2)}) async-start(bf16[64,72,128]{2,1,0:T(8,128)(2,1)} %maximum_maximum_fusion), calls=%async_computation | async-start | bytes 2359296 | tf_op jit(solution)/shard_map/all_to_all | solution.py:549
  75.3 1.0 copy-start.2

commit v7 on v6

--- a/solution.py
+++ b/solution.py
@@ -11,6 +11,8 @@
 GROUP = 16
 UNROLL = 8
 STEPS = 240
+CHUNKS = 4
+PROJECT_US = 200
 
 
 def split_np(x):
@@ -53,10 +55,6 @@
     high = x.astype(jnp.bfloat16)
     low = (x - high.astype(jnp.float32)).astype(jnp.bfloat16)
     return high, low
-
-
-def limit(peak):
-    return jnp.maximum(lax.reduce_precision(peak * (1.0 + 2.0**-7), 8, 7), 2.0**-100)
 
 
 def encode(x, bound):
@@ -505,44 +503,192 @@
             pltpu.SemaphoreType.DMA((2,)),
         ],
         cost_estimate=estimate(14),
-        compiler_params=params(60),
+        compiler_params=params(61),
     )(grad, streams, mixed, filt, prod, conv, weight, *consts)
 
 
-def spread_kernel(back_ref, ig_ref, tg_ref):
-    some, _, width = back_ref.shape
-    chans = width // some
-
-    def part(i):
-        rows = [back_ref[d, pl.ds(i * chans, chans), :].astype(jnp.float32) for d in range(some)]
-        return jnp.concatenate(rows, axis=0)
-
-    for b in range(3):
-        ig_ref[b] = part(b).T.astype(jnp.bfloat16)
-    rows = []
-    for d in range(some):
-        bound = back_ref[d, pl.ds(4 * chans, 8), :].astype(jnp.float32)[7:8]
-        bound = jnp.broadcast_to(bound, (chans, width))
-        rows.append(decode(back_ref[d, pl.ds(3 * chans, chans), :], bound))
-    tg_ref[...] = jnp.concatenate(rows, axis=0).T
+def spread_kernel(back_ref, ig_hbm, tg_hbm, ig_ref, tg_ref, sems):
+    count, _, width = back_ref.shape
+    total = tg_ref.shape[1]
+    chans = total // count
+    some = width // chans
+    wide = total // CHUNKS
+
+    def copies(part):
+        cols = pl.ds(part * wide, wide)
+        return [
+            pltpu.make_async_copy(a.at[..., cols], b.at[..., cols], sems.at[i, part])
+            for i, (a, b) in enumerate(((ig_ref, ig_hbm), (tg_ref, tg_hbm)))
+        ]
+
+    for part in range(CHUNKS):
+        for m in range(part * wide // width, (part + 1) * wide // width):
+            cols = pl.ds(m * width, width)
+            owners = range(m * some, (m + 1) * some)
+            for b in range(3):
+                rows = [back_ref[d, pl.ds(b * chans, chans), :] for d in owners]
+                rows = jnp.concatenate(rows, axis=0).astype(jnp.float32)
+                ig_ref[b, :, cols] = rows.T.astype(jnp.bfloat16)
+            rows = []
+            for d in owners:
+                bound = back_ref[d, pl.ds(4 * chans, 8), :].astype(jnp.float32)[7:8]
+                bound = jnp.broadcast_to(bound, (chans, width))
+                rows.append(decode(back_ref[d, pl.ds(3 * chans, chans), :], bound))
+            tg_ref[:, cols] = jnp.concatenate(rows, axis=0).T
+        for copy in copies(part):
+            copy.start()
+    for part in range(CHUNKS):
+        for copy in copies(part):
+            copy.wait()
 
 
 def spread(back, chans):
-    count, height, width = back.shape
-    some = width // chans
+    count, _, width = back.shape
+    outs = (bf16(3, width, count * chans), f32(width, count * chans))
     return pl.pallas_call(
         spread_kernel,
         name="spread",
-        grid=(count // some,),
-        out_shape=(bf16(3, width, count * chans), f32(width, count * chans)),
-        in_specs=[pl.BlockSpec((some, height, width), lambda i: (i, 0, 0))],
-        out_specs=(
-            pl.BlockSpec((3, width, width), lambda i: (0, 0, i)),
-            pl.BlockSpec((width, width), lambda i: (0, i)),
+        out_shape=outs,
+        in_specs=[vmem()],
+        out_specs=(hbm(), hbm()),
+        scratch_shapes=room(*outs) + [pltpu.SemaphoreType.DMA((2, CHUNKS))],
+        cost_estimate=estimate(4),
+        compiler_params=params(24),
+    )(back)
+
+
+def collect_kernel(in_hbm, taps_hbm, out_hbm, query_hbm, in_ref, taps_ref, out_ref, query_ref, sems):
+    total = taps_ref.shape[1]
+    count, chans, width = query_ref.shape
+    some = width // chans
+    wide = total // CHUNKS
+    owners = count // CHUNKS
+    taps_copy = pltpu.make_async_copy(taps_hbm, taps_ref, sems.at[3, 0])
+    taps_copy.start()
+
+    def fetch(part):
+        cols = pl.ds(part * wide, wide)
+        return pltpu.make_async_copy(in_hbm.at[..., cols], in_ref.at[..., cols], sems.at[0, part])
+
+    def puts(part):
+        these = pl.ds(part * owners, owners)
+        return [
+            pltpu.make_async_copy(a.at[these], b.at[these], sems.at[1 + i, part])
+            for i, (a, b) in enumerate(((out_ref, out_hbm), (query_ref, query_hbm)))
+        ]
+
+    for part in range(CHUNKS):
+        fetch(part).start()
+    taps_copy.wait()
+    most = jnp.max(jnp.abs(taps_ref[...]), axis=0, keepdims=True)
+    most = jnp.max(most, axis=1, keepdims=True)
+    most = jnp.maximum(most * (1.0 + 2.0**-7), 2.0**-100).astype(jnp.bfloat16)
+    mark = jnp.broadcast_to(most, (8, width))
+    bound = jnp.broadcast_to(most.astype(jnp.float32), (width, width))
+    for part in range(CHUNKS):
+        fetch(part).wait()
+        for m in range(part * wide // width, (part + 1) * wide // width):
+            cols = pl.ds(m * width, width)
+            blocks = [in_ref[b, :, cols].astype(jnp.float32).T.astype(jnp.bfloat16) for b in range(3)]
+            blocks.append(encode(taps_ref[:, cols].T, bound))
+            for h in range(some):
+                d = m * some + h
+                at = slice(h * chans, (h + 1) * chans)
+                query_ref[d] = blocks[0][at]
+                for b in range(3):
+                    out_ref[d, pl.ds(b * chans, chans), :] = blocks[b + 1][at]
+                out_ref[d, pl.ds(3 * chans, 8), :] = mark
+        for copy in puts(part):
+            copy.start()
+    for part in range(CHUNKS):
+        for copy in puts(part):
+            copy.wait()
+
+
+def collect(inputs, taps, count):
+    rows, total = taps.shape
+    chans = total // count
+    outs = (bf16(count, 3 * chans + 8, rows), bf16(count, chans, rows))
+    return pl.pallas_call(
+        collect_kernel,
+        name="collect",
+        out_shape=outs,
+        in_specs=[hbm(), hbm()],
+        out_specs=(hbm(), hbm()),
+        scratch_shapes=room(inputs, taps, *outs) + [pltpu.SemaphoreType.DMA((4, CHUNKS))],
+        cost_estimate=estimate(5),
+        compiler_params=params(60),
+    )(inputs, taps)
+
+
+def project_kernel(which_ref, own_w, other_w, own_ref, other_ref, query_ref, out_ref, grad, peak):
+    step = pl.program_id(0)
+    rows, width = own_w.shape[0], own_ref.shape[0]
+    count, chans, _ = query_ref.shape
+
+    def part(a, b):
+        return lax.dot_general(
+            a[...], b[...], (((1,), (1,)), ((), ())), preferred_element_type=jnp.float32
+        )
+
+    block = part(own_w, own_ref) + part(other_w, other_ref)
+    grad[pl.ds(pl.multiple_of(step * rows, rows), rows), :] = block
+    most = jnp.max(jnp.abs(block), axis=0, keepdims=True)
+
+    @pl.when(step == 0)
+    def _():
+        peak[...] = jnp.broadcast_to(most, peak.shape)
+
+    @pl.when(step > 0)
+    def _():
+        peak[...] = jnp.maximum(peak[...], most)
+
+    @pl.when(step == pl.num_programs(0) - 1)
+    def _():
+        most = jnp.max(peak[...], axis=1, keepdims=True)
+        most = jnp.maximum(most * (1.0 + 2.0**-7), 2.0**-100).astype(jnp.bfloat16)
+        mark = jnp.broadcast_to(most, (8, width))
+        bound = jnp.broadcast_to(most[:1].astype(jnp.float32), (chans, width))
+
+        def fill(i, carry):
+            for u in range(UNROLL):
+                d = i * UNROLL + u
+                out_ref[d, pl.ds(0, chans), :] = query_ref[d]
+                out_ref[d, pl.ds(chans, chans), :] = encode(grad[row_of(d, chans), :], bound)
+                out_ref[d, pl.ds(2 * chans, 8), :] = mark
+            return carry
+
+        lax.fori_loop(0, count // UNROLL, fill, 0)
+
+
+def project(which, w_out, own, other, query):
+    count, chans, rows = query.shape
+    depth = own.shape[1]
+    tile = 256
+    whole = lambda shape: pl.BlockSpec(shape, lambda i, which: (0,) * len(shape))
+    return pl.pallas_call(
+        project_kernel,
+        name="project",
+        grid_spec=pltpu.PrefetchScalarGridSpec(
+            num_scalar_prefetch=1,
+            grid=(w_out.shape[0] // tile,),
+            in_specs=[
+                pl.BlockSpec((tile, depth), lambda i, which: (i, which[0])),
+                pl.BlockSpec((tile, depth), lambda i, which: (i, 1 - which[0])),
+                whole(own.shape),
+                whole(other.shape),
+                whole(query.shape),
+            ],
+            out_specs=whole((count, 2 * chans + 8, rows)),
+            scratch_shapes=[
+                pltpu.VMEM((count * chans, rows), jnp.float32),
+                pltpu.VMEM((8, rows), jnp.float32),
+            ],
         ),
-        cost_estimate=estimate(4),
-        compiler_params=params(16),
-    )(back)
+        out_shape=bf16(count, 2 * chans + 8, rows),
+        cost_estimate=estimate(PROJECT_US),
+        compiler_params=params(40),
+    )(which, w_out, w_out, own, other, query)
 
 
 def regroup(x):
@@ -556,32 +702,11 @@
     chans = local // count
     scale = 1.0 / math.sqrt(count * rows)
 
-    def by_owner(x):
-        return x.reshape(-1, rows, count, chans).transpose(2, 0, 3, 1).reshape(count, -1, rows)
-
-    def with_bound(x, bound):
-        bound = jnp.broadcast_to(bound.astype(jnp.bfloat16), (count, 8, rows))
-        return jnp.concatenate([x, bound], axis=1)
-
-    bound = limit(jnp.max(jnp.abs(taps)))
-    streams = jnp.concatenate([inputs[1:], encode(taps, bound)[None]], axis=0)
-    streams = with_bound(by_owner(streams), bound)
+    streams, query = collect(inputs, taps, count)
     other = lax.ppermute(grad_out, "tp", [(0, 1), (1, 0)])
-    streams, other = lax.optimization_barrier((streams, other))
     streams = regroup(streams)
-
-    first = lax.axis_index("tp") == 0
-    whole = jnp.where(
-        first,
-        jnp.concatenate([grad_out, other], axis=1),
-        jnp.concatenate([other, grad_out], axis=1),
-    )
-    gated = lax.dot_general(
-        w_out, whole, (((1,), (1,)), ((), ())), preferred_element_type=jnp.float32
-    )
-    bound = limit(jnp.max(jnp.abs(gated)))
-    gated = encode(gated, bound).reshape(count, chans, rows)
-    gated = regroup(with_bound(jnp.concatenate([by_owner(inputs[:1]), gated], axis=1), bound))
+    which = lax.axis_index("tp").astype(jnp.int32).reshape(1)
+    gated = regroup(project(which, w_out, grad_out, other, query))
 
     weight = lax.dynamic_slice_in_dim(short_weight, where * chans, chans, axis=2)
     weight = jnp.broadcast_to(weight.reshape(9, chans, 1), (9, chans, rows))

time: 137 us -> 122 us (0.89)
  matrix products: 13.3 us -> 0 us
  Pallas kernels: 33.9 us -> 45.7 us
  local copies, waits for them, and re-layouts: 8.37 us -> 2.07 us
  other arithmetic: 6.05 us -> 0.04 us
  waiting for transfers between devices: 13 us -> 17.5 us
  between operations: 4.6 us -> 0.93 us
    dot_general x1 -> x0, matrix products: 13.3 us -> none  [shards(): lax.dot_general(w_out, whole, (((1,), (1,)), ((), ())), preferred_element...]
    pallas_call x1 -> x3, Pallas kernels: 6.26 us -> 18.1 us  [the longest x1 12.4 us: project(): pl.pallas_call(project_kernel, name='project', grid_spec=pltpu.PrefetchSc...]
    all_to_all x2, waiting for transfers between devices: 8.98 us -> 17.5 us  [regroup(): return lax.all_to_all(x, 'ctx', split_axis=0, concat_axis=0, tiled=True)]
    ppermute x1, waiting for transfers between devices: 4.03 us -> 0.01 us  [shards(): other = lax.ppermute(grad_out, 'tp', [(0, 1), (1, 0)])]
    convert_element_type x2 -> x0, other arithmetic: 3.89 us -> none  [encode(): return jnp.where(x < 0, -code, code).astype(jnp.bfloat16)]
    convert_element_type x2 -> x0, local copies, waits for them, and re-layouts: 2.31 us -> none  [encode(): return jnp.where(x < 0, -code, code).astype(jnp.bfloat16)]
    unnamed x13 -> x8, local copies, waits for them, and re-layouts: 2.06 us -> 0.03 us
    concatenate x2 -> x0, local copies, waits for them, and re-layouts: 1.41 us -> none  [with_bound(): return jnp.concatenate([x, bound], axis=1)]
  transfers between devices with their start and end apart: 3 -> 3, of which waited for: 3 -> 2; matrix products, arithmetic and copies ran while one was open for 18% -> 1% of each run, Pallas kernels for 9% -> 23%
where the time goes in v7:
time: 122 us
  Pallas kernels  45.7 us (37%)
  blocking collectives  36.6 us (30%)
  starting transfers between devices  19.1 us (16%)
  waiting for transfers between devices  17.5 us (14%)
  local copies, waits for them, and re-layouts  2.07 us (2%)
    all_to_all x1, blocking collectives, regroup(): return lax.all_to_all(x, 'ctx', split_axis=0, concat_axis=0, tiled=True)  36.6 us
    all_to_all x2, waiting for transfers between devices, regroup(): return lax.all_to_all(x, 'ctx', split_axis=0, concat_axis=0, tiled=True)  17.5 us
    pallas_call x1, Pallas kernels, stage_two(): pl.pallas_call(lambda *refs: last_kernel(scale, *refs), name='stage_two',...  15.8 us
    all_to_all x2, starting transfers between devices, regroup(): return lax.all_to_all(x, 'ctx', split_axis=0, concat_axis=0, tiled=True)  15.3 us
    pallas_call x1, Pallas kernels, project(): pl.pallas_call(project_kernel, name='project', grid_spec=pltpu.PrefetchSc...  12.4 us
    pallas_call x1, Pallas kernels, stage_one(): pl.pallas_call(lambda *refs: first_kernel(scale, *refs), name='stage_one'...  11.9 us
    ppermute x1, starting transfers between devices, shards(): other = lax.ppermute(grad_out, 'tp', [(0, 1), (1, 0)])  3.82 us
    pallas_call x1, Pallas kernels, collect(): pl.pallas_call(collect_kernel, name='collect', out_shape=outs, in_specs=[...  3.77 us
  transfers between devices with their start and end apart: 3, of which 2 were waited for; matrix products, arithmetic and copies ran while one was open for 1% of the time, Pallas kernels for 23%

profile of v7, /device:TPU:1, one launch (start us, length us, event | category | flops | bytes accessed | tf_op | source)
XLA Modules:
  0.0 121.9 jit_solution(3559035010480223722)
XLA Ops:
  0.6 0.0 copy-start
  0.6 3.8 %collective-permute-start = (bf16[128,2048]{1,0:T(8,128)(2,1)}, bf16[128,2048]{1,0:T(8,128)(2,1)S(1)}, u32[]{:S(2)}, u32[]{:S(2)}) collective-permute-start(bf16[128,2048]{1,0:T(8,128)(2,1)} %own_ref.1), channel_id=1, source_target_pairs={{0,1},{1,0},{2,3},{3,2},{4,5},{5,4},{6,7},{7,6},{8,9},{9,8},{10,11... | collective-permute-start | bytes 1572872 | tf_op jit(solution)/shard_map/ppermute | solution.py:706
  4.5 3.8 %collect.1 = (bf16[64,104,128]{2,1,0:T(8,128)(2,1)}, bf16[64,32,128]{2,1,0:T(8,128)(2,1)}) custom-call(bf16[3,128,2048]{2,1,0:T(8,128)(2,1)} %in_hbm.1, f32[128,2048]{1,0:T(8,128)} %taps_hbm.1), custom_call_target="tpu_custom_call" | custom-call | flops 500000000 | bytes 15000000 | tf_op jit(solution)/shard_map/collect/pallas_call | solution.py:612
  8.2 0.0 copy-start.1
  8.3 0.0 copy-start.2
  8.3 9.5 %all-to-all-start.1 = ((bf16[64,104,128]{2,1,0:T(8,128)(2,1)}), bf16[64,104,128]{2,1,0:T(8,128)(2,1)S(1)}, u32[]{:S(2)}, u32[]{:S(2)}) async-start(bf16[64,104,128]{2,1,0:T(8,128)(2,1)} %get-tuple-element.12), calls=%async_computation.1 | async-start | bytes 3407872 | tf_op jit(solution)/shard_map/all_to_all | solution.py:695
  17.8 0.0 collective-permute-done.other_ref
  17.8 0.0 copy-done.1
  17.8 0.0 copy-done.2
  17.9 12.4 %project.1 = bf16[64,72,128]{2,1,0:T(8,128)(2,1)} custom-call(s32[1]{0:T(128)} %bitcast.which_ref, bf16[2048,4096]{1,0:T(8,128)(2,1)} %other_w.1, bf16[2048,4096]{1,0:T(8,128)(2,1)} %other_w.1, bf16[128,2048]{1,0:T(8,128)(2,1)S(1)} %copy-done.1, bf16[128,2048]{1,0:T(8,128)(2,1)S(1)} %collective-permute-done.other_ref, bf16[64,32,128]{2,1,0:T(8,128)(2,1)S(1)} %copy-done.2), custom_call_target="tpu_custom_call" | custom-call | flops 20000000000 | bytes 600000000 | tf_op jit(solution)/shard_map/project/pallas_call | solution.py:669
  30.3 11.7 %all-to-all-done.1.refs_0_.refs_1_ = bf16[64,104,128]{2,1,0:T(8,128)(2,1)S(1)} async-done(((bf16[64,104,128]{2,1,0:T(8,128)(2,1)}), bf16[64,104,128]{2,1,0:T(8,128)(2,1)S(1)}, u32[]{:S(2)}, u32[]{:S(2)}) %all-to-all-start.1) | async-done | bytes 1703968 | tf_op jit(solution)/shard_map/all_to_all | solution.py:695
  42.0 0.0 copy-start.3
  42.0 5.7 %all-to-all-start = ((bf16[64,72,128]{2,1,0:T(8,128)(2,1)}), bf16[64,72,128]{2,1,0:T(8,128)(2,1)}, u32[]{:S(2)}, u32[]{:S(2)}) async-start(bf16[64,72,128]{2,1,0:T(8,128)(2,1)} %project.1), calls=%async_computation | async-start | bytes 2359296 | tf_op jit(solution)/shard_map/all_to_all | solution.py:695
  47.8 0.0 copy-done
  47.8 0.1 constant_dynamic-slice_fusion
  47.9 0.8 broadcast_in_dim.8.refs_1_.refs_6_
  48.6 0.0 copy-done.3
  48.6 11.9 %stage_one.1 = (f32[2,2048,128]{2,1,0:T(8,128)}, f32[2048,256]{1,0:T(8,128)}, f32[2048,256]{1,0:T(8,128)}, f32[2048,128]{1,0:T(8,128)}) custom-call(bf16[64,104,128]{2,1,0:T(8,128)(2,1)} %copy-done.3, f32[9,32,128]{2,1,0:T(8,128)} %broadcast_in_dim.8.refs_1_.refs_6_, bf16[128,192]{1,0:T(8,128)(2,1)} %constant.26.clone.refs_2_.refs_7_, ...), custom_call_target="tpu_custom_call" | custom-call | flops 1400000000 | bytes 42000000 | tf_op jit(solution)/shard_map/stage_one/pallas_call | solution.py:455
  60.5 5.7 %all-to-all-done.refs_0_ = bf16[64,72,128]{2,1,0:T(8,128)(2,1)} async-done(((bf16[64,72,128]{2,1,0:T(8,128)(2,1)}), bf16[64,72,128]{2,1,0:T(8,128)(2,1)}, u32[]{:S(2)}, u32[]{:S(2)}) %all-to-all-start) | async-done | bytes 1179680 | tf_op jit(solution)/shard_map/all_to_all | solution.py:695
  66.2 15.8 %stage_two.1 = bf16[64,136,128]{2,1,0:T(8,128)(2,1)} custom-call(bf16[64,72,128]{2,1,0:T(8,128)(2,1)} %all-to-all-done.refs_0_, bf16[64,104,128]{2,1,0:T(8,128)(2,1)} %copy-done.3, f32[2,2048,128]{2,1,0:T(8,128)} %get-tuple-element.13.refs_2_, f32[2048,256]{1,0:T(8,128)} %get-tuple-element.14.refs_3_, f32[2048,256]{1,0:T(8,128)} %get-tuple-element.15.refs_4_, ...), custom_call_target="tpu_custom_call" | custom-call | flops 1400000000 | bytes 42000000 | tf_op jit(solution)/shard_map/stage_two/pallas_call | solution.py:476
  82.0 36.6 %all_to_all.15.back_ref = bf16[64,136,128]{2,1,0:T(8,128)(2,1)S(1)} all-to-all(bf16[64,136,128]{2,1,0:T(8,128)(2,1)} %stage_two.1), channel_id=1, replica_groups=mesh['ctx'=64,'tp'=2] {'ctx'}, dimensions={0} | all-to-all | bytes 4456448 | tf_op jit(solution)/shard_map/all_to_all | solution.py:695
  118.6 0.2 copy.16
  118.9 0.2 copy.15
  119.0 0.8 reshape.28
  119.8 1.9 %spread.1 = (bf16[3,128,2048]{2,1,0:T(8,128)(2,1)}, f32[128,2048]{1,0:T(8,128)}) custom-call(bf16[64,136,128]{2,1,0:T(8,128)(2,1)S(1)} %all_to_all.15.back_ref), custom_call_target="tpu_custom_call" | custom-call | flops 400000000 | bytes 12000000 | tf_op jit(solution)/shard_map/spread/pallas_call | solution.py:548
  (4 shorter events, 0.1 us)
Async XLA Ops:
  0.6 47.1 %copy-start = (f32[3,3,2048]{2,1,0:T(4,128)S(1)}, f32[3,3,2048]{2,1,0:T(4,128)}, u32[]{:S(2)}) copy-start(f32[3,3,2048]{2,1,0:T(4,128)} %param.11) | copy-start | bytes 221188
  0.6 17.2 %collective-permute-start = (bf16[128,2048]{1,0:T(8,128)(2,1)}, bf16[128,2048]{1,0:T(8,128)(2,1)S(1)}, u32[]{:S(2)}, u32[]{:S(2)}) collective-permute-start(bf16[128,2048]{1,0:T(8,128)(2,1)} %own_ref.1), channel_id=1, source_target_pairs={{0,1},{1,0},{2,3},{3,2},{4,5},{5,4},{6,7},{7,6},{8,9},{9,8},{10,11... | collective-permute-start | bytes 1572872 | tf_op jit(solution)/shard_map/ppermute | solution.py:706
  8.2 9.6 %copy-start.1 = (bf16[128,2048]{1,0:T(8,128)(2,1)S(1)}, bf16[128,2048]{1,0:T(8,128)(2,1)}, u32[]{:S(2)}) copy-start(bf16[128,2048]{1,0:T(8,128)(2,1)} %own_ref.1) | copy-start | bytes 1572868
  8.3 9.6 %copy-start.2 = (bf16[64,32,128]{2,1,0:T(8,128)(2,1)S(1)}, bf16[64,32,128]{2,1,0:T(8,128)(2,1)}, u32[]{:S(2)}) copy-start(bf16[64,32,128]{2,1,0:T(8,128)(2,1)} %get-tuple-element.11.query_ref) | copy-start | bytes 1572868
  8.3 33.7 %all-to-all-start.1 = ((bf16[64,104,128]{2,1,0:T(8,128)(2,1)}), bf16[64,104,128]{2,1,0:T(8,128)(2,1)S(1)}, u32[]{:S(2)}, u32[]{:S(2)}) async-start(bf16[64,104,128]{2,1,0:T(8,128)(2,1)} %get-tuple-element.12), calls=%async_computation.1 | async-start | bytes 3407872 | tf_op jit(solution)/shard_map/all_to_all | solution.py:695
  42.0 6.6 %copy-start.3 = (bf16[64,104,128]{2,1,0:T(8,128)(2,1)}, bf16[64,104,128]{2,1,0:T(8,128)(2,1)S(1)}, u32[]{:S(2)}) copy-start(bf16[64,104,128]{2,1,0:T(8,128)(2,1)S(1)} %all-to-all-done.1.refs_0_.refs_1_) | copy-start | bytes 5111812
  42.0 24.2 %all-to-all-start = ((bf16[64,72,128]{2,1,0:T(8,128)(2,1)}), bf16[64,72,128]{2,1,0:T(8,128)(2,1)}, u32[]{:S(2)}, u32[]{:S(2)}) async-start(bf16[64,72,128]{2,1,0:T(8,128)(2,1)} %project.1), calls=%async_computation | async-start | bytes 2359296 | tf_op jit(solution)/shard_map/all_to_all | solution.py:695

commit v8 on v7

--- a/solution.py
+++ b/solution.py
@@ -170,9 +170,9 @@
 
 
 def first_kernel(scale, in_hbm, weight_ref, *refs):
-    const_in, (mixed_out, filt_out, prod_out, conv_out) = refs[:5], refs[5:9]
-    in_ref, src, mixed_ref, filt_ref, prod_ref, conv_ref = refs[9:15]
-    consts, const_sems, in_sems, out_sems = refs[15:20], refs[20], refs[21], refs[22]
+    const_in, (mixed_out, filt_out, prod_out, conv_out, edge_out) = refs[:5], refs[5:10]
+    in_ref, src, mixed_ref, filt_ref, prod_ref, conv_ref, edge_ref = refs[10:17]
+    consts, const_sems, in_sems, out_sems = refs[17:22], refs[22], refs[23], refs[24]
     first_ref, last_ref, forward_ref, backward_ref, twiddle_ref = consts
     blocks, width = in_ref.shape[0], in_ref.shape[2]
     chans = weight_ref.shape[1]
@@ -201,6 +201,31 @@
     lax.fori_loop(0, blocks // UNROLL, prepare, 0)
     mixed_copy = pltpu.make_async_copy(mixed_ref, mixed_out, out_sems.at[0])
     mixed_copy.start()
+
+    row = lax.broadcasted_iota(jnp.int32, (8, width), 0)
+    group = lax.broadcasted_iota(jnp.int32, (8, width), 1) // chans
+
+    def edges(step, carry):
+        for u in range(0, UNROLL, 2):
+            n1 = step * UNROLL + u
+            two = [in_ref[n1 + h, pl.ds(0, 2 * chans), :].astype(jnp.float32) for h in (0, 1)]
+            turned = jnp.concatenate(two, axis=0).T
+            ends = (turned[width - 8 :], turned[:8])
+            for h in (0, 1):
+                tile = jnp.zeros((8, width), jnp.float32)
+                for i, (end, stream, down) in enumerate(
+                    ((0, 0, 2), (0, 1, 4), (1, 0, 4), (1, 1, 6))
+                ):
+                    part = pltpu.roll(ends[end], down, 0)
+                    shift = (3 - 2 * h - stream) % 4 * chans
+                    part = pltpu.roll(part, shift, 1) if shift else part
+                    tile = jnp.where((row // 2 == i) & (group == 3), part, tile)
+                edge_ref[n1 + h] = tile
+        return carry
+
+    lax.fori_loop(0, blocks // UNROLL, edges, 0)
+    edge_copy = pltpu.make_async_copy(edge_ref, edge_out, out_sems.at[4])
+    edge_copy.start()
     for copy in const_copies:
         copy.wait()
     cos, sin = twiddle_ref[0], twiddle_ref[1]
@@ -236,16 +261,17 @@
     conv_copy = pltpu.make_async_copy(conv_ref, conv_out, out_sems.at[3])
     conv_copy.start()
     mixed_copy.wait()
+    edge_copy.wait()
     pltpu.make_async_copy(filt_ref, filt_out, out_sems.at[1]).wait()
     pltpu.make_async_copy(prod_ref, prod_out, out_sems.at[2]).wait()
     conv_copy.wait()
 
 
-def last_kernel(scale, grad_in, streams_in, mixed_in, filt_in, prod_in, conv_in, weight_ref, *refs):
+def last_kernel(scale, grad_in, streams_in, mixed_in, filt_in, prod_in, conv_in, edge_in, weight_ref, *refs):
     const_in, out_hbm = refs[:5], refs[5]
     query_ref, in_ref, mixed_ref, filt_ref, prod_ref, conv_ref = refs[6:12]
-    grad_ref, src, res, sums, peak, out_ref, tail_ref = refs[12:19]
-    consts, const_sems, grad_sems, sems, spec_sems, out_sems = refs[19:24], *refs[24:29]
+    grad_ref, src, res, sums, peak, halo, lines, edge_ref, out_ref, tail_ref = refs[12:22]
+    consts, const_sems, grad_sems, sems, spec_sems, out_sems = refs[22:27], *refs[27:32]
     first_ref, last_ref, forward_ref, backward_ref, twiddle_ref = consts
     blocks, width = in_ref.shape[0], in_ref.shape[2]
     chans = weight_ref.shape[1]
@@ -253,7 +279,12 @@
     copies = [
         pltpu.make_async_copy(a, b, sems.at[i])
         for i, (a, b) in enumerate(
-            ((mixed_in, mixed_ref), (conv_in, conv_ref), (streams_in, in_ref))
+            (
+                (mixed_in, mixed_ref),
+                (conv_in, conv_ref),
+                (streams_in, in_ref),
+                (edge_in, edge_ref.at[pl.ds(1, blocks)]),
+            )
         )
     ]
 
@@ -286,6 +317,8 @@
 
     lax.fori_loop(0, blocks // UNROLL, prepare, 0)
     peak[...] = jnp.zeros_like(peak)
+    halo[...] = jnp.zeros_like(halo)
+    column = lax.broadcasted_iota(jnp.int32, (blocks, width), 1)
     for copy in const_copies:
         copy.wait()
     cos, sin = twiddle_ref[0], twiddle_ref[1]
@@ -319,8 +352,10 @@
 
             def put(g, out):
                 res[s, pl.ds(base + g, blocks, stride=chans), :] = out
-                if s == 1:
-                    peak[...] = jnp.maximum(peak[...], jnp.abs(out))
+                peak[s] = jnp.maximum(peak[s], jnp.abs(out))
+                if s == 0:
+                    for p in range(2):
+                        halo[p] = jnp.where(column == base + g, out[:, p : p + 1], halo[p])
 
             inverse_one(
                 back[s * part : (s + 1) * part], put, last_ref, cos, sin, blocks, width
@@ -331,39 +366,40 @@
     for copy in copies:
         copy.wait()
 
-    def gradients(n1):
+    def query_grad(n1):
         at = row_of(n1, chans)
-        dz = res[0, at, :]
-        return [
-            grad_ref[at, :] * conv_ref[at, :],
-            dz * mixed_ref[1, at, :],
-            dz * mixed_ref[0, at, :],
-        ]
+        return grad_ref[at, :] * conv_ref[at, :]
 
     sums[...] = jnp.zeros_like(sums)
-    most = jnp.max(jnp.max(peak[...], axis=0, keepdims=True), axis=1, keepdims=True)
-    most = jnp.maximum(most * scale * (1.0 + 2.0**-7), 2.0**-100)
-    bound = jnp.broadcast_to(most.astype(jnp.bfloat16).astype(jnp.float32), (chans, width))
+
+    def most(i):
+        peak_i = jnp.max(jnp.max(peak[i], axis=0, keepdims=True), axis=1, keepdims=True)
+        peak_i = jnp.maximum(peak_i * (scale if i else 1.0) * (1.0 + 2.0**-7), 2.0**-100)
+        peak_i = peak_i.astype(jnp.bfloat16).astype(jnp.float32)
+        return jnp.broadcast_to(peak_i, (chans, width))
+
+    bounds = [most(0), most(1)]
 
     def finish(step, cur):
-        cur = list(cur)
         adds = [None] * 9
         for u in range(UNROLL):
             n1 = step * UNROLL + u
             at = row_of(n1, chans)
-            follow = gradients(jnp.minimum(n1 + 1, blocks - 1))
+            follow = query_grad(jnp.minimum(n1 + 1, blocks - 1))
             if u == UNROLL - 1:
-                follow = [jnp.where(n1 + 1 < blocks, f, 0.0) for f in follow]
-            for b in range(3):
-                weights = [weight_ref[3 * b + j] for j in range(3)]
-                out = ahead(weights, cur[b], follow[b], chans, width)
-                out_ref[n1, pl.ds(b * chans, chans), :] = out.astype(jnp.bfloat16)
-            out_ref[n1, pl.ds(3 * chans, chans), :] = encode(res[1, at, :] * scale, bound)
+                follow = jnp.where(n1 + 1 < blocks, follow, 0.0)
+            weights = [weight_ref[j] for j in range(3)]
+            out = ahead(weights, cur, follow, chans, width)
+            dz = res[0, at, :]
+            out_ref[n1, pl.ds(0, chans), :] = out.astype(jnp.bfloat16)
+            out_ref[n1, pl.ds(chans, chans), :] = encode(dz, bounds[0])
+            out_ref[n1, pl.ds(2 * chans, chans), :] = encode(res[1, at, :] * scale, bounds[1])
+            full = [cur, dz * mixed_ref[1, at, :], dz * mixed_ref[0, at, :]]
             for b in range(3):
                 ref, place = (in_ref, b - 1) if b else (query_ref, 0)
                 parts = lagged(ref, n1, place, chans, width)
                 for j in range(3):
-                    term = cur[b] * parts[j]
+                    term = full[b] * parts[j]
                     old = adds[3 * b + j]
                     adds[3 * b + j] = term if old is None else old + term
             cur = follow
@@ -371,43 +407,52 @@
             sums[t] += adds[t]
         some = pl.ds(step * UNROLL, UNROLL)
         pltpu.make_async_copy(
-            out_ref.at[some], out_hbm.at[some, pl.ds(0, 4 * chans)], out_sems.at[0]
+            out_ref.at[some], out_hbm.at[some, pl.ds(0, 3 * chans)], out_sems.at[0]
         ).start()
-        return tuple(cur)
-
-    lax.fori_loop(0, blocks // UNROLL, finish, tuple(gradients(0)))
-
+        return cur
+
+    lax.fori_loop(0, blocks // UNROLL, finish, query_grad(0))
+
+    edge_ref[0] = jnp.zeros(edge_ref.shape[1:], jnp.float32)
+    edge_ref[blocks + 1] = jnp.zeros(edge_ref.shape[1:], jnp.float32)
     total = jnp.zeros((chans, width), jnp.float32)
     for t in range(9):
         column = jnp.sum(sums[t], axis=1, keepdims=True) * scale
         total = total + jnp.where(lane == t, column, 0.0)
-    per = width // chans
-    total = jnp.concatenate([total] + [jnp.zeros_like(total)] * (per - 1), axis=0).T
-    high = total.astype(jnp.bfloat16).astype(jnp.float32)
-    mid = (total - high).astype(jnp.bfloat16).astype(jnp.float32)
-    low = total - high - mid
-    lines = [p[t : t + 1] for p in (high, mid, low) for t in range(9)]
-    lines += [jnp.where(lane[:1] < chans, bound[:1], 0.0)] * (8 * per - 27)
-    packed = []
-    for r in range(8):
-        row = jnp.zeros((1, width), jnp.float32)
-        for a, line in enumerate(lines[per * r : per * r + per]):
-            row = row + (pltpu.roll(line, a * chans, 1) if a else line)
-        packed.append(row)
-    packed = jnp.concatenate(packed, axis=0).astype(jnp.bfloat16)
+    pad = [jnp.zeros_like(total)] * (width // chans - 1)
+    total = jnp.concatenate([total] + pad, axis=0).T
+    high, low = [p.astype(jnp.float32) for p in split(total)]
+    row = lax.broadcasted_iota(jnp.int32, (8, width), 0)
+    group = lax.broadcasted_iota(jnp.int32, (8, width), 1) // chans
+    fixed = high[:8] + pltpu.roll(low[:8], chans, 1)
+    extra = jnp.where(row == 0, high[8:9], 0.0) + jnp.where(row == 1, low[8:9], 0.0)
+    extra = jnp.where(row == 6, bounds[1][:1], extra)
+    extra = jnp.where(row == 7, bounds[0][:1], extra)
+    extra = pltpu.roll(jnp.where(group == 0, extra, 0.0), 2 * chans, 1)
+    fixed = fixed + extra
+    for p in range(2):
+        high, low = [x.astype(jnp.float32) for x in split(halo[p])]
+        lines[p, pl.ds(0, blocks), :] = pltpu.roll(high, 2 * chans, 1)
+        lines[2 + p, pl.ds(0, blocks), :] = pltpu.roll(low, 2 * chans, 1)
+        lines[p, pl.ds(blocks, 8), :] = jnp.zeros((8, width), jnp.float32)
+        lines[2 + p, pl.ds(blocks, 8), :] = jnp.zeros((8, width), jnp.float32)
 
     def attach(n1, carry):
-        tail_ref[n1] = packed
+        tile = fixed
+        for i in range(4):
+            tile = tile + jnp.where(row == 2 + i, lines[i, pl.ds(n1 + 1, 1), :], 0.0)
+        tile = tile + jnp.where(row < 4, edge_ref[n1], edge_ref[n1 + 2])
+        tail_ref[n1] = tile.astype(jnp.bfloat16)
         return carry
 
     lax.fori_loop(0, blocks, attach, 0)
     tail = pltpu.make_async_copy(
-        tail_ref, out_hbm.at[:, pl.ds(4 * chans, 8)], out_sems.at[1]
+        tail_ref, out_hbm.at[:, pl.ds(3 * chans, 8)], out_sems.at[1]
     )
     tail.start()
     tail.wait()
     pltpu.make_async_copy(
-        out_ref, out_hbm.at[:, pl.ds(0, 4 * chans)], out_sems.at[0]
+        out_ref, out_hbm.at[:, pl.ds(0, 3 * chans)], out_sems.at[0]
     ).wait()
 
 
@@ -452,32 +497,33 @@
     chans = weight.shape[1]
     rows = blocks * chans
     shapes = [f32(2, rows, width), f32(rows, 2 * width), f32(rows, 2 * width), f32(rows, width)]
+    shapes.append(f32(blocks, 8, width))
     return pl.pallas_call(
         lambda *refs: first_kernel(scale, *refs),
         name="stage_one",
         out_shape=tuple(shapes),
         in_specs=[hbm(), vmem()] + [hbm()] * 5,
-        out_specs=(hbm(),) * 4,
+        out_specs=(hbm(),) * 5,
         scratch_shapes=room(streams, f32(2, rows, width), *shapes, *consts)
         + [
             pltpu.SemaphoreType.DMA((5,)),
             pltpu.SemaphoreType.DMA((blocks // UNROLL,)),
-            pltpu.SemaphoreType.DMA((4,)),
+            pltpu.SemaphoreType.DMA((5,)),
         ],
         cost_estimate=estimate(14),
         compiler_params=params(60),
     )(streams, weight, *consts)
 
 
-def stage_two(grad, streams, mixed, filt, prod, conv, weight, consts, scale):
+def stage_two(grad, streams, mixed, filt, prod, conv, edge, weight, consts, scale):
     blocks, width = streams.shape[0], streams.shape[2]
     chans = weight.shape[1]
     rows = blocks * chans
     return pl.pallas_call(
         lambda *refs: last_kernel(scale, *refs),
         name="stage_two",
-        out_shape=bf16(blocks, 4 * chans + 8, width),
-        in_specs=[hbm()] * 6 + [vmem()] + [hbm()] * 5,
+        out_shape=bf16(blocks, 3 * chans + 8, width),
+        in_specs=[hbm()] * 7 + [vmem()] + [hbm()] * 5,
         out_specs=hbm(),
         scratch_shapes=room(
             grad,
@@ -490,29 +536,40 @@
             f32(rows, width),
             f32(2, rows, width),
             f32(9, chans, width),
-            f32(blocks, width),
-            bf16(blocks, 4 * chans, width),
+            f32(2, blocks, width),
+            f32(2, blocks, width),
+            f32(4, blocks + 8, width),
+            f32(blocks + 2, 8, width),
+            bf16(blocks, 3 * chans, width),
             bf16(blocks, 8, width),
             *consts,
         )
         + [
             pltpu.SemaphoreType.DMA((5,)),
             pltpu.SemaphoreType.DMA((blocks // UNROLL,)),
-            pltpu.SemaphoreType.DMA((3,)),
+            pltpu.SemaphoreType.DMA((4,)),
             pltpu.SemaphoreType.DMA((2, chans // GROUP)),
             pltpu.SemaphoreType.DMA((2,)),
         ],
         cost_estimate=estimate(14),
         compiler_params=params(61),
-    )(grad, streams, mixed, filt, prod, conv, weight, *consts)
-
-
-def spread_kernel(back_ref, ig_hbm, tg_hbm, ig_ref, tg_ref, sems):
+    )(grad, streams, mixed, filt, prod, conv, edge, weight, *consts)
+
+
+def spread_kernel(back_ref, in_hbm, weight_ref, ig_hbm, tg_hbm, sg_ref, in_ref, ig_ref, tg_ref, sems):
     count, _, width = back_ref.shape
     total = tg_ref.shape[1]
     chans = total // count
     some = width // chans
     wide = total // CHUNKS
+    row = lax.broadcasted_iota(jnp.int32, (8, width), 0)
+    group = lax.broadcasted_iota(jnp.int32, (8, width), 1) // chans
+
+    def fetch(part):
+        cols = pl.ds(part * wide, wide)
+        return pltpu.make_async_copy(
+            in_hbm.at[pl.ds(1, 2), :, cols], in_ref.at[..., cols], sems.at[2, part]
+        )
 
     def copies(part):
         cols = pl.ds(part * wide, wide)
@@ -522,19 +579,52 @@
         ]
 
     for part in range(CHUNKS):
+        fetch(part).start()
+    for part in range(CHUNKS):
+        fetch(part).wait()
         for m in range(part * wide // width, (part + 1) * wide // width):
             cols = pl.ds(m * width, width)
             owners = range(m * some, (m + 1) * some)
-            for b in range(3):
-                rows = [back_ref[d, pl.ds(b * chans, chans), :] for d in owners]
-                rows = jnp.concatenate(rows, axis=0).astype(jnp.float32)
-                ig_ref[b, :, cols] = rows.T.astype(jnp.bfloat16)
-            rows = []
-            for d in owners:
-                bound = back_ref[d, pl.ds(4 * chans, 8), :].astype(jnp.float32)[7:8]
-                bound = jnp.broadcast_to(bound, (chans, width))
-                rows.append(decode(back_ref[d, pl.ds(3 * chans, chans), :], bound))
-            tg_ref[:, cols] = jnp.concatenate(rows, axis=0).T
+            parts = []
+            for i in range(3):
+                rows = [back_ref[d, pl.ds(i * chans, chans), :] for d in owners]
+                parts.append(jnp.concatenate(rows, axis=0).astype(jnp.float32).T)
+            ig_ref[0, :, cols] = parts[0].astype(jnp.bfloat16)
+            sums = jnp.zeros((8, width), jnp.float32)
+            extra = jnp.zeros((8, width), jnp.float32)
+            edge = jnp.zeros((8, width), jnp.float32)
+            for a, d in enumerate(owners):
+                tile = back_ref[d, pl.ds(3 * chans, 8), :].astype(jnp.float32)
+                turned = [pltpu.roll(tile, (a - i) % some * chans, 1) if a != i else tile for i in range(4)]
+                sums = jnp.where(group == a, turned[0] + turned[1], sums)
+                extra = jnp.where(group == a, turned[2], extra)
+                edge = jnp.where(group == a, turned[3], edge)
+            for t in range(9):
+                line = sums[t : t + 1] if t < 8 else extra[:1] + extra[1:2]
+                sg_ref[t // 3, pl.ds(t % 3, 1), cols] = line
+            tg_ref[:, cols] = decode(parts[2], extra[6:7])
+            dz = decode(parts[1], extra[7:8])
+            after = pltpu.roll(extra, 6, 0) + pltpu.roll(extra, 4, 0)
+            dz = jnp.concatenate([dz, jnp.where(row < 2, after, 0.0)], axis=0)
+            weights = [[weight_ref[b, pl.ds(j, 1), cols] for j in range(3)] for b in range(3)]
+            for b in (1, 2):
+                other = 3 - b
+                x = jnp.concatenate(
+                    [
+                        pltpu.roll(edge, 8 - 2 * other, 0),
+                        in_ref[other - 1, :, cols].astype(jnp.float32),
+                        pltpu.roll(edge, 6 - 2 * other, 0),
+                    ],
+                    axis=0,
+                )
+                mixed = weights[other][0] * x
+                for j in (1, 2):
+                    mixed = mixed + weights[other][j] * pltpu.roll(x, j, 0)
+                dm = dz * mixed[8:]
+                out = weights[b][0] * dm
+                for j in (1, 2):
+                    out = out + weights[b][j] * pltpu.roll(dm, dm.shape[0] - j, 0)
+                ig_ref[b, :, cols] = out[:width].astype(jnp.bfloat16)
         for copy in copies(part):
             copy.start()
     for part in range(CHUNKS):
@@ -542,19 +632,19 @@
             copy.wait()
 
 
-def spread(back, chans):
-    count, _, width = back.shape
-    outs = (bf16(3, width, count * chans), f32(width, count * chans))
+def spread(back, inputs, weight):
+    rows, total = inputs.shape[1:]
+    outs = (bf16(3, rows, total), f32(rows, total))
     return pl.pallas_call(
         spread_kernel,
         name="spread",
-        out_shape=outs,
-        in_specs=[vmem()],
-        out_specs=(hbm(), hbm()),
-        scratch_shapes=room(*outs) + [pltpu.SemaphoreType.DMA((2, CHUNKS))],
-        cost_estimate=estimate(4),
+        out_shape=outs + (f32(*weight.shape),),
+        in_specs=[vmem(), hbm(), vmem()],
+        out_specs=(hbm(), hbm(), vmem()),
+        scratch_shapes=room(bf16(2, rows, total), *outs) + [pltpu.SemaphoreType.DMA((3, CHUNKS))],
+        cost_estimate=estimate(5),
         compiler_params=params(24),
-    )(back)
+    )(back, inputs, weight)
 
 
 def collect_kernel(in_hbm, taps_hbm, out_hbm, query_hbm, in_ref, taps_ref, out_ref, query_ref, sems):
@@ -706,21 +796,18 @@
     other = lax.ppermute(grad_out, "tp", [(0, 1), (1, 0)])
     streams = regroup(streams)
     which = lax.axis_index("tp").astype(jnp.int32).reshape(1)
-    gated = regroup(project(which, w_out, grad_out, other, query))
+    gated = project(which, w_out, grad_out, other, query)
+    gated = regroup(gated)
 
     weight = lax.dynamic_slice_in_dim(short_weight, where * chans, chans, axis=2)
     weight = jnp.broadcast_to(weight.reshape(9, chans, 1), (9, chans, rows))
 
     consts = [jnp.asarray(t) for t in tables(count, rows)]
-    mixed, filt, prod, conv = stage_one(streams, weight, consts, scale)
-    back = stage_two(gated, streams, mixed, filt, prod, conv, weight, consts, scale)
+    mixed, filt, prod, conv, edge = stage_one(streams, weight, consts, scale)
+    back = stage_two(gated, streams, mixed, filt, prod, conv, edge, weight, consts, scale)
 
     back = regroup(back)
-    inputs_grad, taps_grad = spread(back, chans)
-    sums = back[:, 4 * chans :].astype(jnp.float32)
-    sums = sums.reshape(count, 8 * rows)[:, : 27 * chans].reshape(count, 3, 9, chans)
-    short_grad = jnp.sum(sums, axis=1).transpose(1, 0, 2).reshape(3, 3, local)
-    return inputs_grad, taps_grad, short_grad
+    return spread(back, inputs, short_weight)
 
 
 def solution(mesh):

time: 122 us -> 119 us (0.975)
  blocking collectives: 36.6 us -> 30.1 us
  Pallas kernels: 45.7 us -> 51.9 us
  waiting for transfers between devices: 17.5 us -> 14.8 us
    all_to_all x1, blocking collectives: 36.6 us -> 30.1 us  [regroup(): return lax.all_to_all(x, 'ctx', split_axis=0, concat_axis=0, tiled=True)]
    pallas_call x1, Pallas kernels: 1.87 us -> 5.12 us  [spread(): pl.pallas_call(spread_kernel, name='spread', out_shape=outs + (f32(*weigh...]
    all_to_all x2, waiting for transfers between devices: 17.5 us -> 14.8 us  [regroup(): return lax.all_to_all(x, 'ctx', split_axis=0, concat_axis=0, tiled=True)]
    pallas_call x1, Pallas kernels: 11.9 us -> 14.4 us  [stage_one(): pl.pallas_call(lambda *refs: first_kernel(scale, *refs), name='stage_one'...]
  transfers between devices with their start and end apart: 3 -> 3, of which waited for: 2 -> 2; matrix products, arithmetic and copies ran while one was open for 1% -> 1% of each run, Pallas kernels for 23% -> 26%
where the time goes in v8:
time: 119 us; the launch traced here: 118 us
  Pallas kernels  51.9 us (44%)
  blocking collectives  30.1 us (25%)
  starting transfers between devices  18.7 us (16%)
  waiting for transfers between devices  14.8 us (12%)
  local copies, waits for them, and re-layouts  1.89 us (2%)
    all_to_all x1, blocking collectives, regroup(): return lax.all_to_all(x, 'ctx', split_axis=0, concat_axis=0, tiled=True)  30.1 us
    pallas_call x1, Pallas kernels, stage_two(): pl.pallas_call(lambda *refs: last_kernel(scale, *refs), name='stage_two',...  16.1 us
    all_to_all x2, starting transfers between devices, regroup(): return lax.all_to_all(x, 'ctx', split_axis=0, concat_axis=0, tiled=True)  14.9 us
    all_to_all x2, waiting for transfers between devices, regroup(): return lax.all_to_all(x, 'ctx', split_axis=0, concat_axis=0, tiled=True)  14.8 us
    pallas_call x1, Pallas kernels, stage_one(): pl.pallas_call(lambda *refs: first_kernel(scale, *refs), name='stage_one'...  14.4 us
    pallas_call x1, Pallas kernels, project(): pl.pallas_call(project_kernel, name='project', grid_spec=pltpu.PrefetchSc...  12.4 us
    pallas_call x1, Pallas kernels, spread(): pl.pallas_call(spread_kernel, name='spread', out_shape=outs + (f32(*weigh...  5.12 us
    ppermute x1, starting transfers between devices, shards(): other = lax.ppermute(grad_out, 'tp', [(0, 1), (1, 0)])  3.82 us
  transfers between devices with their start and end apart: 3, of which 2 were waited for; matrix products, arithmetic and copies ran while one was open for 1% of the time, Pallas kernels for 26%

profile of v8, /device:TPU:1, one launch (start us, length us, event | category | flops | bytes accessed | tf_op | source)
XLA Modules:
  0.0 118.4 jit_solution(14667645060229973920)
XLA Ops:
  0.6 3.8 %collective-permute-start = (bf16[128,2048]{1,0:T(8,128)(2,1)}, bf16[128,2048]{1,0:T(8,128)(2,1)S(1)}, u32[]{:S(2)}, u32[]{:S(2)}) collective-permute-start(bf16[128,2048]{1,0:T(8,128)(2,1)} %own_ref.1), channel_id=1, source_target_pairs={{0,1},{1,0},{2,3},{3,2},{4,5},{5,4},{6,7},{7,6},{8,9},{9,8},{10,11... | collective-permute-start | bytes 1572872 | tf_op jit(solution)/shard_map/ppermute | solution.py:796
  4.5 3.8 %collect.1 = (bf16[64,104,128]{2,1,0:T(8,128)(2,1)}, bf16[64,32,128]{2,1,0:T(8,128)(2,1)}) custom-call(bf16[3,128,2048]{2,1,0:T(8,128)(2,1)} %in_hbm.3, f32[128,2048]{1,0:T(8,128)} %taps_hbm.1), custom_call_target="tpu_custom_call" | custom-call | flops 500000000 | bytes 15000000 | tf_op jit(solution)/shard_map/collect/pallas_call | solution.py:702
  8.2 0.0 copy-start.2
  8.2 0.0 copy-start.3
  8.3 9.5 %all-to-all-start.1 = ((bf16[64,104,128]{2,1,0:T(8,128)(2,1)}), bf16[64,104,128]{2,1,0:T(8,128)(2,1)S(1)}, u32[]{:S(2)}, u32[]{:S(2)}) async-start(bf16[64,104,128]{2,1,0:T(8,128)(2,1)} %get-tuple-element.11), calls=%async_computation.1 | async-start | bytes 3407872 | tf_op jit(solution)/shard_map/all_to_all | solution.py:785
  17.8 0.0 collective-permute-done.other_ref
  17.8 0.0 copy-done.2
  17.8 0.0 copy-done.3
  17.8 12.4 %project.1 = bf16[64,72,128]{2,1,0:T(8,128)(2,1)} custom-call(s32[1]{0:T(128)} %bitcast.which_ref, bf16[2048,4096]{1,0:T(8,128)(2,1)} %other_w.1, bf16[2048,4096]{1,0:T(8,128)(2,1)} %other_w.1, bf16[128,2048]{1,0:T(8,128)(2,1)S(1)} %copy-done.2, bf16[128,2048]{1,0:T(8,128)(2,1)S(1)} %collective-permute-done.other_ref, bf16[64,32,128]{2,1,0:T(8,128)(2,1)S(1)} %copy-done.3), custom_call_target="tpu_custom_call" | custom-call | flops 20000000000 | bytes 600000000 | tf_op jit(solution)/shard_map/project/pallas_call | solution.py:759
  30.2 0.0 copy-start.1
  30.3 11.7 %all-to-all-done.1.refs_0_.refs_1_ = bf16[64,104,128]{2,1,0:T(8,128)(2,1)S(1)} async-done(((bf16[64,104,128]{2,1,0:T(8,128)(2,1)}), bf16[64,104,128]{2,1,0:T(8,128)(2,1)S(1)}, u32[]{:S(2)}, u32[]{:S(2)}) %all-to-all-start.1) | async-done | bytes 1703968 | tf_op jit(solution)/shard_map/all_to_all | solution.py:785
  42.0 0.0 copy-start.4
  42.0 5.4 %all-to-all-start = ((bf16[64,72,128]{2,1,0:T(8,128)(2,1)}), bf16[64,72,128]{2,1,0:T(8,128)(2,1)S(1)}, u32[]{:S(2)}, u32[]{:S(2)}) async-start(bf16[64,72,128]{2,1,0:T(8,128)(2,1)} %project.1), calls=%async_computation | async-start | bytes 2359296 | tf_op jit(solution)/shard_map/all_to_all | solution.py:785
  47.4 0.0 copy-done.1
  47.4 0.1 constant_dynamic-slice_fusion
  47.5 0.8 broadcast_in_dim.8.refs_1_.refs_7_
  48.2 0.0 copy-done.4
  48.2 14.4 %stage_one.1 = (f32[2,2048,128]{2,1,0:T(8,128)}, f32[2048,256]{1,0:T(8,128)}, f32[2048,256]{1,0:T(8,128)}, f32[2048,128]{1,0:T(8,128)}, f32[64,8,128]{2,1,0:T(8,128)}) custom-call(bf16[64,104,128]{2,1,0:T(8,128)(2,1)} %copy-done.4, f32[9,32,128]{2,1,0:T(8,128)} %broadcast_in_dim.8.refs_1_.refs_7_, bf16[128,192]{1,0:T(8,128)(2,1)} %constant.24.clone.refs_2_.refs_8_, ...), custom_call_target="tpu_custom_call" | custom-call | flops 1400000000 | bytes 42000000 | tf_op jit(solution)/shard_map/stage_one/pallas_call | solution.py:501
  62.7 3.1 %all-to-all-done.refs_0_ = bf16[64,72,128]{2,1,0:T(8,128)(2,1)S(1)} async-done(((bf16[64,72,128]{2,1,0:T(8,128)(2,1)}), bf16[64,72,128]{2,1,0:T(8,128)(2,1)S(1)}, u32[]{:S(2)}, u32[]{:S(2)}) %all-to-all-start) | async-done | bytes 1179680 | tf_op jit(solution)/shard_map/all_to_all | solution.py:785
  65.8 0.0 copy-start.5
  65.8 1.0 copy-done.5
  66.8 16.1 %stage_two.1 = bf16[64,104,128]{2,1,0:T(8,128)(2,1)} custom-call(bf16[64,72,128]{2,1,0:T(8,128)(2,1)} %copy-done.5, bf16[64,104,128]{2,1,0:T(8,128)(2,1)} %copy-done.4, f32[2,2048,128]{2,1,0:T(8,128)} %get-tuple-element.12.refs_2_, f32[2048,256]{1,0:T(8,128)} %get-tuple-element.13.refs_3_, f32[2048,256]{1,0:T(8,128)} %get-tuple-element.14.refs_4_, ...), custom_call_target="tpu_custom_call" | custom-call | flops 1400000000 | bytes 42000000 | tf_op jit(solution)/shard_map/stage_two/pallas_call | solution.py:522
  82.9 0.0 copy-start
  82.9 30.1 %all_to_all.15.back_ref = bf16[64,104,128]{2,1,0:T(8,128)(2,1)S(1)} all-to-all(bf16[64,104,128]{2,1,0:T(8,128)(2,1)} %stage_two.1), channel_id=1, replica_groups=mesh['ctx'=64,'tp'=2] {'ctx'}, dimensions={0} | all-to-all | bytes 3407872 | tf_op jit(solution)/shard_map/all_to_all | solution.py:785
  113.1 0.0 copy-done
  113.1 5.1 %spread.1 = (bf16[3,128,2048]{2,1,0:T(8,128)(2,1)}, f32[128,2048]{1,0:T(8,128)}, f32[3,3,2048]{2,1,0:T(4,128)}) custom-call(bf16[64,104,128]{2,1,0:T(8,128)(2,1)S(1)} %all_to_all.15.back_ref, bf16[3,128,2048]{2,1,0:T(8,128)(2,1)S(1)} %copy-done, f32[3,3,2048]{2,1,0:T(4,128)S(1)} %copy-done.1), custom_call_target="tpu_custom_call" | custom-call | flops 500000000 | bytes 15000000 | tf_op jit(solution)/shard_map/spread/pallas_call | solution.py:638
  (1 shorter events, 0.0 us)
Async XLA Ops:
  0.6 17.2 %collective-permute-start = (bf16[128,2048]{1,0:T(8,128)(2,1)}, bf16[128,2048]{1,0:T(8,128)(2,1)S(1)}, u32[]{:S(2)}, u32[]{:S(2)}) collective-permute-start(bf16[128,2048]{1,0:T(8,128)(2,1)} %own_ref.1), channel_id=1, source_target_pairs={{0,1},{1,0},{2,3},{3,2},{4,5},{5,4},{6,7},{7,6},{8,9},{9,8},{10,11... | collective-permute-start | bytes 1572872 | tf_op jit(solution)/shard_map/ppermute | solution.py:796
  8.2 9.6 %copy-start.2 = (bf16[128,2048]{1,0:T(8,128)(2,1)S(1)}, bf16[128,2048]{1,0:T(8,128)(2,1)}, u32[]{:S(2)}) copy-start(bf16[128,2048]{1,0:T(8,128)(2,1)} %own_ref.1) | copy-start | bytes 1572868
  8.2 9.6 %copy-start.3 = (bf16[64,32,128]{2,1,0:T(8,128)(2,1)S(1)}, bf16[64,32,128]{2,1,0:T(8,128)(2,1)}, u32[]{:S(2)}) copy-start(bf16[64,32,128]{2,1,0:T(8,128)(2,1)} %get-tuple-element.10.query_ref) | copy-start | bytes 1572868
  8.3 33.7 %all-to-all-start.1 = ((bf16[64,104,128]{2,1,0:T(8,128)(2,1)}), bf16[64,104,128]{2,1,0:T(8,128)(2,1)S(1)}, u32[]{:S(2)}, u32[]{:S(2)}) async-start(bf16[64,104,128]{2,1,0:T(8,128)(2,1)} %get-tuple-element.11), calls=%async_computation.1 | async-start | bytes 3407872 | tf_op jit(solution)/shard_map/all_to_all | solution.py:785
  30.2 17.1 %copy-start.1 = (f32[3,3,2048]{2,1,0:T(4,128)S(1)}, f32[3,3,2048]{2,1,0:T(4,128)}, u32[]{:S(2)}) copy-start(f32[3,3,2048]{2,1,0:T(4,128)} %weight_ref.1) | copy-start | bytes 221188
  42.0 6.2 %copy-start.4 = (bf16[64,104,128]{2,1,0:T(8,128)(2,1)}, bf16[64,104,128]{2,1,0:T(8,128)(2,1)S(1)}, u32[]{:S(2)}) copy-start(bf16[64,104,128]{2,1,0:T(8,128)(2,1)S(1)} %all-to-all-done.1.refs_0_.refs_1_) | copy-start | bytes 5111812
  42.0 23.8 %all-to-all-start = ((bf16[64,72,128]{2,1,0:T(8,128)(2,1)}), bf16[64,72,128]{2,1,0:T(8,128)(2,1)S(1)}, u32[]{:S(2)}, u32[]{:S(2)}) async-start(bf16[64,72,128]{2,1,0:T(8,128)(2,1)} %project.1), calls=%async_computation | async-start | bytes 2359296 | tf_op jit(solution)/shard_map/all_to_all | solution.py:785
  65.8 1.0 copy-start.5
  82.9 30.1 %copy-start = (bf16[3,128,2048]{2,1,0:T(8,128)(2,1)S(1)}, bf16[3,128,2048]{2,1,0:T(8,128)(2,1)}, u32[]{:S(2)}) copy-start(bf16[3,128,2048]{2,1,0:T(8,128)(2,1)} %in_hbm.3) | copy-start | bytes 4718596

commit v9 on v8

--- a/solution.py
+++ b/solution.py
@@ -12,6 +12,8 @@
 UNROLL = 8
 STEPS = 240
 CHUNKS = 4
+ONE_MIB = 60
+TWO_MIB = 62
 PROJECT_US = 200
 
 
@@ -57,8 +59,8 @@
     return high, low
 
 
-def encode(x, bound):
-    root = jnp.minimum(jnp.sqrt(jnp.abs(x) * (1.0 / bound)), 1.0)
+def encode(x, inverse):
+    root = jnp.minimum(jnp.sqrt(jnp.abs(x) * inverse), 1.0)
     n = jnp.floor(root * (STEPS * 128.0) + 0.5)
     high = jnp.floor(n * (1.0 / 128.0))
     code = jnp.exp2(high - STEPS / 2) * (1.0 + (n - 128.0 * high) * (1.0 / 128.0))
@@ -149,6 +151,7 @@
 
 def coded(in_ref, n1, b, chans):
     bound = in_ref[n1, pl.ds((b + 1) * chans, 8), :].astype(jnp.float32)
+    bound = jnp.broadcast_to(bound[:, :1], bound.shape)
     bound = jnp.concatenate([bound] * (chans // 8), axis=0)
     return decode(in_ref[n1, pl.ds(b * chans, chans), :], bound)
 
@@ -170,9 +173,9 @@
 
 
 def first_kernel(scale, in_hbm, weight_ref, *refs):
-    const_in, (mixed_out, filt_out, prod_out, conv_out, edge_out) = refs[:5], refs[5:10]
-    in_ref, src, mixed_ref, filt_ref, prod_ref, conv_ref, edge_ref = refs[10:17]
-    consts, const_sems, in_sems, out_sems = refs[17:22], refs[22], refs[23], refs[24]
+    const_in, (mixed_out, filt_out, prod_out, conv_out) = refs[:5], refs[5:9]
+    in_ref, src, mixed_ref, filt_ref, prod_ref, conv_ref = refs[9:15]
+    consts, const_sems, in_sems, out_sems = refs[15:20], refs[20], refs[21], refs[22]
     first_ref, last_ref, forward_ref, backward_ref, twiddle_ref = consts
     blocks, width = in_ref.shape[0], in_ref.shape[2]
     chans = weight_ref.shape[1]
@@ -201,31 +204,6 @@
     lax.fori_loop(0, blocks // UNROLL, prepare, 0)
     mixed_copy = pltpu.make_async_copy(mixed_ref, mixed_out, out_sems.at[0])
     mixed_copy.start()
-
-    row = lax.broadcasted_iota(jnp.int32, (8, width), 0)
-    group = lax.broadcasted_iota(jnp.int32, (8, width), 1) // chans
-
-    def edges(step, carry):
-        for u in range(0, UNROLL, 2):
-            n1 = step * UNROLL + u
-            two = [in_ref[n1 + h, pl.ds(0, 2 * chans), :].astype(jnp.float32) for h in (0, 1)]
-            turned = jnp.concatenate(two, axis=0).T
-            ends = (turned[width - 8 :], turned[:8])
-            for h in (0, 1):
-                tile = jnp.zeros((8, width), jnp.float32)
-                for i, (end, stream, down) in enumerate(
-                    ((0, 0, 2), (0, 1, 4), (1, 0, 4), (1, 1, 6))
-                ):
-                    part = pltpu.roll(ends[end], down, 0)
-                    shift = (3 - 2 * h - stream) % 4 * chans
-                    part = pltpu.roll(part, shift, 1) if shift else part
-                    tile = jnp.where((row // 2 == i) & (group == 3), part, tile)
-                edge_ref[n1 + h] = tile
-        return carry
-
-    lax.fori_loop(0, blocks // UNROLL, edges, 0)
-    edge_copy = pltpu.make_async_copy(edge_ref, edge_out, out_sems.at[4])
-    edge_copy.start()
     for copy in const_copies:
         copy.wait()
     cos, sin = twiddle_ref[0], twiddle_ref[1]
@@ -261,17 +239,16 @@
     conv_copy = pltpu.make_async_copy(conv_ref, conv_out, out_sems.at[3])
     conv_copy.start()
     mixed_copy.wait()
-    edge_copy.wait()
     pltpu.make_async_copy(filt_ref, filt_out, out_sems.at[1]).wait()
     pltpu.make_async_copy(prod_ref, prod_out, out_sems.at[2]).wait()
     conv_copy.wait()
 
 
-def last_kernel(scale, grad_in, streams_in, mixed_in, filt_in, prod_in, conv_in, edge_in, weight_ref, *refs):
+def last_kernel(scale, grad_in, streams_in, mixed_in, filt_in, prod_in, conv_in, weight_ref, *refs):
     const_in, out_hbm = refs[:5], refs[5]
     query_ref, in_ref, mixed_ref, filt_ref, prod_ref, conv_ref = refs[6:12]
-    grad_ref, src, res, sums, peak, halo, lines, edge_ref, out_ref, tail_ref = refs[12:22]
-    consts, const_sems, grad_sems, sems, spec_sems, out_sems = refs[22:27], *refs[27:32]
+    grad_ref, src, res, sums, peak, halo, lines, out_ref, tail_ref = refs[12:21]
+    consts, const_sems, grad_sems, sems, spec_sems, out_sems = refs[21:26], *refs[26:31]
     first_ref, last_ref, forward_ref, backward_ref, twiddle_ref = consts
     blocks, width = in_ref.shape[0], in_ref.shape[2]
     chans = weight_ref.shape[1]
@@ -283,7 +260,6 @@
                 (mixed_in, mixed_ref),
                 (conv_in, conv_ref),
                 (streams_in, in_ref),
-                (edge_in, edge_ref.at[pl.ds(1, blocks)]),
             )
         )
     ]
@@ -379,6 +355,7 @@
         return jnp.broadcast_to(peak_i, (chans, width))
 
     bounds = [most(0), most(1)]
+    inverses = [1.0 / bound for bound in bounds]
 
     def finish(step, cur):
         adds = [None] * 9
@@ -392,8 +369,8 @@
             out = ahead(weights, cur, follow, chans, width)
             dz = res[0, at, :]
             out_ref[n1, pl.ds(0, chans), :] = out.astype(jnp.bfloat16)
-            out_ref[n1, pl.ds(chans, chans), :] = encode(dz, bounds[0])
-            out_ref[n1, pl.ds(2 * chans, chans), :] = encode(res[1, at, :] * scale, bounds[1])
+            out_ref[n1, pl.ds(chans, chans), :] = encode(dz, inverses[0])
+            out_ref[n1, pl.ds(2 * chans, chans), :] = encode(res[1, at, :] * scale, inverses[1])
             full = [cur, dz * mixed_ref[1, at, :], dz * mixed_ref[0, at, :]]
             for b in range(3):
                 ref, place = (in_ref, b - 1) if b else (query_ref, 0)
@@ -413,8 +390,6 @@
 
     lax.fori_loop(0, blocks // UNROLL, finish, query_grad(0))
 
-    edge_ref[0] = jnp.zeros(edge_ref.shape[1:], jnp.float32)
-    edge_ref[blocks + 1] = jnp.zeros(edge_ref.shape[1:], jnp.float32)
     total = jnp.zeros((chans, width), jnp.float32)
     for t in range(9):
         column = jnp.sum(sums[t], axis=1, keepdims=True) * scale
@@ -441,7 +416,13 @@
         tile = fixed
         for i in range(4):
             tile = tile + jnp.where(row == 2 + i, lines[i, pl.ds(n1 + 1, 1), :], 0.0)
-        tile = tile + jnp.where(row < 4, edge_ref[n1], edge_ref[n1 + 2])
+        near = [
+            in_ref[i, pl.ds(3 * chans, 8), :].astype(jnp.float32)
+            for i in (jnp.maximum(n1 - 1, 0), jnp.minimum(n1 + 1, blocks - 1))
+        ]
+        keep = ((row < 4) & (n1 > 0)) | ((row >= 4) & (n1 + 1 < blocks))
+        edge = jnp.where(row < 4, near[0], near[1])
+        tile = jnp.where(group == 3, jnp.where(keep, edge, 0.0), tile)
         tail_ref[n1] = tile.astype(jnp.bfloat16)
         return carry
 
@@ -497,25 +478,24 @@
     chans = weight.shape[1]
     rows = blocks * chans
     shapes = [f32(2, rows, width), f32(rows, 2 * width), f32(rows, 2 * width), f32(rows, width)]
-    shapes.append(f32(blocks, 8, width))
     return pl.pallas_call(
         lambda *refs: first_kernel(scale, *refs),
         name="stage_one",
         out_shape=tuple(shapes),
         in_specs=[hbm(), vmem()] + [hbm()] * 5,
-        out_specs=(hbm(),) * 5,
+        out_specs=(hbm(),) * 4,
         scratch_shapes=room(streams, f32(2, rows, width), *shapes, *consts)
         + [
             pltpu.SemaphoreType.DMA((5,)),
             pltpu.SemaphoreType.DMA((blocks // UNROLL,)),
-            pltpu.SemaphoreType.DMA((5,)),
+            pltpu.SemaphoreType.DMA((4,)),
         ],
         cost_estimate=estimate(14),
-        compiler_params=params(60),
+        compiler_params=params(ONE_MIB),
     )(streams, weight, *consts)
 
 
-def stage_two(grad, streams, mixed, filt, prod, conv, edge, weight, consts, scale):
+def stage_two(grad, streams, mixed, filt, prod, conv, weight, consts, scale):
     blocks, width = streams.shape[0], streams.shape[2]
     chans = weight.shape[1]
     rows = blocks * chans
@@ -523,7 +503,7 @@
         lambda *refs: last_kernel(scale, *refs),
         name="stage_two",
         out_shape=bf16(blocks, 3 * chans + 8, width),
-        in_specs=[hbm()] * 7 + [vmem()] + [hbm()] * 5,
+        in_specs=[hbm()] * 6 + [vmem()] + [hbm()] * 5,
         out_specs=hbm(),
         scratch_shapes=room(
             grad,
@@ -539,7 +519,6 @@
             f32(2, blocks, width),
             f32(2, blocks, width),
             f32(4, blocks + 8, width),
-            f32(blocks + 2, 8, width),
             bf16(blocks, 3 * chans, width),
             bf16(blocks, 8, width),
             *consts,
@@ -547,13 +526,13 @@
         + [
             pltpu.SemaphoreType.DMA((5,)),
             pltpu.SemaphoreType.DMA((blocks // UNROLL,)),
-            pltpu.SemaphoreType.DMA((4,)),
+            pltpu.SemaphoreType.DMA((3,)),
             pltpu.SemaphoreType.DMA((2, chans // GROUP)),
             pltpu.SemaphoreType.DMA((2,)),
         ],
         cost_estimate=estimate(14),
-        compiler_params=params(61),
-    )(grad, streams, mixed, filt, prod, conv, edge, weight, *consts)
+        compiler_params=params(TWO_MIB),
+    )(grad, streams, mixed, filt, prod, conv, weight, *consts)
 
 
 def spread_kernel(back_ref, in_hbm, weight_ref, ig_hbm, tg_hbm, sg_ref, in_ref, ig_ref, tg_ref, sems):
@@ -673,21 +652,32 @@
     most = jnp.max(jnp.abs(taps_ref[...]), axis=0, keepdims=True)
     most = jnp.max(most, axis=1, keepdims=True)
     most = jnp.maximum(most * (1.0 + 2.0**-7), 2.0**-100).astype(jnp.bfloat16)
-    mark = jnp.broadcast_to(most, (8, width))
-    bound = jnp.broadcast_to(most.astype(jnp.float32), (width, width))
+    mark = jnp.broadcast_to(most.astype(jnp.float32), (8, width))
+    row = lax.broadcasted_iota(jnp.int32, (8, width), 0)
+    group = lax.broadcasted_iota(jnp.int32, (8, width), 1) // chans
+    inverse = jnp.broadcast_to(1.0 / most.astype(jnp.float32), (width, width))
     for part in range(CHUNKS):
         fetch(part).wait()
         for m in range(part * wide // width, (part + 1) * wide // width):
             cols = pl.ds(m * width, width)
             blocks = [in_ref[b, :, cols].astype(jnp.float32).T.astype(jnp.bfloat16) for b in range(3)]
-            blocks.append(encode(taps_ref[:, cols].T, bound))
+            blocks.append(encode(taps_ref[:, cols].T, inverse))
+            edge = jnp.zeros((8, width), jnp.float32)
+            for i, (at, stream, down) in enumerate(
+                ((width - 16, 1, 2), (width - 16, 2, 4), (0, 1, 4), (0, 2, 6))
+            ):
+                end = in_ref[stream, pl.ds(at, 16), cols].astype(jnp.float32)
+                end = pltpu.roll(end[8:] if at else end[:8], down, 0)
+                edge = jnp.where(row // 2 == i, end, edge)
             for h in range(some):
                 d = m * some + h
                 at = slice(h * chans, (h + 1) * chans)
                 query_ref[d] = blocks[0][at]
                 for b in range(3):
                     out_ref[d, pl.ds(b * chans, chans), :] = blocks[b + 1][at]
-                out_ref[d, pl.ds(3 * chans, 8), :] = mark
+                turned = pltpu.roll(edge, (some - 1 - h) * chans, 1) if h < some - 1 else edge
+                tile = jnp.where(group == some - 1, turned, mark)
+                out_ref[d, pl.ds(3 * chans, 8), :] = tile.astype(jnp.bfloat16)
         for copy in puts(part):
             copy.start()
     for part in range(CHUNKS):
@@ -738,13 +728,13 @@
         most = jnp.max(peak[...], axis=1, keepdims=True)
         most = jnp.maximum(most * (1.0 + 2.0**-7), 2.0**-100).astype(jnp.bfloat16)
         mark = jnp.broadcast_to(most, (8, width))
-        bound = jnp.broadcast_to(most[:1].astype(jnp.float32), (chans, width))
+        inverse = jnp.broadcast_to(1.0 / most[:1].astype(jnp.float32), (chans, width))
 
         def fill(i, carry):
             for u in range(UNROLL):
                 d = i * UNROLL + u
                 out_ref[d, pl.ds(0, chans), :] = query_ref[d]
-                out_ref[d, pl.ds(chans, chans), :] = encode(grad[row_of(d, chans), :], bound)
+                out_ref[d, pl.ds(chans, chans), :] = encode(grad[row_of(d, chans), :], inverse)
                 out_ref[d, pl.ds(2 * chans, 8), :] = mark
             return carry
 
@@ -803,8 +793,8 @@
     weight = jnp.broadcast_to(weight.reshape(9, chans, 1), (9, chans, rows))
 
     consts = [jnp.asarray(t) for t in tables(count, rows)]
-    mixed, filt, prod, conv, edge = stage_one(streams, weight, consts, scale)
-    back = stage_two(gated, streams, mixed, filt, prod, conv, edge, weight, consts, scale)
+    mixed, filt, prod, conv = stage_one(streams, weight, consts, scale)
+    back = stage_two(gated, streams, mixed, filt, prod, conv, weight, consts, scale)
 
     back = regroup(back)
     return spread(back, inputs, short_weight)

time: 119 us -> 118 us (level)
  waiting for transfers between devices: 14.8 us -> 17.5 us
  Pallas kernels: 51.9 us -> 49.5 us
    all_to_all x2, waiting for transfers between devices: 14.8 us -> 17.5 us  [regroup(): return lax.all_to_all(x, 'ctx', split_axis=0, concat_axis=0, tiled=True)]
    pallas_call x1, Pallas kernels: 14.4 us -> 11.8 us  [stage_one(): pl.pallas_call(lambda *refs: first_kernel(scale, *refs), name='stage_one'...]
  transfers between devices with their start and end apart: 3 -> 3, of which waited for: 2 -> 2; matrix products, arithmetic and copies ran while one was open for 1% -> 1% of each run, Pallas kernels for 26% -> 24%
where the time goes in v9:
time: 118 us
  Pallas kernels  49.5 us (42%)
  blocking collectives  29.7 us (25%)
  starting transfers between devices  19.1 us (16%)
  waiting for transfers between devices  17.5 us (15%)
    all_to_all x1, blocking collectives, regroup(): return lax.all_to_all(x, 'ctx', split_axis=0, concat_axis=0, tiled=True)  29.7 us
    all_to_all x2, waiting for transfers between devices, regroup(): return lax.all_to_all(x, 'ctx', split_axis=0, concat_axis=0, tiled=True)  17.5 us
    pallas_call x1, Pallas kernels, stage_two(): pl.pallas_call(lambda *refs: last_kernel(scale, *refs), name='stage_two',...  16.3 us
    all_to_all x2, starting transfers between devices, regroup(): return lax.all_to_all(x, 'ctx', split_axis=0, concat_axis=0, tiled=True)  15.3 us
    pallas_call x1, Pallas kernels, project(): pl.pallas_call(project_kernel, name='project', grid_spec=pltpu.PrefetchSc...  12.4 us
    pallas_call x1, Pallas kernels, stage_one(): pl.pallas_call(lambda *refs: first_kernel(scale, *refs), name='stage_one'...  11.8 us
    pallas_call x1, Pallas kernels, spread(): pl.pallas_call(spread_kernel, name='spread', out_shape=outs + (f32(*weigh...  5.12 us
    pallas_call x1, Pallas kernels, collect(): pl.pallas_call(collect_kernel, name='collect', out_shape=outs, in_specs=[...  3.85 us
  transfers between devices with their start and end apart: 3, of which 2 were waited for; matrix products, arithmetic and copies ran while one was open for 1% of the time, Pallas kernels for 24%

profile of v9, /device:TPU:1, one launch (start us, length us, event | category | flops | bytes accessed | tf_op | source)
XLA Modules:
  0.0 117.6 jit_solution(5053627788488630251)
XLA Ops:
  0.6 3.8 %collective-permute-start = (bf16[128,2048]{1,0:T(8,128)(2,1)}, bf16[128,2048]{1,0:T(8,128)(2,1)S(1)}, u32[]{:S(2)}, u32[]{:S(2)}) collective-permute-start(bf16[128,2048]{1,0:T(8,128)(2,1)} %own_ref.1), channel_id=1, source_target_pairs={{0,1},{1,0},{2,3},{3,2},{4,5},{5,4},{6,7},{7,6},{8,9},{9,8},{10,11... | collective-permute-start | bytes 1572872 | tf_op jit(solution)/shard_map/ppermute | solution.py:786
  4.5 3.9 %collect.1 = (bf16[64,104,128]{2,1,0:T(8,128)(2,1)}, bf16[64,32,128]{2,1,0:T(8,128)(2,1)}) custom-call(bf16[3,128,2048]{2,1,0:T(8,128)(2,1)} %in_hbm.3, f32[128,2048]{1,0:T(8,128)} %taps_hbm.1), custom_call_target="tpu_custom_call" | custom-call | flops 500000000 | bytes 15000000 | tf_op jit(solution)/shard_map/collect/pallas_call | solution.py:692
  8.3 0.0 copy-start.2
  8.3 0.0 copy-start.3
  8.3 9.5 %all-to-all-start.1 = ((bf16[64,104,128]{2,1,0:T(8,128)(2,1)}), bf16[64,104,128]{2,1,0:T(8,128)(2,1)S(1)}, u32[]{:S(2)}, u32[]{:S(2)}) async-start(bf16[64,104,128]{2,1,0:T(8,128)(2,1)} %get-tuple-element.10), calls=%async_computation.1 | async-start | bytes 3407872 | tf_op jit(solution)/shard_map/all_to_all | solution.py:775
  17.9 0.0 collective-permute-done.other_ref
  17.9 0.0 copy-done.2
  17.9 0.0 copy-done.3
  17.9 12.4 %project.1 = bf16[64,72,128]{2,1,0:T(8,128)(2,1)} custom-call(s32[1]{0:T(128)} %bitcast.which_ref, bf16[2048,4096]{1,0:T(8,128)(2,1)} %other_w.1, bf16[2048,4096]{1,0:T(8,128)(2,1)} %other_w.1, bf16[128,2048]{1,0:T(8,128)(2,1)S(1)} %copy-done.2, bf16[128,2048]{1,0:T(8,128)(2,1)S(1)} %collective-permute-done.other_ref, bf16[64,32,128]{2,1,0:T(8,128)(2,1)S(1)} %copy-done.3), custom_call_target="tpu_custom_call" | custom-call | flops 20000000000 | bytes 600000000 | tf_op jit(solution)/shard_map/project/pallas_call | solution.py:749
  30.3 0.0 copy-start.1
  30.3 11.7 %all-to-all-done.1.refs_0_.refs_1_ = bf16[64,104,128]{2,1,0:T(8,128)(2,1)S(1)} async-done(((bf16[64,104,128]{2,1,0:T(8,128)(2,1)}), bf16[64,104,128]{2,1,0:T(8,128)(2,1)S(1)}, u32[]{:S(2)}, u32[]{:S(2)}) %all-to-all-start.1) | async-done | bytes 1703968 | tf_op jit(solution)/shard_map/all_to_all | solution.py:775
  42.1 0.0 copy-start.4
  42.1 5.8 %all-to-all-start = ((bf16[64,72,128]{2,1,0:T(8,128)(2,1)}), bf16[64,72,128]{2,1,0:T(8,128)(2,1)}, u32[]{:S(2)}, u32[]{:S(2)}) async-start(bf16[64,72,128]{2,1,0:T(8,128)(2,1)} %project.1), calls=%async_computation | async-start | bytes 2359296 | tf_op jit(solution)/shard_map/all_to_all | solution.py:775
  47.8 0.0 copy-done.1
  47.9 0.1 constant_dynamic-slice_fusion
  47.9 0.8 broadcast_in_dim.8.refs_1_.refs_6_
  48.7 0.0 copy-done.4
  48.7 11.8 %stage_one.1 = (f32[2,2048,128]{2,1,0:T(8,128)}, f32[2048,256]{1,0:T(8,128)}, f32[2048,256]{1,0:T(8,128)}, f32[2048,128]{1,0:T(8,128)}) custom-call(bf16[64,104,128]{2,1,0:T(8,128)(2,1)} %copy-done.4, f32[9,32,128]{2,1,0:T(8,128)} %broadcast_in_dim.8.refs_1_.refs_6_, bf16[128,192]{1,0:T(8,128)(2,1)} %constant.24.clone.refs_2_.refs_7_, ...), custom_call_target="tpu_custom_call" | custom-call | flops 1400000000 | bytes 42000000 | tf_op jit(solution)/shard_map/stage_one/pallas_call | solution.py:481
  60.5 5.8 %all-to-all-done.refs_0_ = bf16[64,72,128]{2,1,0:T(8,128)(2,1)} async-done(((bf16[64,72,128]{2,1,0:T(8,128)(2,1)}), bf16[64,72,128]{2,1,0:T(8,128)(2,1)}, u32[]{:S(2)}, u32[]{:S(2)}) %all-to-all-start) | async-done | bytes 1179680 | tf_op jit(solution)/shard_map/all_to_all | solution.py:775
  66.3 16.3 %stage_two.1 = bf16[64,104,128]{2,1,0:T(8,128)(2,1)} custom-call(bf16[64,72,128]{2,1,0:T(8,128)(2,1)} %all-to-all-done.refs_0_, bf16[64,104,128]{2,1,0:T(8,128)(2,1)} %copy-done.4, f32[2,2048,128]{2,1,0:T(8,128)} %get-tuple-element.11.refs_2_, f32[2048,256]{1,0:T(8,128)} %get-tuple-element.12.refs_3_, f32[2048,256]{1,0:T(8,128)} %get-tuple-element.13.refs_4_, ...), custom_call_target="tpu_custom_call" | custom-call | flops 1400000000 | bytes 42000000 | tf_op jit(solution)/shard_map/stage_two/pallas_call | solution.py:502
  82.6 0.0 copy-start
  82.6 29.7 %all_to_all.15.back_ref = bf16[64,104,128]{2,1,0:T(8,128)(2,1)S(1)} all-to-all(bf16[64,104,128]{2,1,0:T(8,128)(2,1)} %stage_two.1), channel_id=1, replica_groups=mesh['ctx'=64,'tp'=2] {'ctx'}, dimensions={0} | all-to-all | bytes 3407872 | tf_op jit(solution)/shard_map/all_to_all | solution.py:775
  112.3 0.0 copy-done
  112.3 5.1 %spread.1 = (bf16[3,128,2048]{2,1,0:T(8,128)(2,1)}, f32[128,2048]{1,0:T(8,128)}, f32[3,3,2048]{2,1,0:T(4,128)}) custom-call(bf16[64,104,128]{2,1,0:T(8,128)(2,1)S(1)} %all_to_all.15.back_ref, bf16[3,128,2048]{2,1,0:T(8,128)(2,1)S(1)} %copy-done, f32[3,3,2048]{2,1,0:T(4,128)S(1)} %copy-done.1), custom_call_target="tpu_custom_call" | custom-call | flops 500000000 | bytes 15000000 | tf_op jit(solution)/shard_map/spread/pallas_call | solution.py:617
  (1 shorter events, 0.0 us)
Async XLA Ops:
  0.6 17.3 %collective-permute-start = (bf16[128,2048]{1,0:T(8,128)(2,1)}, bf16[128,2048]{1,0:T(8,128)(2,1)S(1)}, u32[]{:S(2)}, u32[]{:S(2)}) collective-permute-start(bf16[128,2048]{1,0:T(8,128)(2,1)} %own_ref.1), channel_id=1, source_target_pairs={{0,1},{1,0},{2,3},{3,2},{4,5},{5,4},{6,7},{7,6},{8,9},{9,8},{10,11... | collective-permute-start | bytes 1572872 | tf_op jit(solution)/shard_map/ppermute | solution.py:786
  8.3 9.6 %copy-start.2 = (bf16[128,2048]{1,0:T(8,128)(2,1)S(1)}, bf16[128,2048]{1,0:T(8,128)(2,1)}, u32[]{:S(2)}) copy-start(bf16[128,2048]{1,0:T(8,128)(2,1)} %own_ref.1) | copy-start | bytes 1572868
  8.3 9.6 %copy-start.3 = (bf16[64,32,128]{2,1,0:T(8,128)(2,1)S(1)}, bf16[64,32,128]{2,1,0:T(8,128)(2,1)}, u32[]{:S(2)}) copy-start(bf16[64,32,128]{2,1,0:T(8,128)(2,1)} %get-tuple-element.9.query_ref) | copy-start | bytes 1572868
  8.3 33.7 %all-to-all-start.1 = ((bf16[64,104,128]{2,1,0:T(8,128)(2,1)}), bf16[64,104,128]{2,1,0:T(8,128)(2,1)S(1)}, u32[]{:S(2)}, u32[]{:S(2)}) async-start(bf16[64,104,128]{2,1,0:T(8,128)(2,1)} %get-tuple-element.10), calls=%async_computation.1 | async-start | bytes 3407872 | tf_op jit(solution)/shard_map/all_to_all | solution.py:775
  30.3 17.5 %copy-start.1 = (f32[3,3,2048]{2,1,0:T(4,128)S(1)}, f32[3,3,2048]{2,1,0:T(4,128)}, u32[]{:S(2)}) copy-start(f32[3,3,2048]{2,1,0:T(4,128)} %weight_ref.1) | copy-start | bytes 221188
  42.1 6.6 %copy-start.4 = (bf16[64,104,128]{2,1,0:T(8,128)(2,1)}, bf16[64,104,128]{2,1,0:T(8,128)(2,1)S(1)}, u32[]{:S(2)}) copy-start(bf16[64,104,128]{2,1,0:T(8,128)(2,1)S(1)} %all-to-all-done.1.refs_0_.refs_1_) | copy-start | bytes 5111812
  42.1 24.2 %all-to-all-start = ((bf16[64,72,128]{2,1,0:T(8,128)(2,1)}), bf16[64,72,128]{2,1,0:T(8,128)(2,1)}, u32[]{:S(2)}, u32[]{:S(2)}) async-start(bf16[64,72,128]{2,1,0:T(8,128)(2,1)} %project.1), calls=%async_computation | async-start | bytes 2359296 | tf_op jit(solution)/shard_map/all_to_all | solution.py:775
  82.6 29.7 %copy-start = (bf16[3,128,2048]{2,1,0:T(8,128)(2,1)S(1)}, bf16[3,128,2048]{2,1,0:T(8,128)(2,1)}, u32[]{:S(2)}) copy-start(bf16[3,128,2048]{2,1,0:T(8,128)(2,1)} %in_hbm.3) | copy-start | bytes 4718596

commit v10 on v9

--- a/solution.py
+++ b/solution.py
@@ -173,9 +173,9 @@
 
 
 def first_kernel(scale, in_hbm, weight_ref, *refs):
-    const_in, (mixed_out, filt_out, prod_out, conv_out) = refs[:5], refs[5:9]
-    in_ref, src, mixed_ref, filt_ref, prod_ref, conv_ref = refs[9:15]
-    consts, const_sems, in_sems, out_sems = refs[15:20], refs[20], refs[21], refs[22]
+    const_in, (mixed_out, filt_out, prod_out, conv_out, lag_out) = refs[:5], refs[5:10]
+    in_ref, src, mixed_ref, filt_ref, prod_ref, conv_ref, lag_ref = refs[10:17]
+    consts, const_sems, in_sems, out_sems = refs[17:22], refs[22], refs[23], refs[24]
     first_ref, last_ref, forward_ref, backward_ref, twiddle_ref = consts
     blocks, width = in_ref.shape[0], in_ref.shape[2]
     chans = weight_ref.shape[1]
@@ -195,7 +195,11 @@
             at = row_of(n1, chans)
             mixed = []
             for b in range(2):
-                mixed.append(mix(weight_ref, b + 1, lagged(in_ref, n1, b, chans, width)))
+                parts = lagged(in_ref, n1, b, chans, width)
+                for j in (1, 2):
+                    at_lag = pl.ds((2 * b + j - 1) * chans, chans)
+                    lag_ref[n1, at_lag, :] = parts[j].astype(jnp.bfloat16)
+                mixed.append(mix(weight_ref, b + 1, parts))
                 mixed_ref[b, at, :] = mixed[b]
             src[0, at, :] = coded(in_ref, n1, 2, chans) * scale
             src[1, at, :] = mixed[0] * mixed[1]
@@ -204,6 +208,8 @@
     lax.fori_loop(0, blocks // UNROLL, prepare, 0)
     mixed_copy = pltpu.make_async_copy(mixed_ref, mixed_out, out_sems.at[0])
     mixed_copy.start()
+    lag_copy = pltpu.make_async_copy(lag_ref, lag_out, out_sems.at[4])
+    lag_copy.start()
     for copy in const_copies:
         copy.wait()
     cos, sin = twiddle_ref[0], twiddle_ref[1]
@@ -239,16 +245,17 @@
     conv_copy = pltpu.make_async_copy(conv_ref, conv_out, out_sems.at[3])
     conv_copy.start()
     mixed_copy.wait()
+    lag_copy.wait()
     pltpu.make_async_copy(filt_ref, filt_out, out_sems.at[1]).wait()
     pltpu.make_async_copy(prod_ref, prod_out, out_sems.at[2]).wait()
     conv_copy.wait()
 
 
-def last_kernel(scale, grad_in, streams_in, mixed_in, filt_in, prod_in, conv_in, weight_ref, *refs):
+def last_kernel(scale, grad_in, streams_in, mixed_in, filt_in, prod_in, conv_in, lag_in, weight_ref, *refs):
     const_in, out_hbm = refs[:5], refs[5]
     query_ref, in_ref, mixed_ref, filt_ref, prod_ref, conv_ref = refs[6:12]
-    grad_ref, src, res, sums, peak, halo, lines, out_ref, tail_ref = refs[12:21]
-    consts, const_sems, grad_sems, sems, spec_sems, out_sems = refs[21:26], *refs[26:31]
+    grad_ref, src, res, sums, peak, halo, lines, lag_ref, out_ref, tail_ref = refs[12:22]
+    consts, const_sems, grad_sems, sems, spec_sems, out_sems = refs[22:27], *refs[27:32]
     first_ref, last_ref, forward_ref, backward_ref, twiddle_ref = consts
     blocks, width = in_ref.shape[0], in_ref.shape[2]
     chans = weight_ref.shape[1]
@@ -260,6 +267,7 @@
                 (mixed_in, mixed_ref),
                 (conv_in, conv_ref),
                 (streams_in, in_ref),
+                (lag_in, lag_ref),
             )
         )
     ]
@@ -312,7 +320,7 @@
             for copy in fetch(step + 1):
                 copy.start()
 
-        @pl.when(step + 1 == steps)
+        @pl.when(step == 0)
         def _():
             for copy in copies:
                 copy.start()
@@ -373,8 +381,13 @@
             out_ref[n1, pl.ds(2 * chans, chans), :] = encode(res[1, at, :] * scale, inverses[1])
             full = [cur, dz * mixed_ref[1, at, :], dz * mixed_ref[0, at, :]]
             for b in range(3):
-                ref, place = (in_ref, b - 1) if b else (query_ref, 0)
-                parts = lagged(ref, n1, place, chans, width)
+                if b:
+                    parts = [in_ref[n1, pl.ds((b - 1) * chans, chans), :]]
+                    for j in (0, 1):
+                        parts.append(lag_ref[n1, pl.ds((2 * b - 2 + j) * chans, chans), :])
+                    parts = [part.astype(jnp.float32) for part in parts]
+                else:
+                    parts = lagged(query_ref, n1, 0, chans, width)
                 for j in range(3):
                     term = full[b] * parts[j]
                     old = adds[3 * b + j]
@@ -478,24 +491,25 @@
     chans = weight.shape[1]
     rows = blocks * chans
     shapes = [f32(2, rows, width), f32(rows, 2 * width), f32(rows, 2 * width), f32(rows, width)]
+    shapes.append(bf16(blocks, 4 * chans, width))
     return pl.pallas_call(
         lambda *refs: first_kernel(scale, *refs),
         name="stage_one",
         out_shape=tuple(shapes),
         in_specs=[hbm(), vmem()] + [hbm()] * 5,
-        out_specs=(hbm(),) * 4,
+        out_specs=(hbm(),) * 5,
         scratch_shapes=room(streams, f32(2, rows, width), *shapes, *consts)
         + [
             pltpu.SemaphoreType.DMA((5,)),
             pltpu.SemaphoreType.DMA((blocks // UNROLL,)),
-            pltpu.SemaphoreType.DMA((4,)),
+            pltpu.SemaphoreType.DMA((5,)),
         ],
         cost_estimate=estimate(14),
         compiler_params=params(ONE_MIB),
     )(streams, weight, *consts)
 
 
-def stage_two(grad, streams, mixed, filt, prod, conv, weight, consts, scale):
+def stage_two(grad, streams, mixed, filt, prod, conv, lag, weight, consts, scale):
     blocks, width = streams.shape[0], streams.shape[2]
     chans = weight.shape[1]
     rows = blocks * chans
@@ -503,7 +517,7 @@
         lambda *refs: last_kernel(scale, *refs),
         name="stage_two",
         out_shape=bf16(blocks, 3 * chans + 8, width),
-        in_specs=[hbm()] * 6 + [vmem()] + [hbm()] * 5,
+        in_specs=[hbm()] * 7 + [vmem()] + [hbm()] * 5,
         out_specs=hbm(),
         scratch_shapes=room(
             grad,
@@ -519,6 +533,7 @@
             f32(2, blocks, width),
             f32(2, blocks, width),
             f32(4, blocks + 8, width),
+            bf16(blocks, 4 * chans, width),
             bf16(blocks, 3 * chans, width),
             bf16(blocks, 8, width),
             *consts,
@@ -526,13 +541,13 @@
         + [
             pltpu.SemaphoreType.DMA((5,)),
             pltpu.SemaphoreType.DMA((blocks // UNROLL,)),
-            pltpu.SemaphoreType.DMA((3,)),
+            pltpu.SemaphoreType.DMA((4,)),
             pltpu.SemaphoreType.DMA((2, chans // GROUP)),
             pltpu.SemaphoreType.DMA((2,)),
         ],
         cost_estimate=estimate(14),
         compiler_params=params(TWO_MIB),
-    )(grad, streams, mixed, filt, prod, conv, weight, *consts)
+    )(grad, streams, mixed, filt, prod, conv, lag, weight, *consts)
 
 
 def spread_kernel(back_ref, in_hbm, weight_ref, ig_hbm, tg_hbm, sg_ref, in_ref, ig_ref, tg_ref, sems):
@@ -793,8 +808,8 @@
     weight = jnp.broadcast_to(weight.reshape(9, chans, 1), (9, chans, rows))
 
     consts = [jnp.asarray(t) for t in tables(count, rows)]
-    mixed, filt, prod, conv = stage_one(streams, weight, consts, scale)
-    back = stage_two(gated, streams, mixed, filt, prod, conv, weight, consts, scale)
+    mixed, filt, prod, conv, lag = stage_one(streams, weight, consts, scale)
+    back = stage_two(gated, streams, mixed, filt, prod, conv, lag, weight, consts, scale)
 
     back = regroup(back)
     return spread(back, inputs, short_weight)

time: 118 us -> 118 us (level)
  no operation moved by 1% of the time
where the time goes in v10:
time: 118 us; the launch traced here: 117 us
  Pallas kernels  49.2 us (42%)
  blocking collectives  29.7 us (25%)
  starting transfers between devices  19.1 us (16%)
  waiting for transfers between devices  17.5 us (15%)
    all_to_all x1, blocking collectives, regroup(): return lax.all_to_all(x, 'ctx', split_axis=0, concat_axis=0, tiled=True)  29.7 us
    all_to_all x2, waiting for transfers between devices, regroup(): return lax.all_to_all(x, 'ctx', split_axis=0, concat_axis=0, tiled=True)  17.5 us
    pallas_call x1, Pallas kernels, stage_two(): pl.pallas_call(lambda *refs: last_kernel(scale, *refs), name='stage_two',...  16 us
    all_to_all x2, starting transfers between devices, regroup(): return lax.all_to_all(x, 'ctx', split_axis=0, concat_axis=0, tiled=True)  15.3 us
    pallas_call x1, Pallas kernels, project(): pl.pallas_call(project_kernel, name='project', grid_spec=pltpu.PrefetchSc...  12.4 us
    pallas_call x1, Pallas kernels, stage_one(): pl.pallas_call(lambda *refs: first_kernel(scale, *refs), name='stage_one'...  11.9 us
    pallas_call x1, Pallas kernels, spread(): pl.pallas_call(spread_kernel, name='spread', out_shape=outs + (f32(*weigh...  5.12 us
    pallas_call x1, Pallas kernels, collect(): pl.pallas_call(collect_kernel, name='collect', out_shape=outs, in_specs=[...  3.85 us
  transfers between devices with their start and end apart: 3, of which 2 were waited for; matrix products, arithmetic and copies ran while one was open for 1% of the time, Pallas kernels for 24%

profile of v10, /device:TPU:1, one launch (start us, length us, event | category | flops | bytes accessed | tf_op | source)
XLA Modules:
  0.0 117.3 jit_solution(10457155949247995022)
XLA Ops:
  0.6 3.8 %collective-permute-start = (bf16[128,2048]{1,0:T(8,128)(2,1)}, bf16[128,2048]{1,0:T(8,128)(2,1)S(1)}, u32[]{:S(2)}, u32[]{:S(2)}) collective-permute-start(bf16[128,2048]{1,0:T(8,128)(2,1)} %own_ref.1), channel_id=1, source_target_pairs={{0,1},{1,0},{2,3},{3,2},{4,5},{5,4},{6,7},{7,6},{8,9},{9,8},{10,11... | collective-permute-start | bytes 1572872 | tf_op jit(solution)/shard_map/ppermute | solution.py:801
  4.5 3.9 %collect.1 = (bf16[64,104,128]{2,1,0:T(8,128)(2,1)}, bf16[64,32,128]{2,1,0:T(8,128)(2,1)}) custom-call(bf16[3,128,2048]{2,1,0:T(8,128)(2,1)} %in_hbm.3, f32[128,2048]{1,0:T(8,128)} %taps_hbm.1), custom_call_target="tpu_custom_call" | custom-call | flops 500000000 | bytes 15000000 | tf_op jit(solution)/shard_map/collect/pallas_call | solution.py:707
  8.3 0.0 copy-start.2
  8.3 0.0 copy-start.3
  8.3 9.5 %all-to-all-start.1 = ((bf16[64,104,128]{2,1,0:T(8,128)(2,1)}), bf16[64,104,128]{2,1,0:T(8,128)(2,1)S(1)}, u32[]{:S(2)}, u32[]{:S(2)}) async-start(bf16[64,104,128]{2,1,0:T(8,128)(2,1)} %get-tuple-element.11), calls=%async_computation.1 | async-start | bytes 3407872 | tf_op jit(solution)/shard_map/all_to_all | solution.py:790
  17.9 0.0 collective-permute-done.other_ref
  17.9 0.0 copy-done.2
  17.9 0.0 copy-done.3
  17.9 12.4 %project.1 = bf16[64,72,128]{2,1,0:T(8,128)(2,1)} custom-call(s32[1]{0:T(128)} %bitcast.which_ref, bf16[2048,4096]{1,0:T(8,128)(2,1)} %other_w.1, bf16[2048,4096]{1,0:T(8,128)(2,1)} %other_w.1, bf16[128,2048]{1,0:T(8,128)(2,1)S(1)} %copy-done.2, bf16[128,2048]{1,0:T(8,128)(2,1)S(1)} %collective-permute-done.other_ref, bf16[64,32,128]{2,1,0:T(8,128)(2,1)S(1)} %copy-done.3), custom_call_target="tpu_custom_call" | custom-call | flops 20000000000 | bytes 600000000 | tf_op jit(solution)/shard_map/project/pallas_call | solution.py:764
  30.3 0.0 copy-start.1
  30.3 11.7 %all-to-all-done.1.refs_0_.refs_1_ = bf16[64,104,128]{2,1,0:T(8,128)(2,1)S(1)} async-done(((bf16[64,104,128]{2,1,0:T(8,128)(2,1)}), bf16[64,104,128]{2,1,0:T(8,128)(2,1)S(1)}, u32[]{:S(2)}, u32[]{:S(2)}) %all-to-all-start.1) | async-done | bytes 1703968 | tf_op jit(solution)/shard_map/all_to_all | solution.py:790
  42.1 0.0 copy-start.4
  42.1 5.7 %all-to-all-start = ((bf16[64,72,128]{2,1,0:T(8,128)(2,1)}), bf16[64,72,128]{2,1,0:T(8,128)(2,1)}, u32[]{:S(2)}, u32[]{:S(2)}) async-start(bf16[64,72,128]{2,1,0:T(8,128)(2,1)} %project.1), calls=%async_computation | async-start | bytes 2359296 | tf_op jit(solution)/shard_map/all_to_all | solution.py:790
  47.8 0.0 copy-done.1
  47.8 0.1 constant_dynamic-slice_fusion
  47.9 0.8 broadcast_in_dim.8.refs_1_.refs_7_
  48.7 0.0 copy-done.4
  48.7 11.9 %stage_one.1 = (f32[2,2048,128]{2,1,0:T(8,128)}, f32[2048,256]{1,0:T(8,128)}, f32[2048,256]{1,0:T(8,128)}, f32[2048,128]{1,0:T(8,128)}, bf16[64,128,128]{2,1,0:T(8,128)(2,1)}) custom-call(bf16[64,104,128]{2,1,0:T(8,128)(2,1)} %copy-done.4, f32[9,32,128]{2,1,0:T(8,128)} %broadcast_in_dim.8.refs_1_.refs_7_, bf16[128,192]{1,0:T(8,128)(2,1)} %constant.24.clone.refs_2_.refs_8_, ...), custom_call_target="tpu_custom_call" | custom-call | flops 1400000000 | bytes 42000000 | tf_op jit(solution)/shard_map/stage_one/pallas_call | solution.py:495
  60.6 5.7 %all-to-all-done.refs_0_ = bf16[64,72,128]{2,1,0:T(8,128)(2,1)} async-done(((bf16[64,72,128]{2,1,0:T(8,128)(2,1)}), bf16[64,72,128]{2,1,0:T(8,128)(2,1)}, u32[]{:S(2)}, u32[]{:S(2)}) %all-to-all-start) | async-done | bytes 1179680 | tf_op jit(solution)/shard_map/all_to_all | solution.py:790
  66.3 16.0 %stage_two.1 = bf16[64,104,128]{2,1,0:T(8,128)(2,1)} custom-call(bf16[64,72,128]{2,1,0:T(8,128)(2,1)} %all-to-all-done.refs_0_, bf16[64,104,128]{2,1,0:T(8,128)(2,1)} %copy-done.4, f32[2,2048,128]{2,1,0:T(8,128)} %get-tuple-element.12.refs_2_, f32[2048,256]{1,0:T(8,128)} %get-tuple-element.13.refs_3_, f32[2048,256]{1,0:T(8,128)} %get-tuple-element.14.refs_4_, ...), custom_call_target="tpu_custom_call" | custom-call | flops 1400000000 | bytes 42000000 | tf_op jit(solution)/shard_map/stage_two/pallas_call | solution.py:516
  82.3 0.0 copy-start
  82.3 29.7 %all_to_all.15.back_ref = bf16[64,104,128]{2,1,0:T(8,128)(2,1)S(1)} all-to-all(bf16[64,104,128]{2,1,0:T(8,128)(2,1)} %stage_two.1), channel_id=1, replica_groups=mesh['ctx'=64,'tp'=2] {'ctx'}, dimensions={0} | all-to-all | bytes 3407872 | tf_op jit(solution)/shard_map/all_to_all | solution.py:790
  112.1 0.0 copy-done
  112.1 5.1 %spread.1 = (bf16[3,128,2048]{2,1,0:T(8,128)(2,1)}, f32[128,2048]{1,0:T(8,128)}, f32[3,3,2048]{2,1,0:T(4,128)}) custom-call(bf16[64,104,128]{2,1,0:T(8,128)(2,1)S(1)} %all_to_all.15.back_ref, bf16[3,128,2048]{2,1,0:T(8,128)(2,1)S(1)} %copy-done, f32[3,3,2048]{2,1,0:T(4,128)S(1)} %copy-done.1), custom_call_target="tpu_custom_call" | custom-call | flops 500000000 | bytes 15000000 | tf_op jit(solution)/shard_map/spread/pallas_call | solution.py:632
  (1 shorter events, 0.0 us)
Async XLA Ops:
  0.6 17.3 %collective-permute-start = (bf16[128,2048]{1,0:T(8,128)(2,1)}, bf16[128,2048]{1,0:T(8,128)(2,1)S(1)}, u32[]{:S(2)}, u32[]{:S(2)}) collective-permute-start(bf16[128,2048]{1,0:T(8,128)(2,1)} %own_ref.1), channel_id=1, source_target_pairs={{0,1},{1,0},{2,3},{3,2},{4,5},{5,4},{6,7},{7,6},{8,9},{9,8},{10,11... | collective-permute-start | bytes 1572872 | tf_op jit(solution)/shard_map/ppermute | solution.py:801
  8.3 9.6 %copy-start.2 = (bf16[128,2048]{1,0:T(8,128)(2,1)S(1)}, bf16[128,2048]{1,0:T(8,128)(2,1)}, u32[]{:S(2)}) copy-start(bf16[128,2048]{1,0:T(8,128)(2,1)} %own_ref.1) | copy-start | bytes 1572868
  8.3 9.6 %copy-start.3 = (bf16[64,32,128]{2,1,0:T(8,128)(2,1)S(1)}, bf16[64,32,128]{2,1,0:T(8,128)(2,1)}, u32[]{:S(2)}) copy-start(bf16[64,32,128]{2,1,0:T(8,128)(2,1)} %get-tuple-element.10.query_ref) | copy-start | bytes 1572868
  8.3 33.7 %all-to-all-start.1 = ((bf16[64,104,128]{2,1,0:T(8,128)(2,1)}), bf16[64,104,128]{2,1,0:T(8,128)(2,1)S(1)}, u32[]{:S(2)}, u32[]{:S(2)}) async-start(bf16[64,104,128]{2,1,0:T(8,128)(2,1)} %get-tuple-element.11), calls=%async_computation.1 | async-start | bytes 3407872 | tf_op jit(solution)/shard_map/all_to_all | solution.py:790
  30.3 17.5 %copy-start.1 = (f32[3,3,2048]{2,1,0:T(4,128)S(1)}, f32[3,3,2048]{2,1,0:T(4,128)}, u32[]{:S(2)}) copy-start(f32[3,3,2048]{2,1,0:T(4,128)} %weight_ref.1) | copy-start | bytes 221188
  42.1 6.6 %copy-start.4 = (bf16[64,104,128]{2,1,0:T(8,128)(2,1)}, bf16[64,104,128]{2,1,0:T(8,128)(2,1)S(1)}, u32[]{:S(2)}) copy-start(bf16[64,104,128]{2,1,0:T(8,128)(2,1)S(1)} %all-to-all-done.1.refs_0_.refs_1_) | copy-start | bytes 5111812
  42.1 24.2 %all-to-all-start = ((bf16[64,72,128]{2,1,0:T(8,128)(2,1)}), bf16[64,72,128]{2,1,0:T(8,128)(2,1)}, u32[]{:S(2)}, u32[]{:S(2)}) async-start(bf16[64,72,128]{2,1,0:T(8,128)(2,1)} %project.1), calls=%async_computation | async-start | bytes 2359296 | tf_op jit(solution)/shard_map/all_to_all | solution.py:790
  82.3 29.8 %copy-start = (bf16[3,128,2048]{2,1,0:T(8,128)(2,1)S(1)}, bf16[3,128,2048]{2,1,0:T(8,128)(2,1)}, u32[]{:S(2)}) copy-start(bf16[3,128,2048]{2,1,0:T(8,128)(2,1)} %in_hbm.3) | copy-start | bytes 4718596
